TPU v7x, 256 devices: a whole 4x4x8 slice. The times are simulated.
256 devices in a mesh: row: 16 (over z, core), col: 16 (over y, x).
Axes of the slice: x: 4, y: 4, z: 8, core: 2. Of those that a mesh axis runs over, the one named last changes fastest.
Arguments:
- right_sides: float32 [4, 1024, 4096], P(None, 'row', 'col'), may hold values from -6 to 6
- low_left: bfloat16 [6, 4096, 128], P(None, 'col'), may hold values from -0.25 to 0.25
- low_right: bfloat16 [6, 4096, 128], P(None, 'col'), may hold values from -0.09375 to 0.09375
- up_left: bfloat16 [6, 4096, 128], P(None, 'col'), may hold values from -0.25 to 0.25
- up_right: bfloat16 [6, 4096, 128], P(None, 'col'), may hold values from -0.09375 to 0.09375
- low_ranks: int32 [6], replicated, may hold values from 1 to 4
- up_ranks: int32 [6], replicated, may hold values from 1 to 4
- inv_lower: bfloat16 [4, 4096, 4096], P(None, 'col', 'row'), may hold values from -0.09375 to 0.09375
- inv_upper: bfloat16 [4, 4096, 4096], P(None, 'col', 'row'), may hold values from -0.09375 to 0.09375
Outputs:
- solution: float32 [4, 1024, 4096], P(None, 'row', 'col')
Inputs may be any that keep to these rules, and one draw needn't show every extreme that they name: `low_ranks`: factor columns beyond 32 times this value are padding with arbitrary values and must be masked out. `up_ranks`: factor columns beyond 32 times this value are padding with arbitrary values and must be masked out.
All inputs are finite; a program needn't handle non-finite values.
Results may differ from a plain program's by a relative error of at most 0.03.
Values may be sent and summed in bfloat16 or wider, within the bound.
No kernel may reach another device: no remote copies, remote signals or barrier semaphores. Data moves between devices by JAX's collectives and lax.ppermute only.
A program may use at most 64 MiB of HBM per device.

v0:
```python
import jax
import jax.numpy as jnp
import numpy as np
from jax import lax
from jax.sharding import PartitionSpec as P

RBLK = 32


def laid_out(parts, dim):
    parts = jnp.moveaxis(parts, 0, dim)
    lengths = parts.shape
    return parts.reshape(*lengths[:dim], lengths[dim] * lengths[dim + 1], *lengths[dim + 2 :])


def from_everyone(value, axis):
    length = lax.axis_size(axis)
    return lax.all_to_all(
        jnp.broadcast_to(value[None], (length, *value.shape)), axis, 0, 0, tiled=True
    )


def gathered_copies(value, axis, dim):
    return laid_out(from_everyone(value, axis), dim)


def of_everyone(value, axis):
    everything = from_everyone(value, axis)
    return jnp.sum(everything.astype(jnp.float32), axis=0)


def rank_mask(ranks, pair_index, rank_cols):
    columns = jnp.arange(rank_cols, dtype=jnp.int32)
    return (columns[None, :] < RBLK * ranks[pair_index][:, None]).astype(jnp.float32)


def times_inverse(block, inverse):
    return lax.dot_general(
        block, inverse, (((1,), (1,)), ((), ())), preferred_element_type=jnp.float32
    )


def fold_columns(whole, piece):
    return times_inverse(whole, piece)


def shards(
    right_sides, low_left, low_right, up_left, up_right, low_ranks, up_ranks, inv_lower, inv_upper
):
    tile_count = right_sides.shape[0]
    rank_cols = low_left.shape[2]
    residual = right_sides
    forward = []
    for section in range(tile_count):
        rounded = residual[section].astype(jnp.bfloat16)
        whole = gathered_copies(rounded, "col", 1)
        solved = fold_columns(whole, lax.all_gather(inv_lower[section], "row", axis=1, tiled=True))
        forward.append(solved)
        if section + 1 < tile_count:
            pair_index = np.array(
                [tile * (tile - 1) // 2 + section for tile in range(section + 1, tile_count)],
                dtype=np.int32,
            )
            projections = jnp.einsum(
                "nw,mwr->mnr",
                solved.astype(jnp.bfloat16),
                low_right[pair_index],
                preferred_element_type=jnp.float32,
            )
            summed = of_everyone(projections.astype(jnp.bfloat16), "col").astype(jnp.float32)
            masked = (summed * rank_mask(low_ranks, pair_index, rank_cols)[:, None, :]).astype(
                jnp.bfloat16
            )
            update = jnp.einsum(
                "mnr,mwr->mnw", masked, low_left[pair_index], preferred_element_type=jnp.float32
            )
            residual = residual.at[section + 1 :].add(-update)
    state = jnp.stack(forward)
    solutions = [None] * tile_count
    for section in range(tile_count - 1, -1, -1):
        rounded = state[section].astype(jnp.bfloat16)
        whole = gathered_copies(rounded, "col", 1)
        solved = fold_columns(whole, lax.all_gather(inv_upper[section], "row", axis=1, tiled=True))
        solutions[section] = solved
        if section > 0:
            pair_index = np.array(
                [section * (section - 1) // 2 + tile for tile in range(section)], dtype=np.int32
            )
            projections = jnp.einsum(
                "nw,mwr->mnr",
                solved.astype(jnp.bfloat16),
                up_right[pair_index],
                preferred_element_type=jnp.float32,
            )
            summed = of_everyone(projections.astype(jnp.bfloat16), "col").astype(jnp.float32)
            masked = (summed * rank_mask(up_ranks, pair_index, rank_cols)[:, None, :]).astype(
                jnp.bfloat16
            )
            update = jnp.einsum(
                "mnr,mwr->mnw", masked, up_left[pair_index], preferred_element_type=jnp.float32
            )
            state = state.at[:section].add(-update)
    return jnp.stack(solutions)


def solution(mesh):
    in_specs = (
        P(None, "row", "col"),
        P(None, "col", None),
        P(None, "col", None),
        P(None, "col", None),
        P(None, "col", None),
        P(),
        P(),
        P(None, "col", "row"),
        P(None, "col", "row"),
    )
    out_specs = P(None, "row", "col")
    return jax.shard_map(shards, mesh=mesh, in_specs=in_specs, out_specs=out_specs, check_vma=False)
```

profile of v0, /device:TPU:2, one launch (start us, length us, event | category | flops | bytes accessed | tf_op | source)
XLA Modules:
  0.0 355.8 jit_solution(16431836217036689485)
XLA Ops:
  6.5 1.9 fusion.70
  10.6 1.9 fusion.69
  13.4 7.5 %all-to-all-start = ((bf16[16,64,256]{2,1,0:T(8,128)(2,1)}), bf16[16,64,256]{2,1,0:T(8,128)(2,1)S(1)}, u32[]{:S(2)}, u32[]{:S(2)}) async-start(bf16[16,64,256]{2,1,0:T(8,128)(2,1)} %broadcast_in_dim.83), calls=%async_computation | async-start | bytes 1048576 | tf_op jit(solution)/shard_map/all_to_all | solution.py:18
  21.5 9.6 %all-to-all-done = bf16[16,64,256]{2,1,0:T(8,128)(2,1)S(1)} async-done(((bf16[16,64,256]{2,1,0:T(8,128)(2,1)}), bf16[16,64,256]{2,1,0:T(8,128)(2,1)S(1)}, u32[]{:S(2)}, u32[]{:S(2)}) %all-to-all-start) | async-done | bytes 524320 | tf_op jit(solution)/shard_map/all_to_all | solution.py:18
  31.1 21.9 %all-gather.17.cloned.1.call-done = bf16[1,256,4096]{2,1,0:T(8,128)(2,1)} async-done(((bf16[1,256,256]{2,1,0:T(8,128)(2,1)}), bf16[1,256,4096]{2,1,0:T(8,128)(2,1)}) %all-gather.17.cloned.1.call-update) | async-done | bytes 2097168 | tf_op jit(solution)/shard_map/all_gather | solution.py:57
  53.0 2.3 fusion.14
  55.6 1.1 broadcast_in_dim.85
  56.6 7.3 %all-to-all-start.1 = ((bf16[16,3,64,128]{3,2,1,0:T(8,128)(2,1)}), bf16[16,3,64,128]{3,2,1,0:T(8,128)(2,1)S(1)}, u32[]{:S(2)}, u32[]{:S(2)}) async-start(bf16[16,3,64,128]{3,2,1,0:T(8,128)(2,1)} %broadcast_in_dim.85), calls=%async_computation.1 | async-start | bytes 1572864 | tf_op jit(solution)/shard_map/all_to_all | solution.py:18
  65.9 11.5 %all-to-all-done.1 = bf16[16,3,64,128]{3,2,1,0:T(8,128)(2,1)S(1)} async-done(((bf16[16,3,64,128]{3,2,1,0:T(8,128)(2,1)}), bf16[16,3,64,128]{3,2,1,0:T(8,128)(2,1)S(1)}, u32[]{:S(2)}, u32[]{:S(2)}) %all-to-all-start.1) | async-done | bytes 786464 | tf_op jit(solution)/shard_map/all_to_all | solution.py:18
  78.5 4.8 %all-to-all-start.2 = ((bf16[16,64,256]{2,1,0:T(8,128)(2,1)}), bf16[16,64,256]{2,1,0:T(8,128)(2,1)S(1)}, u32[]{:S(2)}, u32[]{:S(2)}) async-start(bf16[16,64,256]{2,1,0:T(8,128)(2,1)} %broadcast_in_dim.89), calls=%async_computation.2 | async-start | bytes 1048576 | tf_op jit(solution)/shard_map/all_to_all | solution.py:18
  83.9 9.1 %all-to-all-done.2 = bf16[16,64,256]{2,1,0:T(8,128)(2,1)S(1)} async-done(((bf16[16,64,256]{2,1,0:T(8,128)(2,1)}), bf16[16,64,256]{2,1,0:T(8,128)(2,1)S(1)}, u32[]{:S(2)}, u32[]{:S(2)}) %all-to-all-start.2) | async-done | bytes 524320 | tf_op jit(solution)/shard_map/all_to_all | solution.py:18
  93.0 1.9 all-gather.19.cloned.1.call-done
  94.9 2.4 fusion.12
  97.4 0.9 broadcast_in_dim.91
  98.4 7.3 %all-to-all-start.3 = ((bf16[16,2,64,128]{3,2,1,0:T(8,128)(2,1)}), bf16[16,2,64,128]{3,2,1,0:T(8,128)(2,1)S(1)}, u32[]{:S(2)}, u32[]{:S(2)}) async-start(bf16[16,2,64,128]{3,2,1,0:T(8,128)(2,1)} %broadcast_in_dim.91), calls=%async_computation.3 | async-start | bytes 1048576 | tf_op jit(solution)/shard_map/all_to_all | solution.py:18
  107.0 9.3 %all-to-all-done.3 = bf16[16,2,64,128]{3,2,1,0:T(8,128)(2,1)S(1)} async-done(((bf16[16,2,64,128]{3,2,1,0:T(8,128)(2,1)}), bf16[16,2,64,128]{3,2,1,0:T(8,128)(2,1)S(1)}, u32[]{:S(2)}, u32[]{:S(2)}) %all-to-all-start.3) | async-done | bytes 524320 | tf_op jit(solution)/shard_map/all_to_all | solution.py:18
  117.3 4.8 %all-to-all-start.4 = ((bf16[16,64,256]{2,1,0:T(8,128)(2,1)}), bf16[16,64,256]{2,1,0:T(8,128)(2,1)S(1)}, u32[]{:S(2)}, u32[]{:S(2)}) async-start(bf16[16,64,256]{2,1,0:T(8,128)(2,1)} %broadcast_in_dim.187), calls=%async_computation.4 | async-start | bytes 1048576 | tf_op jit(solution)/shard_map/all_to_all | solution.py:18
  122.9 8.8 %all-to-all-done.4 = bf16[16,64,256]{2,1,0:T(8,128)(2,1)S(1)} async-done(((bf16[16,64,256]{2,1,0:T(8,128)(2,1)}), bf16[16,64,256]{2,1,0:T(8,128)(2,1)S(1)}, u32[]{:S(2)}, u32[]{:S(2)}) %all-to-all-start.4) | async-done | bytes 524320 | tf_op jit(solution)/shard_map/all_to_all | solution.py:18
  131.8 5.0 %all-gather.21.cloned.1.call-done = bf16[1,256,4096]{2,1,0:T(8,128)(2,1)} async-done(((bf16[1,256,256]{2,1,0:T(8,128)(2,1)}), bf16[1,256,4096]{2,1,0:T(8,128)(2,1)}) %all-gather.21.cloned.1.call-update) | async-done | bytes 2097168 | tf_op jit(solution)/shard_map/all_gather | solution.py:57
  136.8 2.4 fusion.10
  140.1 7.3 %all-to-all-start.5 = ((bf16[16,1,64,128]{3,2,1,0:T(8,128)(2,1)}), bf16[16,1,64,128]{3,2,1,0:T(8,128)(2,1)S(1)}, u32[]{:S(2)}, u32[]{:S(2)}) async-start(bf16[16,1,64,128]{3,2,1,0:T(8,128)(2,1)} %broadcast_in_dim.191), calls=%async_computation.5 | async-start | bytes 524288 | tf_op jit(solution)/shard_map/all_to_all | solution.py:18
  148.5 6.6 %all-to-all-done.5 = bf16[16,1,64,128]{3,2,1,0:T(8,128)(2,1)S(1)} async-done(((bf16[16,1,64,128]{3,2,1,0:T(8,128)(2,1)}), bf16[16,1,64,128]{3,2,1,0:T(8,128)(2,1)S(1)}, u32[]{:S(2)}, u32[]{:S(2)}) %all-to-all-start.5) | async-done | bytes 262176 | tf_op jit(solution)/shard_map/all_to_all | solution.py:18
  155.3 13.8 %all_to_all.70 = bf16[16,64,256]{2,1,0:T(8,128)(2,1)S(1)} all-to-all(bf16[16,64,256]{2,1,0:T(8,128)(2,1)S(1)} %broadcast_in_dim.195), channel_id=1, replica_groups=mesh['row'=16,'col'=16] {'col'}, dimensions={0} | all-to-all | bytes 1048576 | tf_op jit(solution)/shard_map/all_to_all | solution.py:18
  169.2 9.4 %all-gather.23.cloned.1.call-done = bf16[1,256,4096]{2,1,0:T(8,128)(2,1)} async-done(((bf16[1,256,256]{2,1,0:T(8,128)(2,1)}), bf16[1,256,4096]{2,1,0:T(8,128)(2,1)}) %all-gather.23.cloned.1.call-update) | async-done | bytes 2097168 | tf_op jit(solution)/shard_map/all_gather | solution.py:57
  178.6 2.4 fusion.31
  181.8 7.3 %all-to-all-start.7 = ((bf16[16,64,256]{2,1,0:T(8,128)(2,1)}), bf16[16,64,256]{2,1,0:T(8,128)(2,1)S(1)}, u32[]{:S(2)}, u32[]{:S(2)}) async-start(bf16[16,64,256]{2,1,0:T(8,128)(2,1)} %broadcast_in_dim.196), calls=%async_computation.7 | async-start | bytes 1048576 | tf_op jit(solution)/shard_map/all_to_all | solution.py:18
  189.7 10.0 %all-to-all-done.7 = bf16[16,64,256]{2,1,0:T(8,128)(2,1)S(1)} async-done(((bf16[16,64,256]{2,1,0:T(8,128)(2,1)}), bf16[16,64,256]{2,1,0:T(8,128)(2,1)S(1)}, u32[]{:S(2)}, u32[]{:S(2)}) %all-to-all-start.7) | async-done | bytes 524320 | tf_op jit(solution)/shard_map/all_to_all | solution.py:18
  199.7 20.7 %all-gather.25.cloned.1.call-done = bf16[1,256,4096]{2,1,0:T(8,128)(2,1)} async-done(((bf16[1,256,256]{2,1,0:T(8,128)(2,1)}), bf16[1,256,4096]{2,1,0:T(8,128)(2,1)}) %all-gather.25.cloned.1.call-update) | async-done | bytes 2097168 | tf_op jit(solution)/shard_map/all_gather | solution.py:83
  220.4 2.4 fusion.6
  222.9 1.1 broadcast_in_dim.197
  224.0 7.3 %all-to-all-start.8 = ((bf16[16,3,64,128]{3,2,1,0:T(8,128)(2,1)}), bf16[16,3,64,128]{3,2,1,0:T(8,128)(2,1)S(1)}, u32[]{:S(2)}, u32[]{:S(2)}) async-start(bf16[16,3,64,128]{3,2,1,0:T(8,128)(2,1)} %broadcast_in_dim.197), calls=%async_computation.8 | async-start | bytes 1572864 | tf_op jit(solution)/shard_map/all_to_all | solution.py:18
  232.6 12.1 %all-to-all-done.8 = bf16[16,3,64,128]{3,2,1,0:T(8,128)(2,1)S(1)} async-done(((bf16[16,3,64,128]{3,2,1,0:T(8,128)(2,1)}), bf16[16,3,64,128]{3,2,1,0:T(8,128)(2,1)S(1)}, u32[]{:S(2)}, u32[]{:S(2)}) %all-to-all-start.8) | async-done | bytes 786464 | tf_op jit(solution)/shard_map/all_to_all | solution.py:18
  245.1 0.8 broadcast_in_dim.202
  245.9 4.8 %all-to-all-start.9 = ((bf16[16,64,256]{2,1,0:T(8,128)(2,1)}), bf16[16,64,256]{2,1,0:T(8,128)(2,1)S(1)}, u32[]{:S(2)}, u32[]{:S(2)}) async-start(bf16[16,64,256]{2,1,0:T(8,128)(2,1)} %broadcast_in_dim.202), calls=%async_computation.9 | async-start | bytes 1048576 | tf_op jit(solution)/shard_map/all_to_all | solution.py:18
  252.0 8.4 %all-to-all-done.9 = bf16[16,64,256]{2,1,0:T(8,128)(2,1)S(1)} async-done(((bf16[16,64,256]{2,1,0:T(8,128)(2,1)}), bf16[16,64,256]{2,1,0:T(8,128)(2,1)S(1)}, u32[]{:S(2)}, u32[]{:S(2)}) %all-to-all-start.9) | async-done | bytes 524320 | tf_op jit(solution)/shard_map/all_to_all | solution.py:18
  260.4 1.7 all-gather.27.cloned.1.call-done
  262.1 2.4 fusion.4
  264.6 0.9 broadcast_in_dim.203
  265.6 7.3 %all-to-all-start.10 = ((bf16[16,2,64,128]{3,2,1,0:T(8,128)(2,1)}), bf16[16,2,64,128]{3,2,1,0:T(8,128)(2,1)S(1)}, u32[]{:S(2)}, u32[]{:S(2)}) async-start(bf16[16,2,64,128]{3,2,1,0:T(8,128)(2,1)} %broadcast_in_dim.203), calls=%async_computation.10 | async-start | bytes 1048576 | tf_op jit(solution)/shard_map/all_to_all | solution.py:18
  274.1 9.3 %all-to-all-done.10 = bf16[16,2,64,128]{3,2,1,0:T(8,128)(2,1)S(1)} async-done(((bf16[16,2,64,128]{3,2,1,0:T(8,128)(2,1)}), bf16[16,2,64,128]{3,2,1,0:T(8,128)(2,1)S(1)}, u32[]{:S(2)}, u32[]{:S(2)}) %all-to-all-start.10) | async-done | bytes 524320 | tf_op jit(solution)/shard_map/all_to_all | solution.py:18
  283.7 14.0 %all_to_all.71 = bf16[16,64,256]{2,1,0:T(8,128)(2,1)S(1)} all-to-all(bf16[16,64,256]{2,1,0:T(8,128)(2,1)S(1)} %broadcast_in_dim.208), channel_id=1, replica_groups=mesh['row'=16,'col'=16] {'col'}, dimensions={0} | all-to-all | bytes 1048576 | tf_op jit(solution)/shard_map/all_to_all | solution.py:18
  297.7 6.3 %all-gather.29.cloned.1.call-done = bf16[1,256,4096]{2,1,0:T(8,128)(2,1)} async-done(((bf16[1,256,256]{2,1,0:T(8,128)(2,1)}), bf16[1,256,4096]{2,1,0:T(8,128)(2,1)}) %all-gather.29.cloned.1.call-update) | async-done | bytes 2097168 | tf_op jit(solution)/shard_map/all_gather | solution.py:83
  304.0 2.4 fusion.2
  307.3 7.3 %all-to-all-start.12 = ((bf16[16,1,64,128]{3,2,1,0:T(8,128)(2,1)}), bf16[16,1,64,128]{3,2,1,0:T(8,128)(2,1)S(1)}, u32[]{:S(2)}, u32[]{:S(2)}) async-start(bf16[16,1,64,128]{3,2,1,0:T(8,128)(2,1)} %broadcast_in_dim.210), calls=%async_computation.12 | async-start | bytes 524288 | tf_op jit(solution)/shard_map/all_to_all | solution.py:18
  314.6 7.7 %all-to-all-done.12 = bf16[16,1,64,128]{3,2,1,0:T(8,128)(2,1)S(1)} async-done(((bf16[16,1,64,128]{3,2,1,0:T(8,128)(2,1)}), bf16[16,1,64,128]{3,2,1,0:T(8,128)(2,1)S(1)}, u32[]{:S(2)}, u32[]{:S(2)}) %all-to-all-start.12) | async-done | bytes 262176 | tf_op jit(solution)/shard_map/all_to_all | solution.py:18
  322.5 13.8 %all_to_all.72 = bf16[16,64,256]{2,1,0:T(8,128)(2,1)S(1)} all-to-all(bf16[16,64,256]{2,1,0:T(8,128)(2,1)S(1)} %broadcast_in_dim.214), channel_id=1, replica_groups=mesh['row'=16,'col'=16] {'col'}, dimensions={0} | all-to-all | bytes 1048576 | tf_op jit(solution)/shard_map/all_to_all | solution.py:18
  336.4 9.5 %all-gather.31.cloned.1.call-done = bf16[1,256,4096]{2,1,0:T(8,128)(2,1)} async-done(((bf16[1,256,256]{2,1,0:T(8,128)(2,1)}), bf16[1,256,4096]{2,1,0:T(8,128)(2,1)}) %all-gather.31.cloned.1.call-update) | async-done | bytes 2097168 | tf_op jit(solution)/shard_map/all_gather | solution.py:83
  345.9 2.3 fusion.24
  (106 shorter events, 20.7 us)
Async XLA Ops:
  6.5 14.4 %copy-start.10 = (s32[3]{0:T(128)S(1)}, s32[3]{0:T(128)}, u32[]{:S(2)}) copy-start(s32[3]{0:T(128)} %constant.313) | copy-start | bytes 40
  6.5 6.0 %copy-start.6 = (f32[4,64,256]{2,1,0:T(8,128)S(1)}, f32[4,64,256]{2,1,0:T(8,128)}, u32[]{:S(2)}) copy-start(f32[4,64,256]{2,1,0:T(8,128)} %param.45) | copy-start | bytes 786436
  6.5 14.4 %copy-start.2 = (bf16[6,256,128]{2,1,0:T(8,128)(2,1)S(1)}, bf16[6,256,128]{2,1,0:T(8,128)(2,1)}, u32[]{:S(2)}) copy-start(bf16[6,256,128]{2,1,0:T(8,128)(2,1)} %param.47) | copy-start | bytes 1179652
  6.5 46.5 %all-gather.17.cloned.1.call-start = ((), (), s32[]{:S(2)}) async-start(), calls=%async_computation.14 | async-start | bytes 2228224 | tf_op jit(solution)/shard_map/all_gather | solution.py:57
  8.5 86.4 %all-gather.19.cloned.1.call-start = ((), (), s32[]{:S(2)}) async-start(), calls=%async_computation.15 | async-start | bytes 2228224 | tf_op jit(solution)/shard_map/all_gather | solution.py:57
  9.3 127.6 %all-gather.21.cloned.1.call-start = ((), (), s32[]{:S(2)}) async-start(), calls=%async_computation.16 | async-start | bytes 2228224 | tf_op jit(solution)/shard_map/all_gather | solution.py:57
  10.0 168.6 %all-gather.23.cloned.1.call-start = ((), (), s32[]{:S(2)}) async-start(), calls=%async_computation.17 | async-start | bytes 2228224 | tf_op jit(solution)/shard_map/all_gather | solution.py:57
  10.6 209.8 %all-gather.25.cloned.1.call-start = ((), (), s32[]{:S(2)}) async-start(), calls=%async_computation.18 | async-start | bytes 2228224 | tf_op jit(solution)/shard_map/all_gather | solution.py:83
  13.4 17.6 %all-to-all-start = ((bf16[16,64,256]{2,1,0:T(8,128)(2,1)}), bf16[16,64,256]{2,1,0:T(8,128)(2,1)S(1)}, u32[]{:S(2)}, u32[]{:S(2)}) async-start(bf16[16,64,256]{2,1,0:T(8,128)(2,1)} %broadcast_in_dim.83), calls=%async_computation | async-start | bytes 1048576 | tf_op jit(solution)/shard_map/all_to_all | solution.py:18
  55.4 9.1 %copy-start.3 = (bf16[6,256,128]{2,1,0:T(8,128)(2,1)S(1)}, bf16[6,256,128]{2,1,0:T(8,128)(2,1)}, u32[]{:S(2)}) copy-start(bf16[6,256,128]{2,1,0:T(8,128)(2,1)} %param.46) | copy-start | bytes 1179652
  55.4 9.7 %copy-start = (s32[6]{0:T(128)S(1)}, s32[6]{0:T(128)}, u32[]{:S(2)}) copy-start(s32[6]{0:T(128)} %param.50) | copy-start | bytes 76
  56.6 20.7 %all-to-all-start.1 = ((bf16[16,3,64,128]{3,2,1,0:T(8,128)(2,1)}), bf16[16,3,64,128]{3,2,1,0:T(8,128)(2,1)S(1)}, u32[]{:S(2)}, u32[]{:S(2)}) async-start(bf16[16,3,64,128]{3,2,1,0:T(8,128)(2,1)} %broadcast_in_dim.85), calls=%async_computation.1 | async-start | bytes 1572864 | tf_op jit(solution)/shard_map/all_to_all | solution.py:18
  63.9 198.2 %all-gather.27.cloned.1.call-start = ((), (), s32[]{:S(2)}) async-start(), calls=%async_computation.19 | async-start | bytes 2228224 | tf_op jit(solution)/shard_map/all_gather | solution.py:83
  64.5 18.8 %copy-start.9 = (s32[2]{0:T(128)S(1)}, s32[2]{0:T(128)}, u32[]{:S(2)}) copy-start(s32[2]{0:T(128)} %constant.316) | copy-start | bytes 28
  78.5 14.5 %all-to-all-start.2 = ((bf16[16,64,256]{2,1,0:T(8,128)(2,1)}), bf16[16,64,256]{2,1,0:T(8,128)(2,1)S(1)}, u32[]{:S(2)}, u32[]{:S(2)}) async-start(bf16[16,64,256]{2,1,0:T(8,128)(2,1)} %broadcast_in_dim.89), calls=%async_computation.2 | async-start | bytes 1048576 | tf_op jit(solution)/shard_map/all_to_all | solution.py:18
  98.4 17.8 %all-to-all-start.3 = ((bf16[16,2,64,128]{3,2,1,0:T(8,128)(2,1)}), bf16[16,2,64,128]{3,2,1,0:T(8,128)(2,1)S(1)}, u32[]{:S(2)}, u32[]{:S(2)}) async-start(bf16[16,2,64,128]{3,2,1,0:T(8,128)(2,1)} %broadcast_in_dim.91), calls=%async_computation.3 | async-start | bytes 1048576 | tf_op jit(solution)/shard_map/all_to_all | solution.py:18
  117.3 14.4 %all-to-all-start.4 = ((bf16[16,64,256]{2,1,0:T(8,128)(2,1)}), bf16[16,64,256]{2,1,0:T(8,128)(2,1)S(1)}, u32[]{:S(2)}, u32[]{:S(2)}) async-start(bf16[16,64,256]{2,1,0:T(8,128)(2,1)} %broadcast_in_dim.187), calls=%async_computation.4 | async-start | bytes 1048576 | tf_op jit(solution)/shard_map/all_to_all | solution.py:18
  122.2 181.8 %all-gather.29.cloned.1.call-start = ((), (), s32[]{:S(2)}) async-start(), calls=%async_computation.20 | async-start | bytes 2228224 | tf_op jit(solution)/shard_map/all_gather | solution.py:83
  140.1 15.0 %all-to-all-start.5 = ((bf16[16,1,64,128]{3,2,1,0:T(8,128)(2,1)}), bf16[16,1,64,128]{3,2,1,0:T(8,128)(2,1)S(1)}, u32[]{:S(2)}, u32[]{:S(2)}) async-start(bf16[16,1,64,128]{3,2,1,0:T(8,128)(2,1)} %broadcast_in_dim.191), calls=%async_computation.5 | async-start | bytes 524288 | tf_op jit(solution)/shard_map/all_to_all | solution.py:18
  178.6 10.5 %copy-start.8 = (s32[3]{0:T(128)S(1)}, s32[3]{0:T(128)}, u32[]{:S(2)}) copy-start(s32[3]{0:T(128)} %constant.319) | copy-start | bytes 40
  178.6 10.5 %copy-start.4 = (bf16[6,256,128]{2,1,0:T(8,128)(2,1)S(1)}, bf16[6,256,128]{2,1,0:T(8,128)(2,1)}, u32[]{:S(2)}) copy-start(bf16[6,256,128]{2,1,0:T(8,128)(2,1)} %param.49) | copy-start | bytes 1179652
  181.8 17.8 %all-to-all-start.7 = ((bf16[16,64,256]{2,1,0:T(8,128)(2,1)}), bf16[16,64,256]{2,1,0:T(8,128)(2,1)S(1)}, u32[]{:S(2)}, u32[]{:S(2)}) async-start(bf16[16,64,256]{2,1,0:T(8,128)(2,1)} %broadcast_in_dim.196), calls=%async_computation.7 | async-start | bytes 1048576 | tf_op jit(solution)/shard_map/all_to_all | solution.py:18
  220.4 10.9 %copy-start.5 = (bf16[6,256,128]{2,1,0:T(8,128)(2,1)S(1)}, bf16[6,256,128]{2,1,0:T(8,128)(2,1)}, u32[]{:S(2)}) copy-start(bf16[6,256,128]{2,1,0:T(8,128)(2,1)} %param.48) | copy-start | bytes 1179652
  222.8 9.2 %copy-start.1 = (s32[6]{0:T(128)S(1)}, s32[6]{0:T(128)}, u32[]{:S(2)}) copy-start(s32[6]{0:T(128)} %param.51) | copy-start | bytes 76
  224.0 20.7 %all-to-all-start.8 = ((bf16[16,3,64,128]{3,2,1,0:T(8,128)(2,1)}), bf16[16,3,64,128]{3,2,1,0:T(8,128)(2,1)S(1)}, u32[]{:S(2)}, u32[]{:S(2)}) async-start(bf16[16,3,64,128]{3,2,1,0:T(8,128)(2,1)} %broadcast_in_dim.197), calls=%async_computation.8 | async-start | bytes 1572864 | tf_op jit(solution)/shard_map/all_to_all | solution.py:18
  231.3 20.1 %copy-start.7 = (s32[2]{0:T(128)S(1)}, s32[2]{0:T(128)}, u32[]{:S(2)}) copy-start(s32[2]{0:T(128)} %constant.322) | copy-start | bytes 28
  245.9 14.5 %all-to-all-start.9 = ((bf16[16,64,256]{2,1,0:T(8,128)(2,1)}), bf16[16,64,256]{2,1,0:T(8,128)(2,1)S(1)}, u32[]{:S(2)}, u32[]{:S(2)}) async-start(bf16[16,64,256]{2,1,0:T(8,128)(2,1)} %broadcast_in_dim.202), calls=%async_computation.9 | async-start | bytes 1048576 | tf_op jit(solution)/shard_map/all_to_all | solution.py:18
  250.7 95.2 %all-gather.31.cloned.1.call-start = ((), (), s32[]{:S(2)}) async-start(), calls=%async_computation.21 | async-start | bytes 2228224 | tf_op jit(solution)/shard_map/all_gather | solution.py:83
  265.6 17.9 %all-to-all-start.10 = ((bf16[16,2,64,128]{3,2,1,0:T(8,128)(2,1)}), bf16[16,2,64,128]{3,2,1,0:T(8,128)(2,1)S(1)}, u32[]{:S(2)}, u32[]{:S(2)}) async-start(bf16[16,2,64,128]{3,2,1,0:T(8,128)(2,1)} %broadcast_in_dim.203), calls=%async_computation.10 | async-start | bytes 1048576 | tf_op jit(solution)/shard_map/all_to_all | solution.py:18
  307.3 15.0 %all-to-all-start.12 = ((bf16[16,1,64,128]{3,2,1,0:T(8,128)(2,1)}), bf16[16,1,64,128]{3,2,1,0:T(8,128)(2,1)S(1)}, u32[]{:S(2)}, u32[]{:S(2)}) async-start(bf16[16,1,64,128]{3,2,1,0:T(8,128)(2,1)} %broadcast_in_dim.210), calls=%async_computation.12 | async-start | bytes 524288 | tf_op jit(solution)/shard_map/all_to_all | solution.py:18
Sparse Core Ops, SparseCore 0:
  9.1 43.8 all-gather.16
  54.8 40.1 all-gather.18
  96.7 40.0 all-gather.20
  138.4 40.0 all-gather.22
  180.2 40.1 all-gather.24
  222.0 40.1 all-gather.26
  263.9 40.0 all-gather.28
  305.7 40.1 all-gather.30
where the time goes:
time: 359 us; the launch traced here: 356 us
  waiting for transfers between devices  182 us (51%)
  starting transfers between devices  73 us (20%)
  blocking collectives  41.6 us (12%)
  local copies, waits for them, and re-layouts  21.9 us (6%)
  matrix products  20.8 us (6%)
  between operations  14.4 us (4%)
    all_to_all x11, waiting for transfers between devices, from_everyone(): lax.all_to_all(jnp.broadcast_to(value[None], (length, *value.shape)), axi...  102 us
    all_to_all x11, starting transfers between devices, from_everyone(): lax.all_to_all(jnp.broadcast_to(value[None], (length, *value.shape)), axi...  72.7 us
    all_to_all x3, blocking collectives, from_everyone(): lax.all_to_all(jnp.broadcast_to(value[None], (length, *value.shape)), axi...  41.6 us
    all_gather x4, waiting for transfers between devices, shards(): lax.all_gather(inv_lower[section], 'row', axis=1, tiled=True)  38.2 us
    all_gather x4, waiting for transfers between devices, shards(): lax.all_gather(inv_upper[section], 'row', axis=1, tiled=True)  38.2 us
    dot_general x8, matrix products, times_inverse(): lax.dot_general(block, inverse, (((1,), (1,)), ((), ())), preferred_eleme...  18.9 us
    broadcast_in_dim x19, local copies, waits for them, and re-layouts, from_everyone(): jnp.broadcast_to(value[None], (length, *value.shape))  9.98 us
  transfers between devices with their start and end apart: 19, of which 19 were waited for; matrix products, arithmetic and copies ran while one was open for 11% of the time, Pallas kernels for 0%

commit v1 on v0

v1 whole, which is shorter than its diff:
```python
import jax
import jax.numpy as jnp
from jax import lax
from jax.sharding import PartitionSpec as P

RBLK = 32
BF16 = jnp.bfloat16
F32 = jnp.float32


def from_everyone(value, axis):
    length = lax.axis_size(axis)
    return lax.all_to_all(
        jnp.broadcast_to(value[None], (length, *value.shape)), axis, 0, 0, tiled=True
    )


def matmul(left, right):
    return jnp.dot(left, right, preferred_element_type=F32)


def lower_pair(i, j):
    return i * (i - 1) // 2 + j


def gather_inverse(inverse, group):
    rows = lax.axis_size("row")
    groups = [list(range(s, s + group)) for s in range(0, rows, group)]
    return lax.all_gather(inverse, "row", axis=0, axis_index_groups=groups)


def batched_products(rows, sizes, inverse, group):
    n_rows, n_cols = lax.axis_size("row"), lax.axis_size("col")
    spans = n_rows // group
    inner = n_cols // spans
    moves = []
    for r in range(n_rows):
        for c in range(n_cols):
            to_row = (c // inner) * group + r % group
            to_col = (r // group) * inner + c % inner
            moves.append((r * n_cols + c, to_row * n_cols + to_col))
    swapped = lax.ppermute(rows, ("row", "col"), moves)
    everything = from_everyone(swapped, "col")
    everything = everything.reshape(spans, inner, *rows.shape)
    parts = []
    start = 0
    for tile, size in enumerate(sizes):
        block = everything[:, :, start : start + size]
        parts.append(
            jnp.einsum(
                "sjnw,jaw->sna", block, inverse[:, tile], preferred_element_type=F32
            ).astype(BF16)
        )
        start += size
    partial = jnp.concatenate(parts, axis=1)
    groups = [[s * group + j for s in range(spans)] for j in range(group)]
    received = lax.all_to_all(
        partial, "row", 0, 0, tiled=True, axis_index_groups=groups
    )
    return jnp.sum(received.astype(F32), axis=0)


def summed_over_col(partial):
    length = lax.axis_size("col")
    received = lax.all_to_all(partial.astype(BF16), "col", 0, 0, tiled=True)
    received = received.reshape(length, -1, received.shape[-1])
    mine = jnp.sum(received.astype(F32), axis=0).astype(BF16)
    return from_everyone(mine, "col").reshape(partial.shape)


def sweep(tiles, order, pair, left, right, ranks, inverse, group):
    count = len(order)
    place = {tile: at for at, tile in enumerate(order)}
    before = {tile: order[: place[tile]] for tile in order}
    after = {tile: order[place[tile] + 1 :] for tile in order}
    n, width = tiles[0].shape
    rank_cols = left.shape[2]
    share = rank_cols // lax.axis_size("row")
    mine = lax.axis_index("row") * share
    slices = lax.dynamic_slice_in_dim(left, mine, share, axis=2).transpose(0, 2, 1)
    rows, sizes = [], []
    for tile in range(count):
        rows.append(tiles[tile].astype(BF16))
        for source in before[tile]:
            rows.append(slices[pair(tile, source)])
        sizes.append(n + share * len(before[tile]))
    solved = batched_products(jnp.concatenate(rows, axis=0), sizes, inverse, group)
    dense, extra, extra_at = [], [], {}
    start = 0
    for tile in range(count):
        dense.append(solved[start : start + n])
        for at, source in enumerate(before[tile]):
            extra_at[tile, source] = len(extra)
            extra.append(solved[start + n + share * at : start + n + share * (at + 1)])
        start += sizes[tile]
    extra = from_everyone(jnp.stack(extra).astype(BF16), "row")
    extra = extra.transpose(1, 0, 2, 3).reshape(-1, rank_cols, width)
    projections, at_rows = [], {}
    start = 0
    for tile in order:
        factors = {i: right[pair(i, tile)] for i in after[tile]}
        for i in after[tile]:
            projections.append(matmul(dense[tile].astype(BF16), factors[i]))
            at_rows[i, tile] = start
            start += n
            for source in before[tile]:
                projections.append(matmul(extra[extra_at[tile, source]], factors[i]))
                at_rows[i, tile, source] = start
                start += rank_cols
    sums = summed_over_col(jnp.concatenate(projections, axis=0))
    columns = jnp.arange(rank_cols, dtype=jnp.int32)
    masked = {}
    results = [None] * count
    for tile in order:
        value = dense[tile]
        for source in before[tile]:
            value = value - matmul(masked[tile, source], extra[extra_at[tile, source]])
        results[tile] = value
        for i in after[tile]:
            at = at_rows[i, tile]
            projected = sums[at : at + n].astype(F32)
            for source in before[tile]:
                at = at_rows[i, tile, source]
                projected = projected - matmul(
                    masked[tile, source], sums[at : at + rank_cols]
                )
            keep = (columns < RBLK * ranks[pair(i, tile)]).astype(F32)
            masked[i, tile] = (projected * keep[None, :]).astype(BF16)
    return results


def shards(
    right_sides, low_left, low_right, up_left, up_right, low_ranks, up_ranks, inv_lower, inv_upper
):
    count = right_sides.shape[0]
    group = 4
    lower = gather_inverse(inv_lower, group)
    upper = gather_inverse(inv_upper, group)
    tiles = [right_sides[tile] for tile in range(count)]
    forward = sweep(
        tiles, list(range(count)), lower_pair, low_left, low_right, low_ranks, lower, group
    )
    solved = sweep(
        forward,
        list(range(count))[::-1],
        lambda i, j: lower_pair(j, i),
        up_left,
        up_right,
        up_ranks,
        upper,
        group,
    )
    return jnp.stack(solved)


def solution(mesh):
    in_specs = (
        P(None, "row", "col"),
        P(None, "col", None),
        P(None, "col", None),
        P(None, "col", None),
        P(None, "col", None),
        P(),
        P(),
        P(None, "col", "row"),
        P(None, "col", "row"),
    )
    out_specs = P(None, "row", "col")
    return jax.shard_map(shards, mesh=mesh, in_specs=in_specs, out_specs=out_specs, check_vma=False)
```

time: 359 us -> 291 us (0.81)
  waiting for transfers between devices: 182 us -> 111 us
  local copies, waits for them, and re-layouts: 21.9 us -> 8.24 us
  blocking collectives: 41.6 us -> 55.2 us
  starting transfers between devices: 73 us -> 64.8 us
  between operations: 14.4 us -> 21.5 us
  matrix products: 20.8 us -> 25.1 us
    all_gather x8 -> x2, waiting for transfers between devices: 76.4 us -> 0.01 us  [gather_inverse(): return lax.all_gather(inverse, 'row', axis=0, axis_index_groups=groups)]
    all_to_all x0 -> x4, waiting for transfers between devices: none -> 38.2 us  [the longest x2 22.5 us: batched_products(): lax.all_to_all(partial, 'row', 0, 0, tiled=True, axis_index_groups=groups)]
    all_to_all x11 -> x5, starting transfers between devices: 72.7 us -> 36.2 us  [from_everyone(): lax.all_to_all(jnp.broadcast_to(value[None], (length, *value.shape)), axi...]
    all_to_all x11 -> x5, waiting for transfers between devices: 102 us -> 71.3 us  [from_everyone(): lax.all_to_all(jnp.broadcast_to(value[None], (length, *value.shape)), axi...]
    all_to_all x0 -> x4, starting transfers between devices: none -> 27.3 us  [the longest x2 14 us: batched_products(): lax.all_to_all(partial, 'row', 0, 0, tiled=True, axis_index_groups=groups)]
    all_to_all x3 -> x1, blocking collectives: 41.6 us -> 55.2 us  [from_everyone(): lax.all_to_all(jnp.broadcast_to(value[None], (length, *value.shape)), axi...]
    gather x13 -> x0, local copies, waits for them, and re-layouts: 7.74 us -> none  [the longest x5 3.11 us: rank_mask(): ranks[pair_index][:, None]]
    broadcast_in_dim x19 -> x6, local copies, waits for them, and re-layouts: 9.98 us -> 4.76 us  [from_everyone(): jnp.broadcast_to(value[None], (length, *value.shape))]
  transfers between devices with their start and end apart: 19 -> 13, of which waited for: 19 -> 9; matrix products, arithmetic and copies ran while one was open for 11% -> 7% of each run, Pallas kernels for 0% -> 0%
where the time goes in v1:
time: 291 us; the launch traced here: 289 us
  waiting for transfers between devices  111 us (38%)
  starting transfers between devices  64.8 us (22%)
  blocking collectives  55.2 us (19%)
  matrix products  25.1 us (9%)
  between operations  21.5 us (7%)
  local copies, waits for them, and re-layouts  8.24 us (3%)
    all_to_all x5, waiting for transfers between devices, from_everyone(): lax.all_to_all(jnp.broadcast_to(value[None], (length, *value.shape)), axi...  71.3 us
    all_to_all x1, blocking collectives, from_everyone(): lax.all_to_all(jnp.broadcast_to(value[None], (length, *value.shape)), axi...  55.2 us
    all_to_all x5, starting transfers between devices, from_everyone(): lax.all_to_all(jnp.broadcast_to(value[None], (length, *value.shape)), axi...  36.2 us
    all_to_all x2, waiting for transfers between devices, batched_products(): lax.all_to_all(partial, 'row', 0, 0, tiled=True, axis_index_groups=groups)  22.5 us
    dot_general x36, matrix products, matmul(): return jnp.dot(left, right, preferred_element_type=F32)  17.8 us
    all_to_all x2, waiting for transfers between devices, summed_over_col(): received = lax.all_to_all(partial.astype(BF16), 'col', 0, 0, tiled=True)  15.7 us
    all_to_all x2, starting transfers between devices, batched_products(): lax.all_to_all(partial, 'row', 0, 0, tiled=True, axis_index_groups=groups)  14 us
    all_to_all x2, starting transfers between devices, summed_over_col(): received = lax.all_to_all(partial.astype(BF16), 'col', 0, 0, tiled=True)  13.2 us
  transfers between devices with their start and end apart: 13, of which 9 were waited for; matrix products, arithmetic and copies ran while one was open for 7% of the time, Pallas kernels for 0%

profile of v1, /device:TPU:2, one launch (start us, length us, event | category | flops | bytes accessed | tf_op | source)
XLA Modules:
  0.0 288.7 jit_solution(6739743460674311953)
XLA Ops:
  7.3 1.4 dynamic-slice_bitcast_fusion
  10.2 55.2 %all_to_all.52 = bf16[16,304,256]{2,1,0:T(8,128)(2,1)S(1)} all-to-all(bf16[16,304,256]{2,1,0:T(8,128)(2,1)S(1)} %broadcast_in_dim.12), channel_id=1, replica_groups=mesh['row'=16,'col'=16] {'col'}, dimensions={0} | all-to-all | bytes 4980736 | tf_op jit(solution)/shard_map/all_to_all | solution.py:13
  65.3 1.6 fusion
  66.9 1.4 fusion.2
  69.0 0.9 pad_maximum_fusion
  69.9 7.0 %all-to-all-start.1 = ((bf16[4,304,256]{2,1,0:T(8,128)(2,1)}), bf16[4,304,256]{2,1,0:T(8,128)(2,1)S(1)}, u32[]{:S(2)}, u32[]{:S(2)}) async-start(bf16[4,304,256]{2,1,0:T(8,128)(2,1)} %pad_maximum_fusion), calls=%async_computation.1 | async-start | bytes 1245184 | tf_op jit(solution)/shard_map/all_to_all | solution.py:57
  82.3 10.2 %all-to-all-done.1 = bf16[4,304,256]{2,1,0:T(8,128)(2,1)S(1)} async-done(((bf16[4,304,256]{2,1,0:T(8,128)(2,1)}), bf16[4,304,256]{2,1,0:T(8,128)(2,1)S(1)}, u32[]{:S(2)}, u32[]{:S(2)}) %all-to-all-start.1) | async-done | bytes 622624 | tf_op jit(solution)/shard_map/all_to_all | solution.py:57
  92.6 0.7 fusion.48
  93.4 0.8 broadcast_in_dim.13
  94.2 4.4 %all-to-all-start.2 = ((bf16[16,6,8,256]{3,2,1,0:T(8,128)(2,1)}), bf16[16,6,8,256]{3,2,1,0:T(8,128)(2,1)S(1)}, u32[]{:S(2)}, u32[]{:S(2)}) async-start(bf16[16,6,8,256]{3,2,1,0:T(8,128)(2,1)} %broadcast_in_dim.13), calls=%async_computation.2 | async-start | bytes 786432 | tf_op jit(solution)/shard_map/all_to_all | solution.py:13
  98.6 0.7 fusion.47
  99.3 0.7 fusion.46
  100.1 0.7 fusion.45
  100.8 16.2 %all-to-all-done.2 = bf16[16,6,8,256]{3,2,1,0:T(8,128)(2,1)S(1)} async-done(((bf16[16,6,8,256]{3,2,1,0:T(8,128)(2,1)}), bf16[16,6,8,256]{3,2,1,0:T(8,128)(2,1)S(1)}, u32[]{:S(2)}, u32[]{:S(2)}) %all-to-all-start.2) | async-done | bytes 393248 | tf_op jit(solution)/shard_map/all_to_all | solution.py:13
  117.0 0.8 fusion.24
  117.8 0.7 fusion.44
  118.5 0.8 fusion.23
  119.3 0.7 fusion.43
  120.0 0.8 fusion.22
  120.8 0.8 fusion.21
  121.6 4.9 %all-to-all-start.3 = ((bf16[16,56,128]{2,1,0:T(8,128)(2,1)}), bf16[16,56,128]{2,1,0:T(8,128)(2,1)S(1)}, u32[]{:S(2)}, u32[]{:S(2)}) async-start(bf16[16,56,128]{2,1,0:T(8,128)(2,1)} %bitcast.49), calls=%async_computation.3 | async-start | bytes 458752 | tf_op jit(solution)/shard_map/all_to_all | solution.py:65
  126.5 7.5 %all-to-all-done.3 = bf16[16,56,128]{2,1,0:T(8,128)(2,1)S(1)} async-done(((bf16[16,56,128]{2,1,0:T(8,128)(2,1)}), bf16[16,56,128]{2,1,0:T(8,128)(2,1)S(1)}, u32[]{:S(2)}, u32[]{:S(2)}) %all-to-all-start.3) | async-done | bytes 229408 | tf_op jit(solution)/shard_map/all_to_all | solution.py:65
  134.8 4.8 %all-to-all-start.4 = ((bf16[16,56,128]{2,1,0:T(8,128)(2,1)}), bf16[16,56,128]{2,1,0:T(8,128)(2,1)S(1)}, u32[]{:S(2)}, u32[]{:S(2)}) async-start(bf16[16,56,128]{2,1,0:T(8,128)(2,1)} %broadcast_in_dim.14), calls=%async_computation.4 | async-start | bytes 458752 | tf_op jit(solution)/shard_map/all_to_all | solution.py:13
  139.5 7.2 %all-to-all-done.4 = bf16[16,56,128]{2,1,0:T(8,128)(2,1)S(1)} async-done(((bf16[16,56,128]{2,1,0:T(8,128)(2,1)}), bf16[16,56,128]{2,1,0:T(8,128)(2,1)S(1)}, u32[]{:S(2)}, u32[]{:S(2)}) %all-to-all-start.4) | async-done | bytes 229408 | tf_op jit(solution)/shard_map/all_to_all | solution.py:13
  148.9 1.6 broadcast_in_dim.15
  150.5 18.8 %all-to-all-start.5 = ((bf16[16,304,256]{2,1,0:T(8,128)(2,1)}), bf16[16,304,256]{2,1,0:T(8,128)(2,1)S(1)}, u32[]{:S(2)}, u32[]{:S(2)}) async-start(bf16[16,304,256]{2,1,0:T(8,128)(2,1)} %broadcast_in_dim.15), calls=%async_computation.5 | async-start | bytes 4980736 | tf_op jit(solution)/shard_map/all_to_all | solution.py:13
  169.3 29.7 %all-to-all-done.5 = bf16[16,304,256]{2,1,0:T(8,128)(2,1)S(1)} async-done(((bf16[16,304,256]{2,1,0:T(8,128)(2,1)}), bf16[16,304,256]{2,1,0:T(8,128)(2,1)S(1)}, u32[]{:S(2)}, u32[]{:S(2)}) %all-to-all-start.5) | async-done | bytes 2490400 | tf_op jit(solution)/shard_map/all_to_all | solution.py:13
  199.0 1.6 fusion.1
  200.5 1.4 fusion.3
  202.7 0.9 pad_maximum_fusion.1
  203.6 7.1 %all-to-all-start.6 = ((bf16[4,304,256]{2,1,0:T(8,128)(2,1)}), bf16[4,304,256]{2,1,0:T(8,128)(2,1)S(1)}, u32[]{:S(2)}, u32[]{:S(2)}) async-start(bf16[4,304,256]{2,1,0:T(8,128)(2,1)} %pad_maximum_fusion.1), calls=%async_computation.6 | async-start | bytes 1245184 | tf_op jit(solution)/shard_map/all_to_all | solution.py:57
  215.2 12.3 %all-to-all-done.6 = bf16[4,304,256]{2,1,0:T(8,128)(2,1)S(1)} async-done(((bf16[4,304,256]{2,1,0:T(8,128)(2,1)}), bf16[4,304,256]{2,1,0:T(8,128)(2,1)S(1)}, u32[]{:S(2)}, u32[]{:S(2)}) %all-to-all-start.6) | async-done | bytes 622624 | tf_op jit(solution)/shard_map/all_to_all | solution.py:57
  227.7 0.8 broadcast_in_dim.16
  228.4 3.6 %all-to-all-start.7 = ((bf16[16,6,8,256]{3,2,1,0:T(8,128)(2,1)}), bf16[16,6,8,256]{3,2,1,0:T(8,128)(2,1)S(1)}, u32[]{:S(2)}, u32[]{:S(2)}) async-start(bf16[16,6,8,256]{3,2,1,0:T(8,128)(2,1)} %broadcast_in_dim.16), calls=%async_computation.7 | async-start | bytes 786432 | tf_op jit(solution)/shard_map/all_to_all | solution.py:13
  232.0 0.7 fusion.42
  232.8 0.7 fusion.41
  234.2 0.7 fusion.39
  235.0 10.6 %all-to-all-done.7 = bf16[16,6,8,256]{3,2,1,0:T(8,128)(2,1)S(1)} async-done(((bf16[16,6,8,256]{3,2,1,0:T(8,128)(2,1)}), bf16[16,6,8,256]{3,2,1,0:T(8,128)(2,1)S(1)}, u32[]{:S(2)}, u32[]{:S(2)}) %all-to-all-start.7) | async-done | bytes 393248 | tf_op jit(solution)/shard_map/all_to_all | solution.py:13
  245.5 0.8 fusion.20
  246.3 0.7 fusion.38
  247.1 0.8 fusion.19
  247.8 0.7 fusion.37
  248.6 0.8 fusion.18
  249.3 0.8 fusion.17
  250.1 8.4 %all-to-all-start.8 = ((bf16[16,56,128]{2,1,0:T(8,128)(2,1)}), bf16[16,56,128]{2,1,0:T(8,128)(2,1)S(1)}, u32[]{:S(2)}, u32[]{:S(2)}) async-start(bf16[16,56,128]{2,1,0:T(8,128)(2,1)} %bitcast.97), calls=%async_computation.8 | async-start | bytes 458752 | tf_op jit(solution)/shard_map/all_to_all | solution.py:65
  258.5 8.1 %all-to-all-done.8 = bf16[16,56,128]{2,1,0:T(8,128)(2,1)S(1)} async-done(((bf16[16,56,128]{2,1,0:T(8,128)(2,1)}), bf16[16,56,128]{2,1,0:T(8,128)(2,1)S(1)}, u32[]{:S(2)}, u32[]{:S(2)}) %all-to-all-start.8) | async-done | bytes 229408 | tf_op jit(solution)/shard_map/all_to_all | solution.py:65
  267.4 4.8 %all-to-all-start.9 = ((bf16[16,56,128]{2,1,0:T(8,128)(2,1)}), bf16[16,56,128]{2,1,0:T(8,128)(2,1)S(1)}, u32[]{:S(2)}, u32[]{:S(2)}) async-start(bf16[16,56,128]{2,1,0:T(8,128)(2,1)} %broadcast_in_dim.17), calls=%async_computation.9 | async-start | bytes 458752 | tf_op jit(solution)/shard_map/all_to_all | solution.py:13
  272.1 7.6 %all-to-all-done.9 = bf16[16,56,128]{2,1,0:T(8,128)(2,1)S(1)} async-done(((bf16[16,56,128]{2,1,0:T(8,128)(2,1)}), bf16[16,56,128]{2,1,0:T(8,128)(2,1)S(1)}, u32[]{:S(2)}, u32[]{:S(2)}) %all-to-all-start.9) | async-done | bytes 229408 | tf_op jit(solution)/shard_map/all_to_all | solution.py:13
  (106 shorter events, 12.4 us)
Async XLA Ops:
  6.5 2.2 copy-start.1
  6.5 58.8 %all-gather.5.cloned.1.call-start = ((), (), s32[]{:S(2)}) async-start(), calls=%async_computation.10 | async-start | bytes 2621440 | tf_op jit(solution)/shard_map/all_gather | solution.py:29
  9.3 0.7 collective-permute-start
  65.3 3.0 %copy-start.6 = (bf16[16,256,256]{2,1,0:T(8,128)(2,1)S(1)}, bf16[16,256,256]{2,1,0:T(8,128)(2,1)}, u32[]{:S(2)}) copy-start(bf16[16,256,256]{2,1,0:T(8,128)(2,1)} %all-gather.5.cloned.1.call-done) | copy-start | bytes 6291460
  68.7 8.9 %copy-start.3 = (s32[6]{0:T(128)S(1)}, s32[6]{0:T(128)}, u32[]{:S(2)}) copy-start(s32[6]{0:T(128)} %param.14) | copy-start | bytes 76
  69.9 22.7 %copy-start.2 = (bf16[6,256,128]{2,1,0:T(8,128)(2,1)S(1)}, bf16[6,256,128]{2,1,0:T(8,128)(2,1)}, u32[]{:S(2)}) copy-start(bf16[6,256,128]{2,1,0:T(8,128)(2,1)} %param.11) | copy-start | bytes 1179652
  69.9 22.6 %all-to-all-start.1 = ((bf16[4,304,256]{2,1,0:T(8,128)(2,1)}), bf16[4,304,256]{2,1,0:T(8,128)(2,1)S(1)}, u32[]{:S(2)}, u32[]{:S(2)}) async-start(bf16[4,304,256]{2,1,0:T(8,128)(2,1)} %pad_maximum_fusion), calls=%async_computation.1 | async-start | bytes 1245184 | tf_op jit(solution)/shard_map/all_to_all | solution.py:57
  76.9 92.4 %all-gather.7.cloned.1.call-start = ((), (), s32[]{:S(2)}) async-start(), calls=%async_computation.11 | async-start | bytes 2621440 | tf_op jit(solution)/shard_map/all_gather | solution.py:29
  94.2 22.8 %all-to-all-start.2 = ((bf16[16,6,8,256]{3,2,1,0:T(8,128)(2,1)}), bf16[16,6,8,256]{3,2,1,0:T(8,128)(2,1)S(1)}, u32[]{:S(2)}, u32[]{:S(2)}) async-start(bf16[16,6,8,256]{3,2,1,0:T(8,128)(2,1)} %broadcast_in_dim.13), calls=%async_computation.2 | async-start | bytes 786432 | tf_op jit(solution)/shard_map/all_to_all | solution.py:13
  121.6 12.4 %all-to-all-start.3 = ((bf16[16,56,128]{2,1,0:T(8,128)(2,1)}), bf16[16,56,128]{2,1,0:T(8,128)(2,1)S(1)}, u32[]{:S(2)}, u32[]{:S(2)}) async-start(bf16[16,56,128]{2,1,0:T(8,128)(2,1)} %bitcast.49), calls=%async_computation.3 | async-start | bytes 458752 | tf_op jit(solution)/shard_map/all_to_all | solution.py:65
  134.8 12.0 %all-to-all-start.4 = ((bf16[16,56,128]{2,1,0:T(8,128)(2,1)}), bf16[16,56,128]{2,1,0:T(8,128)(2,1)S(1)}, u32[]{:S(2)}, u32[]{:S(2)}) async-start(bf16[16,56,128]{2,1,0:T(8,128)(2,1)} %broadcast_in_dim.14), calls=%async_computation.4 | async-start | bytes 458752 | tf_op jit(solution)/shard_map/all_to_all | solution.py:13
  148.2 0.7 collective-permute-start.1
  150.5 48.5 %all-to-all-start.5 = ((bf16[16,304,256]{2,1,0:T(8,128)(2,1)}), bf16[16,304,256]{2,1,0:T(8,128)(2,1)S(1)}, u32[]{:S(2)}, u32[]{:S(2)}) async-start(bf16[16,304,256]{2,1,0:T(8,128)(2,1)} %broadcast_in_dim.15), calls=%async_computation.5 | async-start | bytes 4980736 | tf_op jit(solution)/shard_map/all_to_all | solution.py:13
  198.9 3.0 %copy-start.5 = (bf16[16,256,256]{2,1,0:T(8,128)(2,1)S(1)}, bf16[16,256,256]{2,1,0:T(8,128)(2,1)}, u32[]{:S(2)}) copy-start(bf16[16,256,256]{2,1,0:T(8,128)(2,1)} %all-gather.7.cloned.1.call-done) | copy-start | bytes 6291460
  202.3 8.3 %copy-start.4 = (s32[6]{0:T(128)S(1)}, s32[6]{0:T(128)}, u32[]{:S(2)}) copy-start(s32[6]{0:T(128)} %param.15) | copy-start | bytes 76
  203.6 28.4 %copy-start = (bf16[6,256,128]{2,1,0:T(8,128)(2,1)S(1)}, bf16[6,256,128]{2,1,0:T(8,128)(2,1)}, u32[]{:S(2)}) copy-start(bf16[6,256,128]{2,1,0:T(8,128)(2,1)} %param.13) | copy-start | bytes 1179652
  203.6 23.9 %all-to-all-start.6 = ((bf16[4,304,256]{2,1,0:T(8,128)(2,1)}), bf16[4,304,256]{2,1,0:T(8,128)(2,1)S(1)}, u32[]{:S(2)}, u32[]{:S(2)}) async-start(bf16[4,304,256]{2,1,0:T(8,128)(2,1)} %pad_maximum_fusion.1), calls=%async_computation.6 | async-start | bytes 1245184 | tf_op jit(solution)/shard_map/all_to_all | solution.py:57
  228.4 17.1 %all-to-all-start.7 = ((bf16[16,6,8,256]{3,2,1,0:T(8,128)(2,1)}), bf16[16,6,8,256]{3,2,1,0:T(8,128)(2,1)S(1)}, u32[]{:S(2)}, u32[]{:S(2)}) async-start(bf16[16,6,8,256]{3,2,1,0:T(8,128)(2,1)} %broadcast_in_dim.16), calls=%async_computation.7 | async-start | bytes 786432 | tf_op jit(solution)/shard_map/all_to_all | solution.py:13
  250.1 16.5 %all-to-all-start.8 = ((bf16[16,56,128]{2,1,0:T(8,128)(2,1)}), bf16[16,56,128]{2,1,0:T(8,128)(2,1)S(1)}, u32[]{:S(2)}, u32[]{:S(2)}) async-start(bf16[16,56,128]{2,1,0:T(8,128)(2,1)} %bitcast.97), calls=%async_computation.8 | async-start | bytes 458752 | tf_op jit(solution)/shard_map/all_to_all | solution.py:65
  267.4 12.4 %all-to-all-start.9 = ((bf16[16,56,128]{2,1,0:T(8,128)(2,1)}), bf16[16,56,128]{2,1,0:T(8,128)(2,1)S(1)}, u32[]{:S(2)}, u32[]{:S(2)}) async-start(bf16[16,56,128]{2,1,0:T(8,128)(2,1)} %broadcast_in_dim.17), calls=%async_computation.9 | async-start | bytes 458752 | tf_op jit(solution)/shard_map/all_to_all | solution.py:13
Sparse Core Ops, SparseCore 0:
  9.2 34.9 all-gather.4
  79.5 38.5 all-gather.6

commit v2 on v0

v2 whole, which is shorter than its diff:
```python
import jax
import jax.numpy as jnp
from jax import lax
from jax.sharding import PartitionSpec as P

RBLK = 32
BF16 = jnp.bfloat16
F32 = jnp.float32
SIDE = 4
X_GROUPS = [[SIDE * y + x for x in range(SIDE)] for y in range(SIDE)]
Y_GROUPS = [[SIDE * y + x for y in range(SIDE)] for x in range(SIDE)]
Q_GROUPS = [[SIDE * q + j for q in range(SIDE)] for j in range(SIDE)]
Z_GROUPS = [[2 * z + core for z in range(8)] for core in range(2)]


def routes(to):
    index = lambda q, j, y, x: (SIDE * q + j) * SIDE * SIDE + SIDE * y + x
    span = range(SIDE)
    return [
        (index(q, j, y, x), index(*to(q, j, y, x)))
        for q in span for j in span for y in span for x in span
    ]


def permuted(value, to):
    return lax.ppermute(value, ("row", "col"), routes(to))


def exchanged(value, axis, groups):
    return lax.all_to_all(value, axis, 0, 0, tiled=True, axis_index_groups=groups)


def from_everyone(value, axis, groups):
    return exchanged(
        jnp.broadcast_to(value[None], (len(groups[0]), *value.shape)), axis, groups
    )


def over_x(value):
    return exchanged(value, "col", X_GROUPS)


def swapped(value):
    return permuted(value, lambda q, j, y, x: (y, j, q, x))


def by_flips(value, j):
    pairs = jnp.concatenate([value[1:2], value[0:1], value[3:4], value[2:3]], axis=0)
    value = jnp.where(j % 2 == 1, pairs, value)
    return jnp.where(j >= 2, jnp.concatenate([value[2:], value[:2]], axis=0), value)


def matmul(left, right):
    return jnp.dot(left, right, preferred_element_type=F32)


def quad_of(value):
    core = lambda q, j, y, x: (q, j ^ 1, y, x)
    near = permuted(value, core)
    far = permuted(value, lambda q, j, y, x: (q, j ^ 2, y, x))
    return jnp.stack([value, near, far, permuted(far, core)])


def tile_of_x(inverse):
    mine = over_x(inverse)
    return quad_of(mine.reshape(-1, mine.shape[-1]))


def solved_rows(rows, inverse, j):
    moved = swapped(by_flips(rows, j))
    everything = from_everyone(moved, "col", Y_GROUPS)
    partial = jnp.einsum(
        "sinw,iaw->sna", everything, inverse, preferred_element_type=F32
    ).astype(BF16)
    received = exchanged(partial, "row", Q_GROUPS)
    return jnp.sum(received.astype(F32), axis=0)


def summed_over_y(value):
    return jnp.sum(from_everyone(value, "col", Y_GROUPS).astype(F32), axis=0)


def gathered_over_row(value, core):
    same = from_everyone(value, "row", Z_GROUPS)
    other = permuted(same, lambda q, j, y, x: (q, j ^ 1, y, x))
    even = jnp.where(core == 0, same, other)
    odd = jnp.where(core == 0, other, same)
    return jnp.stack([even, odd], axis=1)


class Sweep:
    def __init__(self, order, pair, left, right, ranks):
        self.order, self.pair, self.left, self.right, self.ranks = order, pair, left, right, ranks
        self.place = {tile: at for at, tile in enumerate(order)}
        self.before = {tile: order[: self.place[tile]] for tile in order}
        self.after = {tile: order[self.place[tile] + 1 :] for tile in order}
        self.slots = len(order) - 1

    def slotted(self, pieces, sources, towards):
        out = []
        for tile in range(len(self.order)):
            for slot in range(self.slots):
                known = sources[tile]
                if slot >= len(known):
                    out.append(pieces[0])
                elif towards:
                    out.append(pieces[self.pair(tile, known[slot])])
                else:
                    out.append(pieces[self.pair(known[slot], tile)])
        return jnp.stack(out).reshape(len(self.order), self.slots, *pieces.shape[1:])

    def left_rows(self, row):
        share = self.left.shape[2] // lax.axis_size("row")
        mine = lax.dynamic_slice_in_dim(self.left, row * share, share, axis=2)
        slots = self.slotted(mine.transpose(0, 2, 1), self.before, True)
        return slots.reshape(len(self.order), -1, slots.shape[-1])

    def set_right(self):
        got = over_x(self.slotted(self.right, self.after, False))
        self.factors = got.transpose(1, 0, 2, 3).reshape(self.slots, -1, got.shape[-1])

    def set_extra(self, slices, core, x):
        whole = gathered_over_row(slices, core)
        share = slices.shape[0] // self.slots
        whole = whole.reshape(-1, self.slots, share, slices.shape[1])
        self.extra = whole.transpose(1, 0, 2, 3).reshape(self.slots, -1, slices.shape[1])
        second = x == self.order[1]
        one = matmul(self.extra[0], self.factors[0])
        two = matmul(
            jnp.where(second, self.extra[0], self.extra[1]),
            jnp.where(second, self.factors[1], self.factors[0]),
        )
        return jnp.stack([one, two]).astype(BF16)

    def couplings(self, found):
        first, second, third = self.order[:3]
        last = self.order[3]
        self.coupling = {
            (third, second, first): found[second, 0],
            (last, second, first): found[second, 1],
            (last, third, first): found[third, 0],
            (last, third, second): found[third, 1],
        }

    def finish(self, dense, x):
        n = dense.shape[0]
        rank_cols = self.factors.shape[2]
        projected = jnp.einsum(
            "na,sar->snr", dense.astype(BF16), self.factors, preferred_element_type=F32
        )
        sums = summed_over_y(projected.astype(BF16)).astype(BF16)
        sums = from_everyone(sums, "col", X_GROUPS)
        columns = jnp.arange(rank_cols, dtype=jnp.int32)
        masked = {}
        for tile in self.order:
            for slot, i in enumerate(self.after[tile]):
                value = sums[tile, slot].astype(F32)
                for source in self.before[tile]:
                    value = value - matmul(
                        masked[tile, source], self.coupling[i, tile, source]
                    )
                keep = (columns < RBLK * self.ranks[self.pair(i, tile)]).astype(F32)
                masked[i, tile] = (value * keep[None, :]).astype(BF16)
        nothing = jnp.zeros((n, rank_cols), BF16)
        table = []
        for tile in range(len(self.order)):
            known = self.before[tile]
            table.append(
                jnp.concatenate(
                    [
                        masked[tile, known[slot]] if slot < len(known) else nothing
                        for slot in range(self.slots)
                    ],
                    axis=1,
                )
            )
        mine = lax.dynamic_index_in_dim(jnp.stack(table), x, 0, keepdims=False)
        return dense - matmul(mine, self.extra.reshape(-1, self.extra.shape[-1]))


def lower_pair(i, j):
    return i * (i - 1) // 2 + j


def shards(
    right_sides, low_left, low_right, up_left, up_right, low_ranks, up_ranks, inv_lower, inv_upper
):
    count = right_sides.shape[0]
    row, col = lax.axis_index("row"), lax.axis_index("col")
    j, core, x = row % SIDE, row % 2, col % SIDE
    tiles = list(range(count))
    low = Sweep(tiles, lower_pair, low_left, low_right, low_ranks)
    up = Sweep(
        tiles[::-1], lambda i, k: lower_pair(k, i), up_left, up_right, up_ranks
    )
    lower = tile_of_x(inv_lower)
    dense = solved_rows(over_x(right_sides.astype(BF16)), lower, j)

    upper = tile_of_x(inv_upper)
    low.set_right()
    up.set_right()
    low_rows, up_rows = low.left_rows(row), up.left_rows(row)
    share = low_rows.shape[1]
    both = over_x(jnp.concatenate([low_rows, up_rows], axis=1))
    moved = swapped(by_flips(both, j))
    everything = from_everyone(moved, "col", Y_GROUPS)
    partial = jnp.concatenate(
        [
            jnp.einsum(
                "sinw,iaw->sna", everything[:, :, at : at + share], inverse,
                preferred_element_type=F32,
            )
            for at, inverse in ((0, lower), (share, upper))
        ],
        axis=1,
    ).astype(BF16)
    slices = jnp.sum(exchanged(partial, "row", Q_GROUPS).astype(F32), axis=0).astype(BF16)
    couplings = jnp.stack(
        [
            low.set_extra(slices[:share], core, x),
            up.set_extra(slices[share:], core, x),
        ]
    )
    couplings = summed_over_y(couplings).astype(BF16)
    couplings = from_everyone(couplings, "col", X_GROUPS)
    low.couplings(couplings[:, 0])
    up.couplings(couplings[:, 1])

    forward = low.finish(dense, x)
    n = forward.shape[0]
    rows = forward.astype(BF16).reshape(n, SIDE, -1).transpose(1, 0, 2)
    solved = up.finish(solved_rows(rows, upper, j), x)
    rows = solved.astype(BF16).reshape(n, SIDE, -1).transpose(1, 0, 2)
    return over_x(rows).astype(F32)


def solution(mesh):
    in_specs = (
        P(None, "row", "col"),
        P(None, "col", None),
        P(None, "col", None),
        P(None, "col", None),
        P(None, "col", None),
        P(),
        P(),
        P(None, "col", "row"),
        P(None, "col", "row"),
    )
    out_specs = P(None, "row", "col")
    return jax.shard_map(shards, mesh=mesh, in_specs=in_specs, out_specs=out_specs, check_vma=False)
```

time: 359 us -> 316 us (0.88)
  waiting for transfers between devices: 182 us -> 114 us
  starting transfers between devices: 73 us -> 108 us
  blocking collectives: 41.6 us -> 30.9 us
  other arithmetic: 1.56 us -> 8.33 us
  local copies, waits for them, and re-layouts: 21.9 us -> 28.5 us
  between operations: 14.4 us -> 8.25 us
  matrix products: 20.8 us -> 16 us
    all_gather x8 -> x0, waiting for transfers between devices: 76.4 us -> none  [the longest x4 38.2 us: shards(): lax.all_gather(inv_lower[section], 'row', axis=1, tiled=True)]
    all_to_all x11 -> x19, starting transfers between devices: 72.7 us -> 101 us  [exchanged(): lax.all_to_all(value, axis, 0, 0, tiled=True, axis_index_groups=groups)]
    unnamed x22 -> x71, local copies, waits for them, and re-layouts: 0.05 us -> 14.4 us
    all_to_all x11 -> x19, waiting for transfers between devices: 102 us -> 113 us  [exchanged(): lax.all_to_all(value, axis, 0, 0, tiled=True, axis_index_groups=groups)]
    all_to_all x3 -> x2, blocking collectives: 41.6 us -> 30.9 us  [exchanged(): lax.all_to_all(value, axis, 0, 0, tiled=True, axis_index_groups=groups)]
    gather x13 -> x0, local copies, waits for them, and re-layouts: 7.74 us -> none  [the longest x5 3.11 us: rank_mask(): ranks[pair_index][:, None]]
    ppermute x0 -> x11, starting transfers between devices: none -> 7.14 us  [permuted(): return lax.ppermute(value, ('row', 'col'), routes(to))]
    dot_general x20, matrix products: 20.8 us -> 16 us  [the longest x2 5.83 us: solved_rows(): jnp.einsum('sinw,iaw->sna', everything, inverse, preferred_element_type=F32)]
  transfers between devices with their start and end apart: 19 -> 30, of which waited for: 19 -> 19; matrix products, arithmetic and copies ran while one was open for 11% -> 11% of each run, Pallas kernels for 0% -> 0%
where the time goes in v2:
time: 316 us; the launch traced here: 314 us
  waiting for transfers between devices  114 us (36%)
  starting transfers between devices  108 us (34%)
  blocking collectives  30.9 us (10%)
  local copies, waits for them, and re-layouts  28.5 us (9%)
  matrix products  16 us (5%)
  other arithmetic  8.33 us (3%)
  between operations  8.25 us (3%)
    all_to_all x19, waiting for transfers between devices, exchanged(): lax.all_to_all(value, axis, 0, 0, tiled=True, axis_index_groups=groups)  113 us
    all_to_all x19, starting transfers between devices, exchanged(): lax.all_to_all(value, axis, 0, 0, tiled=True, axis_index_groups=groups)  101 us
    all_to_all x2, blocking collectives, exchanged(): lax.all_to_all(value, axis, 0, 0, tiled=True, axis_index_groups=groups)  30.9 us
    unnamed x71, local copies, waits for them, and re-layouts  14.4 us
    broadcast_in_dim x11, local copies, waits for them, and re-layouts, from_everyone(): jnp.broadcast_to(value[None], (len(groups[0]), *value.shape))  7.95 us
    ppermute x11, starting transfers between devices, permuted(): return lax.ppermute(value, ('row', 'col'), routes(to))  7.14 us
  transfers between devices with their start and end apart: 30, of which 19 were waited for; matrix products, arithmetic and copies ran while one was open for 11% of the time, Pallas kernels for 0%

profile of v2, /device:TPU:2, one launch (start us, length us, event | category | flops | bytes accessed | tf_op | source)
XLA Modules:
  0.0 313.9 jit_solution(18283260595307658086)
XLA Ops:
  0.0 1.4 constant_dynamic-slice_fusion
  2.5 5.5 %all-to-all-start.7 = ((bf16[4,48,256]{2,1,0:T(8,128)(2,1)}), bf16[4,48,256]{2,1,0:T(8,128)(2,1)S(1)}, u32[]{:S(2)}, u32[]{:S(2)}) async-start(bf16[4,48,256]{2,1,0:T(8,128)(2,1)} %pad_maximum_fusion.3), calls=%async_computation.7 | async-start | bytes 196608 | tf_op jit(solution)/shard_map/all_to_all | solution.py:30
  20.7 4.8 %all-to-all-start = ((bf16[4,64,256]{2,1,0:T(8,128)(2,1)}), bf16[4,64,256]{2,1,0:T(8,128)(2,1)S(1)}, u32[]{:S(2)}, u32[]{:S(2)}) async-start(bf16[4,64,256]{2,1,0:T(8,128)(2,1)} %convert_element_type.295), calls=%async_computation | async-start | bytes 262144 | tf_op jit(solution)/shard_map/all_to_all | solution.py:30
  25.5 4.5 %all-to-all-done = bf16[4,64,256]{2,1,0:T(8,128)(2,1)S(1)} async-done(((bf16[4,64,256]{2,1,0:T(8,128)(2,1)}), bf16[4,64,256]{2,1,0:T(8,128)(2,1)S(1)}, u32[]{:S(2)}, u32[]{:S(2)}) %all-to-all-start) | async-done | bytes 131104 | tf_op jit(solution)/shard_map/all_to_all | solution.py:30
  30.0 4.9 %all-to-all-start.2 = ((bf16[4,256,256]{2,1,0:T(8,128)(2,1)}), bf16[4,256,256]{2,1,0:T(8,128)(2,1)S(1)}, u32[]{:S(2)}, u32[]{:S(2)}) async-start(bf16[4,256,256]{2,1,0:T(8,128)(2,1)} %param.16), calls=%async_computation.2 | async-start | bytes 1048576 | tf_op jit(solution)/shard_map/all_to_all | solution.py:30
  34.9 6.6 %all-to-all-done.2 = bf16[4,256,256]{2,1,0:T(8,128)(2,1)S(1)} async-done(((bf16[4,256,256]{2,1,0:T(8,128)(2,1)}), bf16[4,256,256]{2,1,0:T(8,128)(2,1)S(1)}, u32[]{:S(2)}, u32[]{:S(2)}) %all-to-all-start.2) | async-done | bytes 524320 | tf_op jit(solution)/shard_map/all_to_all | solution.py:30
  41.5 4.9 %all-to-all-start.9 = ((bf16[4,256,256]{2,1,0:T(8,128)(2,1)}), bf16[4,256,256]{2,1,0:T(8,128)(2,1)S(1)}, u32[]{:S(2)}, u32[]{:S(2)}) async-start(bf16[4,256,256]{2,1,0:T(8,128)(2,1)} %param.17), calls=%async_computation.9 | async-start | bytes 1048576 | tf_op jit(solution)/shard_map/all_to_all | solution.py:30
  47.7 5.3 %all-to-all-done.9 = bf16[4,256,256]{2,1,0:T(8,128)(2,1)S(1)} async-done(((bf16[4,256,256]{2,1,0:T(8,128)(2,1)}), bf16[4,256,256]{2,1,0:T(8,128)(2,1)S(1)}, u32[]{:S(2)}, u32[]{:S(2)}) %all-to-all-start.9) | async-done | bytes 524320 | tf_op jit(solution)/shard_map/all_to_all | solution.py:30
  53.9 10.0 %all-to-all-start.8 = ((bf16[4,4,48,256]{3,2,1,0:T(8,128)(2,1)}), bf16[4,4,48,256]{3,2,1,0:T(8,128)(2,1)S(1)}, u32[]{:S(2)}, u32[]{:S(2)}) async-start(bf16[4,4,48,256]{3,2,1,0:T(8,128)(2,1)} %broadcast_in_dim.25), calls=%async_computation.8 | async-start | bytes 786432 | tf_op jit(solution)/shard_map/all_to_all | solution.py:30
  64.5 1.9 collective-permute-start.2
  67.0 4.2 %all-to-all-done.8 = bf16[4,4,48,256]{3,2,1,0:T(8,128)(2,1)S(1)} async-done(((bf16[4,4,48,256]{3,2,1,0:T(8,128)(2,1)}), bf16[4,4,48,256]{3,2,1,0:T(8,128)(2,1)S(1)}, u32[]{:S(2)}, u32[]{:S(2)}) %all-to-all-start.8) | async-done | bytes 393248 | tf_op jit(solution)/shard_map/all_to_all | solution.py:30
  71.2 4.8 %all-to-all-start.4 = ((bf16[4,3,256,128]{3,2,1,0:T(8,128)(2,1)}), bf16[4,3,256,128]{3,2,1,0:T(8,128)(2,1)S(1)}, u32[]{:S(2)}, u32[]{:S(2)}) async-start(bf16[4,3,256,128]{3,2,1,0:T(8,128)(2,1)} %bitcast.8), calls=%async_computation.4 | async-start | bytes 1572864 | tf_op jit(solution)/shard_map/all_to_all | solution.py:30
  76.6 1.9 collective-permute-start.6
  79.2 4.8 %all-to-all-done.4 = bf16[4,3,256,128]{3,2,1,0:T(8,128)(2,1)S(1)} async-done(((bf16[4,3,256,128]{3,2,1,0:T(8,128)(2,1)}), bf16[4,3,256,128]{3,2,1,0:T(8,128)(2,1)S(1)}, u32[]{:S(2)}, u32[]{:S(2)}) %all-to-all-start.4) | async-done | bytes 786464 | tf_op jit(solution)/shard_map/all_to_all | solution.py:30
  84.0 4.9 %all-to-all-start.13 = ((bf16[4,3,256,128]{3,2,1,0:T(8,128)(2,1)}), bf16[4,3,256,128]{3,2,1,0:T(8,128)(2,1)S(1)}, u32[]{:S(2)}, u32[]{:S(2)}) async-start(bf16[4,3,256,128]{3,2,1,0:T(8,128)(2,1)} %bitcast.51), calls=%async_computation.13 | async-start | bytes 1572864 | tf_op jit(solution)/shard_map/all_to_all | solution.py:30
  90.3 2.8 fusion.2
  93.1 3.9 %all-to-all-done.13 = bf16[4,3,256,128]{3,2,1,0:T(8,128)(2,1)S(1)} async-done(((bf16[4,3,256,128]{3,2,1,0:T(8,128)(2,1)}), bf16[4,3,256,128]{3,2,1,0:T(8,128)(2,1)S(1)}, u32[]{:S(2)}, u32[]{:S(2)}) %all-to-all-start.13) | async-done | bytes 786464 | tf_op jit(solution)/shard_map/all_to_all | solution.py:30
  97.9 11.8 %all-to-all-start.1 = ((bf16[4,4,64,256]{3,2,1,0:T(8,128)(2,1)}), bf16[4,4,64,256]{3,2,1,0:T(8,128)(2,1)S(1)}, u32[]{:S(2)}, u32[]{:S(2)}) async-start(bf16[4,4,64,256]{3,2,1,0:T(8,128)(2,1)} %broadcast_in_dim.22), calls=%async_computation.1 | async-start | bytes 1048576 | tf_op jit(solution)/shard_map/all_to_all | solution.py:30
  109.7 2.2 fusion.3
  112.6 6.1 %all-to-all-done.1 = bf16[4,4,64,256]{3,2,1,0:T(8,128)(2,1)S(1)} async-done(((bf16[4,4,64,256]{3,2,1,0:T(8,128)(2,1)}), bf16[4,4,64,256]{3,2,1,0:T(8,128)(2,1)S(1)}, u32[]{:S(2)}, u32[]{:S(2)}) %all-to-all-start.1) | async-done | bytes 524320 | tf_op jit(solution)/shard_map/all_to_all | solution.py:30
  118.7 7.9 %all-to-all-start.10 = ((bf16[4,48,1024]{2,1,0:T(8,128)(2,1)}), bf16[4,48,1024]{2,1,0:T(8,128)(2,1)S(1)}, u32[]{:S(2)}, u32[]{:S(2)}) async-start(bf16[4,48,1024]{2,1,0:T(8,128)(2,1)} %pad_maximum_fusion.2), calls=%async_computation.10 | async-start | bytes 786432 | tf_op jit(solution)/shard_map/all_to_all | solution.py:30
  126.6 2.9 fusion
  129.5 9.1 %all-to-all-done.10 = bf16[4,48,1024]{2,1,0:T(8,128)(2,1)S(1)} async-done(((bf16[4,48,1024]{2,1,0:T(8,128)(2,1)}), bf16[4,48,1024]{2,1,0:T(8,128)(2,1)S(1)}, u32[]{:S(2)}, u32[]{:S(2)}) %all-to-all-start.10) | async-done | bytes 393248 | tf_op jit(solution)/shard_map/all_to_all | solution.py:30
  138.6 3.5 %all-to-all-start.3 = ((bf16[4,64,1024]{2,1,0:T(8,128)(2,1)}), bf16[4,64,1024]{2,1,0:T(8,128)(2,1)S(1)}, u32[]{:S(2)}, u32[]{:S(2)}) async-start(bf16[4,64,1024]{2,1,0:T(8,128)(2,1)} %fusion), calls=%async_computation.3 | async-start | bytes 1048576 | tf_op jit(solution)/shard_map/all_to_all | solution.py:30
  142.2 12.5 %all-to-all-done.3 = bf16[4,64,1024]{2,1,0:T(8,128)(2,1)S(1)} async-done(((bf16[4,64,1024]{2,1,0:T(8,128)(2,1)}), bf16[4,64,1024]{2,1,0:T(8,128)(2,1)S(1)}, u32[]{:S(2)}, u32[]{:S(2)}) %all-to-all-start.3) | async-done | bytes 524320 | tf_op jit(solution)/shard_map/all_to_all | solution.py:30
  155.4 3.5 %all-to-all-start.12 = ((bf16[8,24,1024]{2,1,0:T(8,128)(2,1)}), bf16[8,24,1024]{2,1,0:T(8,128)(2,1)S(1)}, u32[]{:S(2)}, u32[]{:S(2)}) async-start(bf16[8,24,1024]{2,1,0:T(8,128)(2,1)} %broadcast_in_dim.27), calls=%async_computation.12 | async-start | bytes 786432 | tf_op jit(solution)/shard_map/all_to_all | solution.py:30
  158.9 11.8 %all-to-all-done.12 = bf16[8,24,1024]{2,1,0:T(8,128)(2,1)S(1)} async-done(((bf16[8,24,1024]{2,1,0:T(8,128)(2,1)}), bf16[8,24,1024]{2,1,0:T(8,128)(2,1)S(1)}, u32[]{:S(2)}, u32[]{:S(2)}) %all-to-all-start.12) | async-done | bytes 393248 | tf_op jit(solution)/shard_map/all_to_all | solution.py:30
  171.5 3.5 %all-to-all-start.11 = ((bf16[8,24,1024]{2,1,0:T(8,128)(2,1)}), bf16[8,24,1024]{2,1,0:T(8,128)(2,1)S(1)}, u32[]{:S(2)}, u32[]{:S(2)}) async-start(bf16[8,24,1024]{2,1,0:T(8,128)(2,1)} %broadcast_in_dim.26), calls=%async_computation.11 | async-start | bytes 786432 | tf_op jit(solution)/shard_map/all_to_all | solution.py:30
  176.9 9.8 %all-to-all-done.11 = bf16[8,24,1024]{2,1,0:T(8,128)(2,1)S(1)} async-done(((bf16[8,24,1024]{2,1,0:T(8,128)(2,1)}), bf16[8,24,1024]{2,1,0:T(8,128)(2,1)S(1)}, u32[]{:S(2)}, u32[]{:S(2)}) %all-to-all-start.11) | async-done | bytes 393248 | tf_op jit(solution)/shard_map/all_to_all | solution.py:30
  187.5 5.8 %all-to-all-start.5 = ((bf16[4,3,64,128]{3,2,1,0:T(8,128)(2,1)}), bf16[4,3,64,128]{3,2,1,0:T(8,128)(2,1)}, u32[]{:S(2)}, u32[]{:S(2)}) async-start(bf16[4,3,64,128]{3,2,1,0:T(8,128)(2,1)} %broadcast_in_dim.23), calls=%async_computation.5 | async-start | bytes 393216 | tf_op jit(solution)/shard_map/all_to_all | solution.py:30
  193.2 1.1 select_bitcast_fusion.1
  196.9 2.8 all-to-all-done.5
  200.6 3.5 %all-to-all-start.14 = ((bf16[4,2,2,128,128]{4,3,2,1,0:T(8,128)(2,1)}), bf16[4,2,2,128,128]{4,3,2,1,0:T(8,128)(2,1)S(1)}, u32[]{:S(2)}, u32[]{:S(2)}) async-start(bf16[4,2,2,128,128]{4,3,2,1,0:T(8,128)(2,1)} %broadcast_in_dim.28), calls=%async_computation.14 | async-start | bytes 1048576 | tf_op jit(solution)/shard_map/all_to_all | solution.py:30
  208.1 4.3 %all-to-all-done.14 = bf16[4,2,2,128,128]{4,3,2,1,0:T(8,128)(2,1)S(1)} async-done(((bf16[4,2,2,128,128]{4,3,2,1,0:T(8,128)(2,1)}), bf16[4,2,2,128,128]{4,3,2,1,0:T(8,128)(2,1)S(1)}, u32[]{:S(2)}, u32[]{:S(2)}) %all-to-all-start.14) | async-done | bytes 524320 | tf_op jit(solution)/shard_map/all_to_all | solution.py:30
  213.1 4.8 %all-to-all-start.6 = ((bf16[4,3,64,128]{3,2,1,0:T(8,128)(2,1)}), bf16[4,3,64,128]{3,2,1,0:T(8,128)(2,1)S(1)}, u32[]{:S(2)}, u32[]{:S(2)}) async-start(bf16[4,3,64,128]{3,2,1,0:T(8,128)(2,1)} %broadcast_in_dim.24), calls=%async_computation.6 | async-start | bytes 393216 | tf_op jit(solution)/shard_map/all_to_all | solution.py:30
  219.8 3.0 all-to-all-done.6
  223.7 5.6 %all-to-all-start.15 = ((bf16[4,2,2,128,128]{4,3,2,1,0:T(8,128)(2,1)}), bf16[4,2,2,128,128]{4,3,2,1,0:T(8,128)(2,1)}, u32[]{:S(2)}, u32[]{:S(2)}) async-start(bf16[4,2,2,128,128]{4,3,2,1,0:T(8,128)(2,1)} %broadcast_in_dim.29), calls=%async_computation.15 | async-start | bytes 1048576 | tf_op jit(solution)/shard_map/all_to_all | solution.py:30
  229.8 6.1 %all-to-all-done.15 = bf16[4,2,2,128,128]{4,3,2,1,0:T(8,128)(2,1)} async-done(((bf16[4,2,2,128,128]{4,3,2,1,0:T(8,128)(2,1)}), bf16[4,2,2,128,128]{4,3,2,1,0:T(8,128)(2,1)}, u32[]{:S(2)}, u32[]{:S(2)}) %all-to-all-start.15) | async-done | bytes 524320 | tf_op jit(solution)/shard_map/all_to_all | solution.py:30
  236.0 1.8 slice_bitcast_fusion
  241.9 22.5 %all_to_all.105 = bf16[4,4,64,256]{3,2,1,0:T(8,128)(2,1)S(1)} all-to-all(bf16[4,4,64,256]{3,2,1,0:T(8,128)(2,1)S(1)} %broadcast_in_dim.30), channel_id=1, replica_groups={{0,4,8,12},{1,5,9,13},{2,6,10,14},{3,7,11,15},{16,20,24,28},{17,21,25,2..., dimensions={0} | all-to-all | bytes 1048576 | tf_op jit(solution)/shard_map/all_to_all | solution.py:30
  264.4 2.9 fusion.1
  267.3 3.6 %all-to-all-start.17 = ((bf16[4,64,1024]{2,1,0:T(8,128)(2,1)}), bf16[4,64,1024]{2,1,0:T(8,128)(2,1)S(1)}, u32[]{:S(2)}, u32[]{:S(2)}) async-start(bf16[4,64,1024]{2,1,0:T(8,128)(2,1)} %fusion.1), calls=%async_computation.17 | async-start | bytes 1048576 | tf_op jit(solution)/shard_map/all_to_all | solution.py:30
  272.9 9.8 %all-to-all-done.17 = bf16[4,64,1024]{2,1,0:T(8,128)(2,1)S(1)} async-done(((bf16[4,64,1024]{2,1,0:T(8,128)(2,1)}), bf16[4,64,1024]{2,1,0:T(8,128)(2,1)S(1)}, u32[]{:S(2)}, u32[]{:S(2)}) %all-to-all-start.17) | async-done | bytes 524320 | tf_op jit(solution)/shard_map/all_to_all | solution.py:30
  283.8 3.4 %all-to-all-start.18 = ((bf16[4,3,64,128]{3,2,1,0:T(8,128)(2,1)}), bf16[4,3,64,128]{3,2,1,0:T(8,128)(2,1)S(1)}, u32[]{:S(2)}, u32[]{:S(2)}) async-start(bf16[4,3,64,128]{3,2,1,0:T(8,128)(2,1)} %broadcast_in_dim.31), calls=%async_computation.18 | async-start | bytes 393216 | tf_op jit(solution)/shard_map/all_to_all | solution.py:30
  288.5 5.0 %all-to-all-done.18 = bf16[4,3,64,128]{3,2,1,0:T(8,128)(2,1)S(1)} async-done(((bf16[4,3,64,128]{3,2,1,0:T(8,128)(2,1)}), bf16[4,3,64,128]{3,2,1,0:T(8,128)(2,1)S(1)}, u32[]{:S(2)}, u32[]{:S(2)}) %all-to-all-start.18) | async-done | bytes 196640 | tf_op jit(solution)/shard_map/all_to_all | solution.py:30
  294.2 4.8 %all-to-all-start.19 = ((bf16[4,3,64,128]{3,2,1,0:T(8,128)(2,1)}), bf16[4,3,64,128]{3,2,1,0:T(8,128)(2,1)S(1)}, u32[]{:S(2)}, u32[]{:S(2)}) async-start(bf16[4,3,64,128]{3,2,1,0:T(8,128)(2,1)} %broadcast_in_dim.32), calls=%async_computation.19 | async-start | bytes 393216 | tf_op jit(solution)/shard_map/all_to_all | solution.py:30
  300.4 3.5 %all-to-all-done.19 = bf16[4,3,64,128]{3,2,1,0:T(8,128)(2,1)S(1)} async-done(((bf16[4,3,64,128]{3,2,1,0:T(8,128)(2,1)}), bf16[4,3,64,128]{3,2,1,0:T(8,128)(2,1)S(1)}, u32[]{:S(2)}, u32[]{:S(2)}) %all-to-all-start.19) | async-done | bytes 196640 | tf_op jit(solution)/shard_map/all_to_all | solution.py:30
  304.8 8.4 %all_to_all.106 = bf16[4,64,256]{2,1,0:T(8,128)(2,1)S(1)} all-to-all(bf16[4,64,256]{2,1,0:T(8,128)(2,1)S(1)} %bitcast.299), channel_id=1, replica_groups={{0,1,2,3},{4,5,6,7},{8,9,10,11},{12,13,14,15},{16,17,18,19},{20,21,22,2..., dimensions={0} | all-to-all | bytes 262144 | tf_op jit(solution)/shard_map/all_to_all | solution.py:30
  (182 shorter events, 41.7 us)
Async XLA Ops:
  1.4 6.7 %copy-start = (bf16[6,256,128]{2,1,0:T(8,128)(2,1)S(1)}, bf16[6,256,128]{2,1,0:T(8,128)(2,1)}, u32[]{:S(2)}) copy-start(bf16[6,256,128]{2,1,0:T(8,128)(2,1)} %param.11) | copy-start | bytes 1179652
  2.5 18.1 %all-to-all-start.7 = ((bf16[4,48,256]{2,1,0:T(8,128)(2,1)}), bf16[4,48,256]{2,1,0:T(8,128)(2,1)S(1)}, u32[]{:S(2)}, u32[]{:S(2)}) async-start(bf16[4,48,256]{2,1,0:T(8,128)(2,1)} %pad_maximum_fusion.3), calls=%async_computation.7 | async-start | bytes 196608 | tf_op jit(solution)/shard_map/all_to_all | solution.py:30
  8.1 6.9 %copy-start.1 = (bf16[6,256,128]{2,1,0:T(8,128)(2,1)S(1)}, bf16[6,256,128]{2,1,0:T(8,128)(2,1)}, u32[]{:S(2)}) copy-start(bf16[6,256,128]{2,1,0:T(8,128)(2,1)} %param.13) | copy-start | bytes 1179652
  12.5 7.5 %copy-start.7 = (f32[4,64,256]{2,1,0:T(8,128)S(1)}, f32[4,64,256]{2,1,0:T(8,128)}, u32[]{:S(2)}) copy-start(f32[4,64,256]{2,1,0:T(8,128)} %param.9) | copy-start | bytes 786436
  20.7 9.3 %all-to-all-start = ((bf16[4,64,256]{2,1,0:T(8,128)(2,1)}), bf16[4,64,256]{2,1,0:T(8,128)(2,1)S(1)}, u32[]{:S(2)}, u32[]{:S(2)}) async-start(bf16[4,64,256]{2,1,0:T(8,128)(2,1)} %convert_element_type.295), calls=%async_computation | async-start | bytes 262144 | tf_op jit(solution)/shard_map/all_to_all | solution.py:30
  30.0 11.5 %all-to-all-start.2 = ((bf16[4,256,256]{2,1,0:T(8,128)(2,1)}), bf16[4,256,256]{2,1,0:T(8,128)(2,1)S(1)}, u32[]{:S(2)}, u32[]{:S(2)}) async-start(bf16[4,256,256]{2,1,0:T(8,128)(2,1)} %param.16), calls=%async_computation.2 | async-start | bytes 1048576 | tf_op jit(solution)/shard_map/all_to_all | solution.py:30
  41.5 11.5 %all-to-all-start.9 = ((bf16[4,256,256]{2,1,0:T(8,128)(2,1)}), bf16[4,256,256]{2,1,0:T(8,128)(2,1)S(1)}, u32[]{:S(2)}, u32[]{:S(2)}) async-start(bf16[4,256,256]{2,1,0:T(8,128)(2,1)} %param.17), calls=%async_computation.9 | async-start | bytes 1048576 | tf_op jit(solution)/shard_map/all_to_all | solution.py:30
  46.4 1.3 collective-permute-start.4
  53.0 56.6 %copy-start.3 = (bf16[4,256,256]{2,1,0:T(8,128)(2,1)}, bf16[4,256,256]{2,1,0:T(8,128)(2,1)S(1)}, u32[]{:S(2)}) copy-start(bf16[4,256,256]{2,1,0:T(8,128)(2,1)S(1)} %all-to-all-done.9) | copy-start | bytes 1572868
  53.9 17.4 %all-to-all-start.8 = ((bf16[4,4,48,256]{3,2,1,0:T(8,128)(2,1)}), bf16[4,4,48,256]{3,2,1,0:T(8,128)(2,1)S(1)}, u32[]{:S(2)}, u32[]{:S(2)}) async-start(bf16[4,4,48,256]{3,2,1,0:T(8,128)(2,1)} %broadcast_in_dim.25), calls=%async_computation.8 | async-start | bytes 786432 | tf_op jit(solution)/shard_map/all_to_all | solution.py:30
  64.5 14.2 %collective-permute-start.2 = (bf16[1024,256]{1,0:T(8,128)(2,1)S(1)}, bf16[1024,256]{1,0:T(8,128)(2,1)}, u32[]{:S(2)}, u32[]{:S(2)}) collective-permute-start(bf16[1024,256]{1,0:T(8,128)(2,1)S(1)} %bitcast.294), channel_id=1, source_target_pairs={{0,32},{1,33},{2,34},{3,35},{4,36},{5,37},{6,38},{7,39},{8,40},{9,... | collective-permute-start | bytes 1572872 | tf_op jit(solution)/shard_map/ppermute | solution.py:26
  71.2 12.8 %all-to-all-start.4 = ((bf16[4,3,256,128]{3,2,1,0:T(8,128)(2,1)}), bf16[4,3,256,128]{3,2,1,0:T(8,128)(2,1)S(1)}, u32[]{:S(2)}, u32[]{:S(2)}) async-start(bf16[4,3,256,128]{3,2,1,0:T(8,128)(2,1)} %bitcast.8), calls=%async_computation.4 | async-start | bytes 1572864 | tf_op jit(solution)/shard_map/all_to_all | solution.py:30
  76.6 12.4 %collective-permute-start.6 = (bf16[1024,256]{1,0:T(8,128)(2,1)S(1)}, bf16[1024,256]{1,0:T(8,128)(2,1)}, u32[]{:S(2)}, u32[]{:S(2)}) collective-permute-start(bf16[1024,256]{1,0:T(8,128)(2,1)S(1)} %bitcast.290), channel_id=1, source_target_pairs={{0,32},{1,33},{2,34},{3,35},{4,36},{5,37},{6,38},{7,39},{8,40},{9,... | collective-permute-start | bytes 1572872 | tf_op jit(solution)/shard_map/ppermute | solution.py:26
  78.6 11.7 %collective-permute-start.1 = (bf16[1024,256]{1,0:T(8,128)(2,1)S(1)}, bf16[1024,256]{1,0:T(8,128)(2,1)}, u32[]{:S(2)}, u32[]{:S(2)}) collective-permute-start(bf16[1024,256]{1,0:T(8,128)(2,1)S(1)} %bitcast.295), channel_id=1, source_target_pairs={{0,16},{1,17},{2,18},{3,19},{4,20},{5,21},{6,22},{7,23},{8,24},{9,... | collective-permute-start | bytes 1572872 | tf_op jit(solution)/shard_map/ppermute | solution.py:26
  78.7 11.6 %collective-permute-start.3 = (bf16[1024,256]{1,0:T(8,128)(2,1)}, bf16[1024,256]{1,0:T(8,128)(2,1)}, u32[]{:S(2)}, u32[]{:S(2)}) collective-permute-start(bf16[1024,256]{1,0:T(8,128)(2,1)} %collective-permute-done.2), channel_id=1, source_target_pairs={{0,16},{1,17},{2,18},{3,19},{4,20},{5,21},{6,22},{7,23},{8,24},{9,... | collective-permute-start | bytes 1572872 | tf_op jit(solution)/shard_map/ppermute | solution.py:26
  84.0 13.0 %all-to-all-start.13 = ((bf16[4,3,256,128]{3,2,1,0:T(8,128)(2,1)}), bf16[4,3,256,128]{3,2,1,0:T(8,128)(2,1)S(1)}, u32[]{:S(2)}, u32[]{:S(2)}) async-start(bf16[4,3,256,128]{3,2,1,0:T(8,128)(2,1)} %bitcast.51), calls=%async_computation.13 | async-start | bytes 1572864 | tf_op jit(solution)/shard_map/all_to_all | solution.py:30
  89.0 20.7 %collective-permute-start.5 = (bf16[1024,256]{1,0:T(8,128)(2,1)S(1)}, bf16[1024,256]{1,0:T(8,128)(2,1)}, u32[]{:S(2)}, u32[]{:S(2)}) collective-permute-start(bf16[1024,256]{1,0:T(8,128)(2,1)S(1)} %bitcast.291), channel_id=1, source_target_pairs={{0,16},{1,17},{2,18},{3,19},{4,20},{5,21},{6,22},{7,23},{8,24},{9,... | collective-permute-start | bytes 1572872 | tf_op jit(solution)/shard_map/ppermute | solution.py:26
  89.1 20.6 %collective-permute-start.7 = (bf16[1024,256]{1,0:T(8,128)(2,1)}, bf16[1024,256]{1,0:T(8,128)(2,1)}, u32[]{:S(2)}, u32[]{:S(2)}) collective-permute-start(bf16[1024,256]{1,0:T(8,128)(2,1)} %collective-permute-done.6), channel_id=1, source_target_pairs={{0,16},{1,17},{2,18},{3,19},{4,20},{5,21},{6,22},{7,23},{8,24},{9,... | collective-permute-start | bytes 1572872 | tf_op jit(solution)/shard_map/ppermute | solution.py:26
  89.6 3.5 %collective-permute-start = (bf16[4,64,256]{2,1,0:T(8,128)(2,1)S(1)}, bf16[4,64,256]{2,1,0:T(8,128)(2,1)S(1)}, u32[]{:S(2)}, u32[]{:S(2)}) collective-permute-start(bf16[4,64,256]{2,1,0:T(8,128)(2,1)S(1)} %maximum_select_fusion.1), channel_id=1, source_target_pairs={{0,0},{1,1},{2,2},{3,3},{4,64},{5,65},{6,66},{7,67},{8,128},{9,129... | collective-permute-start | bytes 393224 | tf_op jit(solution)/shard_map/ppermute | solution.py:26
  97.9 20.9 %all-to-all-start.1 = ((bf16[4,4,64,256]{3,2,1,0:T(8,128)(2,1)}), bf16[4,4,64,256]{3,2,1,0:T(8,128)(2,1)S(1)}, u32[]{:S(2)}, u32[]{:S(2)}) async-start(bf16[4,4,64,256]{3,2,1,0:T(8,128)(2,1)} %broadcast_in_dim.22), calls=%async_computation.1 | async-start | bytes 1048576 | tf_op jit(solution)/shard_map/all_to_all | solution.py:30
  109.7 2.2 copy-start.10
  118.7 19.9 %all-to-all-start.10 = ((bf16[4,48,1024]{2,1,0:T(8,128)(2,1)}), bf16[4,48,1024]{2,1,0:T(8,128)(2,1)S(1)}, u32[]{:S(2)}, u32[]{:S(2)}) async-start(bf16[4,48,1024]{2,1,0:T(8,128)(2,1)} %pad_maximum_fusion.2), calls=%async_computation.10 | async-start | bytes 786432 | tf_op jit(solution)/shard_map/all_to_all | solution.py:30
  138.6 16.0 %all-to-all-start.3 = ((bf16[4,64,1024]{2,1,0:T(8,128)(2,1)}), bf16[4,64,1024]{2,1,0:T(8,128)(2,1)S(1)}, u32[]{:S(2)}, u32[]{:S(2)}) async-start(bf16[4,64,1024]{2,1,0:T(8,128)(2,1)} %fusion), calls=%async_computation.3 | async-start | bytes 1048576 | tf_op jit(solution)/shard_map/all_to_all | solution.py:30
  155.4 15.3 %all-to-all-start.12 = ((bf16[8,24,1024]{2,1,0:T(8,128)(2,1)}), bf16[8,24,1024]{2,1,0:T(8,128)(2,1)S(1)}, u32[]{:S(2)}, u32[]{:S(2)}) async-start(bf16[8,24,1024]{2,1,0:T(8,128)(2,1)} %broadcast_in_dim.27), calls=%async_computation.12 | async-start | bytes 786432 | tf_op jit(solution)/shard_map/all_to_all | solution.py:30
  171.5 15.3 %all-to-all-start.11 = ((bf16[8,24,1024]{2,1,0:T(8,128)(2,1)}), bf16[8,24,1024]{2,1,0:T(8,128)(2,1)S(1)}, u32[]{:S(2)}, u32[]{:S(2)}) async-start(bf16[8,24,1024]{2,1,0:T(8,128)(2,1)} %broadcast_in_dim.26), calls=%async_computation.11 | async-start | bytes 786432 | tf_op jit(solution)/shard_map/all_to_all | solution.py:30
  175.8 17.4 %collective-permute-start.9 = (bf16[8,24,1024]{2,1,0:T(8,128)(2,1)S(1)}, bf16[8,24,1024]{2,1,0:T(8,128)(2,1)}, u32[]{:S(2)}, u32[]{:S(2)}) collective-permute-start(bf16[8,24,1024]{2,1,0:T(8,128)(2,1)S(1)} %all-to-all-done.12), channel_id=1, source_target_pairs={{0,16},{1,17},{2,18},{3,19},{4,20},{5,21},{6,22},{7,23},{8,24},{9,... | collective-permute-start | bytes 1179656 | tf_op jit(solution)/shard_map/ppermute | solution.py:26
  187.5 12.2 %all-to-all-start.5 = ((bf16[4,3,64,128]{3,2,1,0:T(8,128)(2,1)}), bf16[4,3,64,128]{3,2,1,0:T(8,128)(2,1)}, u32[]{:S(2)}, u32[]{:S(2)}) async-start(bf16[4,3,64,128]{3,2,1,0:T(8,128)(2,1)} %broadcast_in_dim.23), calls=%async_computation.5 | async-start | bytes 393216 | tf_op jit(solution)/shard_map/all_to_all | solution.py:30
  193.2 1.7 collective-permute-start.8
  195.0 1.0 copy-start.2
  195.0 1.2 copy-start.8
  195.1 1.3 copy-start.9
  196.9 7.1 %copy-start.11 = (s32[6]{0:T(128)S(1)}, s32[6]{0:T(128)}, u32[]{:S(2)}) copy-start(s32[6]{0:T(128)} %param.14) | copy-start | bytes 76
  200.6 11.8 %all-to-all-start.14 = ((bf16[4,2,2,128,128]{4,3,2,1,0:T(8,128)(2,1)}), bf16[4,2,2,128,128]{4,3,2,1,0:T(8,128)(2,1)S(1)}, u32[]{:S(2)}, u32[]{:S(2)}) async-start(bf16[4,2,2,128,128]{4,3,2,1,0:T(8,128)(2,1)} %broadcast_in_dim.28), calls=%async_computation.14 | async-start | bytes 1048576 | tf_op jit(solution)/shard_map/all_to_all | solution.py:30
  213.1 9.7 %all-to-all-start.6 = ((bf16[4,3,64,128]{3,2,1,0:T(8,128)(2,1)}), bf16[4,3,64,128]{3,2,1,0:T(8,128)(2,1)S(1)}, u32[]{:S(2)}, u32[]{:S(2)}) async-start(bf16[4,3,64,128]{3,2,1,0:T(8,128)(2,1)} %broadcast_in_dim.24), calls=%async_computation.6 | async-start | bytes 393216 | tf_op jit(solution)/shard_map/all_to_all | solution.py:30
  222.8 7.0 %copy-start.6 = (bf16[4,3,64,128]{3,2,1,0:T(8,128)(2,1)}, bf16[4,3,64,128]{3,2,1,0:T(8,128)(2,1)S(1)}, u32[]{:S(2)}) copy-start(bf16[4,3,64,128]{3,2,1,0:T(8,128)(2,1)S(1)} %all-to-all-done.6) | copy-start | bytes 589828
  223.7 12.3 %all-to-all-start.15 = ((bf16[4,2,2,128,128]{4,3,2,1,0:T(8,128)(2,1)}), bf16[4,2,2,128,128]{4,3,2,1,0:T(8,128)(2,1)}, u32[]{:S(2)}, u32[]{:S(2)}) async-start(bf16[4,2,2,128,128]{4,3,2,1,0:T(8,128)(2,1)} %broadcast_in_dim.29), calls=%async_computation.15 | async-start | bytes 1048576 | tf_op jit(solution)/shard_map/all_to_all | solution.py:30
  229.8 8.8 %copy-start.13 = (f32[128]{0:T(128)S(1)}, f32[128]{0:T(128)}, u32[]{:S(2)}) copy-start(f32[128]{0:T(128)} %compare_convert_fusion.9) | copy-start | bytes 1540
  229.8 9.8 %copy-start.14 = (f32[128]{0:T(128)S(1)}, f32[128]{0:T(128)}, u32[]{:S(2)}) copy-start(f32[128]{0:T(128)} %compare_convert_fusion.7) | copy-start | bytes 1540
  241.0 23.4 %copy-start.4 = (bf16[4,256,256]{2,1,0:T(8,128)(2,1)S(1)}, bf16[4,256,256]{2,1,0:T(8,128)(2,1)}, u32[]{:S(2)}) copy-start(bf16[4,256,256]{2,1,0:T(8,128)(2,1)} %copy-done.3) | copy-start | bytes 1572868
  241.0 0.8 collective-permute-start.10
  267.3 3.6 %copy-start.12 = (s32[6]{0:T(128)S(1)}, s32[6]{0:T(128)}, u32[]{:S(2)}) copy-start(s32[6]{0:T(128)} %param.15) | copy-start | bytes 76
  267.3 15.5 %all-to-all-start.17 = ((bf16[4,64,1024]{2,1,0:T(8,128)(2,1)}), bf16[4,64,1024]{2,1,0:T(8,128)(2,1)S(1)}, u32[]{:S(2)}, u32[]{:S(2)}) async-start(bf16[4,64,1024]{2,1,0:T(8,128)(2,1)} %fusion.1), calls=%async_computation.17 | async-start | bytes 1048576 | tf_op jit(solution)/shard_map/all_to_all | solution.py:30
  283.8 9.7 %all-to-all-start.18 = ((bf16[4,3,64,128]{3,2,1,0:T(8,128)(2,1)}), bf16[4,3,64,128]{3,2,1,0:T(8,128)(2,1)S(1)}, u32[]{:S(2)}, u32[]{:S(2)}) async-start(bf16[4,3,64,128]{3,2,1,0:T(8,128)(2,1)} %broadcast_in_dim.31), calls=%async_computation.18 | async-start | bytes 393216 | tf_op jit(solution)/shard_map/all_to_all | solution.py:30
  294.2 9.7 %all-to-all-start.19 = ((bf16[4,3,64,128]{3,2,1,0:T(8,128)(2,1)}), bf16[4,3,64,128]{3,2,1,0:T(8,128)(2,1)S(1)}, u32[]{:S(2)}, u32[]{:S(2)}) async-start(bf16[4,3,64,128]{3,2,1,0:T(8,128)(2,1)} %broadcast_in_dim.32), calls=%async_computation.19 | async-start | bytes 393216 | tf_op jit(solution)/shard_map/all_to_all | solution.py:30
  300.3 3.6 %copy-start.5 = (bf16[4,2,128,128]{3,2,1,0:T(8,128)(2,1)S(1)}, bf16[4,2,128,128]{3,2,1,0:T(8,128)(2,1)}, u32[]{:S(2)}) copy-start(bf16[4,2,128,128]{3,2,1,0:T(8,128)(2,1)} %get-tuple-element.13) | copy-start | bytes 786436

commit v3 on v0

v3 whole, which is shorter than its diff:
```python
import jax
import jax.numpy as jnp
from jax import lax
from jax.experimental import pallas as pl
from jax.experimental.pallas import tpu as pltpu
from jax.sharding import PartitionSpec as P

RBLK = 32
BF16 = jnp.bfloat16
F32 = jnp.float32
SIDE = 4
X_GROUPS = [[SIDE * y + x for x in range(SIDE)] for y in range(SIDE)]
Y_GROUPS = [[SIDE * y + x for y in range(SIDE)] for x in range(SIDE)]
Q_GROUPS = [[SIDE * q + j for q in range(SIDE)] for j in range(SIDE)]
Z_GROUPS = [[2 * z + core for z in range(8)] for core in range(2)]


def routes(to):
    index = lambda q, j, y, x: (SIDE * q + j) * SIDE * SIDE + SIDE * y + x
    span = range(SIDE)
    return [
        (index(q, j, y, x), index(*to(q, j, y, x)))
        for q in span for j in span for y in span for x in span
    ]


def permuted(value, to):
    return lax.ppermute(value, ("row", "col"), routes(to))


def exchanged(value, axis, groups):
    return lax.all_to_all(value, axis, 0, 0, tiled=True, axis_index_groups=groups)


def over_x(value):
    return exchanged(value, "col", X_GROUPS)


def from_everyone(value, axis, groups):
    return exchanged(
        jnp.broadcast_to(value[None], (len(groups[0]), *value.shape)), axis, groups
    )


def swapped(value):
    return permuted(value, lambda q, j, y, x: (y, j, q, x))


def swap_core(value):
    return permuted(value, lambda q, j, y, x: (q, j ^ 1, y, x))


def swap_pair(value):
    return permuted(value, lambda q, j, y, x: (q, j ^ 2, y, x))


def dot(left, right):
    return jnp.dot(left, right, preferred_element_type=F32)


def dot_t(left, right):
    return lax.dot_general(
        left, right, (((1,), (1,)), ((), ())), preferred_element_type=F32
    )


def pair_of(i, j):
    high, low = max(i, j), min(i, j)
    return high * (high - 1) // 2 + low


def partners(tile):
    return [t for t in range(SIDE) if t != tile]


def kernel_call(body, out_shape, smem=(), flops=0, grid=None, in_specs=None, out_specs=None):
    def run(*args):
        specs = in_specs or [
            pl.BlockSpec(memory_space=pltpu.SMEM if at in smem else pltpu.VMEM)
            for at in range(len(args))
        ]
        outs = jax.tree.leaves(out_shape)
        moved = sum(a.size * a.dtype.itemsize for a in [*args, *outs])
        more = {} if grid is None else {"grid": grid, "out_specs": out_specs}
        return pl.pallas_call(
            body,
            out_shape=out_shape,
            in_specs=specs,
            compiler_params=pltpu.CompilerParams(vmem_limit_bytes=30 * 2**20),
            cost_estimate=pl.CostEstimate(
                flops=flops, bytes_accessed=moved, transcendentals=0
            ),
            **more,
        )(*args)

    return run


def pack_kernel(right_ref, low_ref, up_ref, out_ref):
    n = right_ref.shape[1]
    rank_cols = low_ref.shape[2]
    share = rank_cols // lax.axis_size("row")
    row = lax.axis_index("row")
    at = lax.broadcasted_iota(jnp.int32, (share, rank_cols), 1)
    want = lax.broadcasted_iota(jnp.int32, (share, rank_cols), 0) + row * share
    pick = (at == want).astype(F32).astype(BF16)
    for tile in range(SIDE):
        out_ref[tile, :n] = right_ref[tile].astype(BF16)
        pieces = [
            dot_t(pick, (low_ref if t < tile else up_ref)[pair_of(tile, t)])
            for t in partners(tile)
        ]
        out_ref[tile, n:] = jnp.concatenate(pieces, axis=0).astype(BF16)


def turn_kernel(low_ref, up_ref, out_ref):
    rank_cols = low_ref.shape[2]
    one = lax.broadcasted_iota(jnp.int32, (rank_cols, rank_cols), 0)
    two = lax.broadcasted_iota(jnp.int32, (rank_cols, rank_cols), 1)
    eye = (one == two).astype(F32).astype(BF16)
    for tile in range(SIDE):
        for slot, t in enumerate(partners(tile)):
            factor = (up_ref if t < tile else low_ref)[pair_of(tile, t)]
            out_ref[tile, slot * rank_cols : (slot + 1) * rank_cols] = dot_t(
                eye, factor
            ).astype(BF16)


def products_kernel(n, x_ref, *refs):
    lower, upper, out_ref = refs[:SIDE], refs[SIDE : 2 * SIDE], refs[-1]
    flip = lax.rem(lax.axis_index("row"), SIDE)
    rows = x_ref.shape[2]
    for span in range(SIDE):
        blocks = [x_ref[span, at ^ flip] for at in range(SIDE)]
        value = sum(dot_t(blocks[at], lower[at][...]) for at in range(SIDE))
        if rows > n:
            tile = lax.rem(lax.axis_index("col"), SIDE)
            other = sum(dot_t(blocks[at][n:], upper[at][...]) for at in range(SIDE))
            share = (rows - n) // (SIDE - 1)
            slot = lax.broadcasted_iota(jnp.int32, other.shape, 0) // share
            out_ref[span, :n] = value[:n].astype(BF16)
            out_ref[span, n:] = jnp.where(slot < tile, value[n:], other).astype(BF16)
        else:
            out_ref[span] = value.astype(BF16)


def products(n, gathered, *inverses):
    spans, blocks, rows, width = gathered.shape
    total = inverses[0].shape[0]
    return kernel_call(
        lambda *refs: products_kernel(n, *refs),
        jax.ShapeDtypeStruct((spans, rows, total), BF16),
        flops=2 * spans * blocks * rows * width * total,
        grid=(total // 256,),
        in_specs=[pl.BlockSpec(gathered.shape, lambda a: (0, 0, 0, 0))]
        + [pl.BlockSpec((256, width), lambda a: (a, 0)) for _ in inverses],
        out_specs=pl.BlockSpec((spans, rows, 256), lambda a: (0, 0, a)),
    )(gathered, *inverses)


def total_kernel(n, part_ref, dense_ref, extra_ref):
    whole = part_ref[0].astype(F32)
    for at in range(1, SIDE):
        whole = whole + part_ref[at].astype(F32)
    dense_ref[...] = whole[:n]
    extra = whole[n:].astype(BF16)
    for at in range(extra_ref.shape[0]):
        extra_ref[at] = extra


def project(dense, turned_ref, slot, rank_cols):
    width = turned_ref.shape[2]
    return sum(
        dot_t(
            dense[:, at * width : (at + 1) * width],
            turned_ref[at, slot * rank_cols : (slot + 1) * rank_cols],
        )
        for at in range(SIDE)
    )


def couple_kernel(dense_ref, mine_ref, other_ref, turned_ref, extra_ref, send_ref, later_ref):
    n = dense_ref.shape[0]
    slots = SIDE - 1
    rank_cols = turned_ref.shape[1] // slots
    width = turned_ref.shape[2]
    share = mine_ref.shape[1] // slots
    even = lax.rem(lax.axis_index("row"), 2) == 0
    tile = lax.rem(lax.axis_index("col"), SIDE)
    for z in range(mine_ref.shape[0]):
        mine, other = mine_ref[z].astype(F32), other_ref[z].astype(F32)
        first = jnp.where(even, mine, other)
        second = jnp.where(even, other, mine)
        for slot in range(slots):
            at = slice(slot * share, (slot + 1) * share)
            start = slot * rank_cols + z * 2 * share
            extra_ref[start : start + 2 * share] = jnp.concatenate(
                [first[at], second[at]], axis=0
            ).astype(BF16)
    dense = dense_ref[...].astype(BF16)
    pieces = [project(dense, turned_ref, slot, rank_cols) for slot in range(slots)]

    def coupling(left, right):
        left = pl.multiple_of(left * rank_cols, rank_cols)
        right = pl.multiple_of(right * rank_cols, rank_cols)
        return sum(
            dot_t(
                extra_ref[pl.ds(left, rank_cols), at * width : (at + 1) * width],
                turned_ref[at, pl.ds(right, rank_cols), :],
            )
            for at in range(SIDE)
        )

    one = tile == 1
    pick = lambda a, b: jnp.where(one, a, b)
    pieces += [coupling(0, pick(1, 2)), coupling(pick(0, 1), 2)]
    send = jnp.concatenate(pieces, axis=0).astype(BF16)
    for at in range(SIDE):
        send_ref[at] = send
    later_ref[:rank_cols] = coupling(pick(1, 2), 0).astype(BF16)
    later_ref[rank_cols:] = coupling(2, pick(0, 1)).astype(BF16)


def last_project_kernel(part_ref, turned_ref, later_ref, dense_ref, send_ref):
    slots = SIDE - 1
    rank_cols = turned_ref.shape[1] // slots
    whole = part_ref[0].astype(F32)
    for at in range(1, SIDE):
        whole = whole + part_ref[at].astype(F32)
    dense_ref[...] = whole
    dense = whole.astype(BF16)
    pieces = [project(dense, turned_ref, slot, rank_cols) for slot in range(slots)]
    send = jnp.concatenate(pieces, axis=0).astype(BF16)
    n = send.shape[0]
    for at in range(SIDE):
        send_ref[at, :n] = send
        send_ref[at, n:] = later_ref[...]


def add_kernel(part_ref, out_ref):
    whole = part_ref[0].astype(F32)
    for at in range(1, SIDE):
        whole = whole + part_ref[at].astype(F32)
    whole = whole.astype(BF16)
    for at in range(SIDE):
        out_ref[at] = whole


def finish_kernel(is_lower, sums_ref, dense_ref, extra_ref, ranks_ref, out_ref):
    n = dense_ref.shape[0]
    rank_cols = extra_ref.shape[0] // (SIDE - 1)
    width = out_ref.shape[2]
    tile = lax.rem(lax.axis_index("col"), SIDE)
    columns = lax.broadcasted_iota(jnp.int32, (n, rank_cols), 1)
    at_coupling = (SIDE - 1) * n
    coupling = {}
    order = list(range(SIDE)) if is_lower else list(range(SIDE))[::-1]
    first, second, third, last = order
    for which, key in enumerate(((third, second, first), (last, second, first))):
        coupling[key] = (second, which)
    for which, key in enumerate(((last, third, first), (last, third, second))):
        coupling[key] = (third, which)
    if not is_lower:
        coupling = {
            (0, 2, 3): (2, 0), (1, 2, 3): (2, 1), (0, 1, 2): (1, 0), (0, 1, 3): (1, 1)
        }
    masked = {}
    for at, source in enumerate(order):
        for target in order[at + 1 :]:
            slot = partners(source).index(target)
            value = sums_ref[source, slot * n : (slot + 1) * n].astype(F32)
            for before in order[:at]:
                held, which = coupling[target, source, before]
                start = at_coupling + which * rank_cols
                value = value - dot(
                    masked[source, before], sums_ref[held, start : start + rank_cols]
                )
            keep = columns < RBLK * ranks_ref[pair_of(source, target)]
            masked[target, source] = jnp.where(keep, value, 0.0).astype(BF16)
    result = dense_ref[...]
    nothing = jnp.zeros((n, rank_cols), BF16)
    for slot in range(SIDE - 1):
        mine = nothing
        for target in range(SIDE):
            source = partners(target)[slot]
            if (target, source) in masked:
                mine = jnp.where(tile == target, masked[target, source], mine)
        result = result - dot(
            mine, extra_ref[slot * rank_cols : (slot + 1) * rank_cols]
        )
    result = result.astype(BF16)
    for at in range(SIDE):
        out_ref[at] = result[:, at * width : (at + 1) * width]


def quad_of(value):
    far = swap_pair(value)
    return [value, swap_core(value), far, swap_core(far)]


def shards(
    right_sides, low_left, low_right, up_left, up_right, low_ranks, up_ranks, inv_lower, inv_upper
):
    n, width = right_sides.shape[1:]
    rank_cols = low_left.shape[2]
    slots = SIDE - 1
    share = rank_cols // lax.axis_size("row")
    total = SIDE * width
    shape = jax.ShapeDtypeStruct

    lower = quad_of(over_x(inv_lower).reshape(total, width))
    rows = kernel_call(
        pack_kernel, shape((SIDE, n + slots * share, width), BF16)
    )(right_sides, low_left, up_left)
    rows = swapped(over_x(rows))
    upper = quad_of(over_x(inv_upper).reshape(total, width))
    gathered = from_everyone(rows, "col", Y_GROUPS).reshape(SIDE, SIDE, -1, width)
    turned = over_x(
        kernel_call(turn_kernel, shape((SIDE, slots * rank_cols, width), BF16))(
            low_right, up_right
        )
    )
    partial = products(n, gathered, *lower, *upper)
    received = exchanged(partial, "row", Q_GROUPS)
    dense, extra = kernel_call(
        lambda *refs: total_kernel(n, *refs),
        (shape((n, total), F32), shape((8, slots * share, total), BF16)),
    )(received)
    mine = exchanged(extra, "row", Z_GROUPS)
    other = swap_core(mine)
    packed = slots * n + 2 * rank_cols
    extra, send, later = kernel_call(
        couple_kernel,
        (
            shape((slots * rank_cols, total), BF16),
            shape((SIDE, packed, rank_cols), BF16),
            shape((2 * rank_cols, rank_cols), BF16),
        ),
    )(dense, mine, other, turned)

    def finished(is_lower, send, dense, ranks):
        sums = kernel_call(add_kernel, shape((SIDE, packed, rank_cols), BF16))(
            exchanged(send, "col", Y_GROUPS)
        )
        return kernel_call(
            lambda *refs: finish_kernel(is_lower, *refs),
            shape((SIDE, n, width), BF16),
            smem=(3,),
        )(over_x(sums), dense, extra, ranks)

    rows = finished(True, send, dense, low_ranks)
    gathered = from_everyone(swapped(rows), "col", Y_GROUPS)
    gathered = gathered.reshape(SIDE, SIDE, n, width)
    received = exchanged(products(n, gathered, *upper), "row", Q_GROUPS)
    dense, send = kernel_call(
        last_project_kernel,
        (shape((n, total), F32), shape((SIDE, packed, rank_cols), BF16)),
    )(received, turned, later)
    rows = finished(False, send, dense, up_ranks)
    return over_x(rows).astype(F32)


def solution(mesh):
    in_specs = (
        P(None, "row", "col"),
        P(None, "col", None),
        P(None, "col", None),
        P(None, "col", None),
        P(None, "col", None),
        P(),
        P(),
        P(None, "col", "row"),
        P(None, "col", "row"),
    )
    out_specs = P(None, "row", "col")
    return jax.shard_map(shards, mesh=mesh, in_specs=in_specs, out_specs=out_specs, check_vma=False)
```

time: 359 us -> 229 us (0.64)
  waiting for transfers between devices: 182 us -> 31.6 us
  blocking collectives: 41.6 us -> 132 us
  starting transfers between devices: 73 us -> 43.3 us
  matrix products: 20.8 us -> 0 us
  local copies, waits for them, and re-layouts: 21.9 us -> 3.93 us
  Pallas kernels: 0 us -> 16.3 us
  between operations: 14.4 us -> 0.16 us
    all_to_all x3 -> x10, blocking collectives: 41.6 us -> 132 us  [exchanged(): lax.all_to_all(value, axis, 0, 0, tiled=True, axis_index_groups=groups)]
    all_gather x8 -> x0, waiting for transfers between devices: 76.4 us -> none  [the longest x4 38.2 us: shards(): lax.all_gather(inv_lower[section], 'row', axis=1, tiled=True)]
    all_to_all x11 -> x4, waiting for transfers between devices: 102 us -> 31.6 us  [exchanged(): lax.all_to_all(value, axis, 0, 0, tiled=True, axis_index_groups=groups)]
    all_to_all x11 -> x4, starting transfers between devices: 72.7 us -> 36.6 us  [exchanged(): lax.all_to_all(value, axis, 0, 0, tiled=True, axis_index_groups=groups)]
    dot_general x20 -> x0, matrix products: 20.8 us -> none  [the longest x8 18.9 us: times_inverse(): lax.dot_general(block, inverse, (((1,), (1,)), ((), ())), preferred_eleme...]
    pallas_call x0 -> x11, Pallas kernels: none -> 16.3 us  [run(): pl.pallas_call(body, out_shape=out_shape, in_specs=specs, compiler_params...]
    broadcast_in_dim x19 -> x2, local copies, waits for them, and re-layouts: 9.98 us -> 0.95 us  [from_everyone(): jnp.broadcast_to(value[None], (len(groups[0]), *value.shape))]
    gather x13 -> x0, local copies, waits for them, and re-layouts: 7.74 us -> none  [the longest x5 3.11 us: rank_mask(): ranks[pair_index][:, None]]
  transfers between devices with their start and end apart: 19 -> 13, of which waited for: 19 -> 4; matrix products, arithmetic and copies ran while one was open for 11% -> 0% of each run, Pallas kernels for 0% -> 1%
where the time goes in v3:
time: 229 us; the launch traced here: 228 us
  blocking collectives  132 us (58%)
  starting transfers between devices  43.3 us (19%)
  waiting for transfers between devices  31.6 us (14%)
  Pallas kernels  16.3 us (7%)
  local copies, waits for them, and re-layouts  3.93 us (2%)
    all_to_all x10, blocking collectives, exchanged(): lax.all_to_all(value, axis, 0, 0, tiled=True, axis_index_groups=groups)  132 us
    all_to_all x4, starting transfers between devices, exchanged(): lax.all_to_all(value, axis, 0, 0, tiled=True, axis_index_groups=groups)  36.6 us
    all_to_all x4, waiting for transfers between devices, exchanged(): lax.all_to_all(value, axis, 0, 0, tiled=True, axis_index_groups=groups)  31.6 us
    pallas_call x11, Pallas kernels, run(): pl.pallas_call(body, out_shape=out_shape, in_specs=specs, compiler_params...  16.3 us
    ppermute x9, starting transfers between devices, permuted(): return lax.ppermute(value, ('row', 'col'), routes(to))  6.67 us
  transfers between devices with their start and end apart: 13, of which 4 were waited for; matrix products, arithmetic and copies ran while one was open for 0% of the time, Pallas kernels for 1%

profile of v3, /device:TPU:2, one launch (start us, length us, event | category | flops | bytes accessed | tf_op | source)
XLA Modules:
  0.0 228.4 jit_solution(15151108761505365163)
XLA Ops:
  0.0 12.8 %all_to_all.70 = bf16[4,256,256]{2,1,0:T(8,128)(2,1)S(1)} all-to-all(bf16[4,256,256]{2,1,0:T(8,128)(2,1)} %param.16), channel_id=1, replica_groups={{0,1,2,3},{4,5,6,7},{8,9,10,11},{12,13,14,15},{16,17,18,19},{20,21,22,2..., dimensions={0} | all-to-all | bytes 1048576 | tf_op jit(solution)/shard_map/all_to_all | solution.py:32
  12.8 5.0 %all-to-all-start.3 = ((bf16[4,256,256]{2,1,0:T(8,128)(2,1)}), bf16[4,256,256]{2,1,0:T(8,128)(2,1)S(1)}, u32[]{:S(2)}, u32[]{:S(2)}) async-start(bf16[4,256,256]{2,1,0:T(8,128)(2,1)} %param.17), calls=%async_computation.3 | async-start | bytes 1048576 | tf_op jit(solution)/shard_map/all_to_all | solution.py:32
  17.9 1.9 collective-permute-start.2
  19.8 4.7 %all-to-all-done.3 = bf16[4,256,256]{2,1,0:T(8,128)(2,1)S(1)} async-done(((bf16[4,256,256]{2,1,0:T(8,128)(2,1)}), bf16[4,256,256]{2,1,0:T(8,128)(2,1)S(1)}, u32[]{:S(2)}, u32[]{:S(2)}) %all-to-all-start.3) | async-done | bytes 524320 | tf_op jit(solution)/shard_map/all_to_all | solution.py:32
  24.5 2.4 %collective-permute-start.5 = (bf16[1024,256]{1,0:T(8,128)(2,1)S(1)}, bf16[1024,256]{1,0:T(8,128)(2,1)S(1)}, u32[]{:S(2)}, u32[]{:S(2)}) collective-permute-start(bf16[1024,256]{1,0:T(8,128)(2,1)S(1)} %bitcast.2), channel_id=1, source_target_pairs={{0,32},{1,33},{2,34},{3,35},{4,36},{5,37},{6,38},{7,39},{8,40},{9,... | collective-permute-start | bytes 1572872 | tf_op jit(solution)/shard_map/ppermute | solution.py:28
  26.9 0.3 shard_map.91
  27.2 8.6 %all_to_all.71 = bf16[4,88,256]{2,1,0:T(8,128)(2,1)S(1)} all-to-all(bf16[4,88,256]{2,1,0:T(8,128)(2,1)S(1)} %shard_map.91), channel_id=1, replica_groups={{0,1,2,3},{4,5,6,7},{8,9,10,11},{12,13,14,15},{16,17,18,19},{20,21,22,2..., dimensions={0} | all-to-all | bytes 360448 | tf_op jit(solution)/shard_map/all_to_all | solution.py:32
  35.8 0.7 collective-permute-start
  36.5 0.0 collective-permute-done
  36.5 0.9 broadcast_in_dim.4
  37.4 21.8 %all-to-all-start.1 = ((bf16[4,4,88,256]{3,2,1,0:T(8,128)(2,1)}), bf16[4,4,88,256]{3,2,1,0:T(8,128)(2,1)S(1)}, u32[]{:S(2)}, u32[]{:S(2)}) async-start(bf16[4,4,88,256]{3,2,1,0:T(8,128)(2,1)} %broadcast_in_dim.4), calls=%async_computation.1 | async-start | bytes 1441792 | tf_op jit(solution)/shard_map/all_to_all | solution.py:32
  59.2 0.5 collective-permute-start.4
  59.7 0.0 collective-permute-done.2.refs_3_
  59.7 0.0 collective-permute-start.3
  59.7 0.5 collective-permute-start.6
  60.2 8.1 %all-to-all-done.1.refs_0_ = bf16[4,4,88,256]{3,2,1,0:T(8,128)(2,1)S(1)} async-done(((bf16[4,4,88,256]{3,2,1,0:T(8,128)(2,1)}), bf16[4,4,88,256]{3,2,1,0:T(8,128)(2,1)S(1)}, u32[]{:S(2)}, u32[]{:S(2)}) %all-to-all-start.1) | async-done | bytes 720928 | tf_op jit(solution)/shard_map/all_to_all | solution.py:32
  68.3 0.0 collective-permute-done.1.refs_2_
  68.3 0.0 collective-permute-done.4.refs_6_.refs_2_
  68.3 6.6 %shard_map.92 = bf16[4,88,1024]{2,1,0:T(8,128)(2,1)S(1)} custom-call(bf16[4,4,88,256]{3,2,1,0:T(8,128)(2,1)S(1)} %all-to-all-done.1.refs_0_, bf16[1024,256]{1,0:T(8,128)(2,1)S(1)} %bitcast.8, bf16[1024,256]{1,0:T(8,128)(2,1)} %collective-permute-done.1.refs_2_, bf16[1024,256]{1,0:T(8,128)(2,1)} %collective-permute-done.2.refs_3_, ...), custom_call_target="tpu_custom_call" | custom-call | flops 738197504 | bytes 5636096 | tf_op jit(solution)/shard_map/pallas_call | solution.py:85
  75.0 20.9 %all_to_all.72.refs_0_ = bf16[4,88,1024]{2,1,0:T(8,128)(2,1)S(1)} all-to-all(bf16[4,88,1024]{2,1,0:T(8,128)(2,1)S(1)} %shard_map.92), channel_id=1, replica_groups={{0,64,128,192},{16,80,144,208},{32,96,160,224},{48,112,176,240},{1,65,1..., dimensions={0} | all-to-all | bytes 1441792 | tf_op jit(solution)/shard_map/all_to_all | solution.py:32
  95.9 0.8 shard_map.93
  96.7 0.7 copy-done
  97.4 3.6 %all-to-all-start.5 = ((bf16[8,24,1024]{2,1,0:T(8,128)(2,1)}), bf16[8,24,1024]{2,1,0:T(8,128)(2,1)S(1)}, u32[]{:S(2)}, u32[]{:S(2)}) async-start(bf16[8,24,1024]{2,1,0:T(8,128)(2,1)} %get-tuple-element.13), calls=%async_computation.5 | async-start | bytes 786432 | tf_op jit(solution)/shard_map/all_to_all | solution.py:32
  101.0 1.3 shard_map.94
  102.2 10.8 %all-to-all-done.5.mine_ref = bf16[8,24,1024]{2,1,0:T(8,128)(2,1)S(1)} async-done(((bf16[8,24,1024]{2,1,0:T(8,128)(2,1)}), bf16[8,24,1024]{2,1,0:T(8,128)(2,1)S(1)}, u32[]{:S(2)}, u32[]{:S(2)}) %all-to-all-start.5) | async-done | bytes 393248 | tf_op jit(solution)/shard_map/all_to_all | solution.py:32
  113.0 6.2 %all-to-all-start.6 = ((bf16[4,384,256]{2,1,0:T(8,128)(2,1)}), bf16[4,384,256]{2,1,0:T(8,128)(2,1)S(1)}, u32[]{:S(2)}, u32[]{:S(2)}) async-start(bf16[4,384,256]{2,1,0:T(8,128)(2,1)} %shard_map.94), calls=%async_computation.6 | async-start | bytes 1572864 | tf_op jit(solution)/shard_map/all_to_all | solution.py:32
  119.2 0.0 collective-permute-start.7
  119.2 8.0 %all-to-all-done.6.turned_ref = bf16[4,384,256]{2,1,0:T(8,128)(2,1)S(1)} async-done(((bf16[4,384,256]{2,1,0:T(8,128)(2,1)}), bf16[4,384,256]{2,1,0:T(8,128)(2,1)S(1)}, u32[]{:S(2)}, u32[]{:S(2)}) %all-to-all-start.6) | async-done | bytes 786464 | tf_op jit(solution)/shard_map/all_to_all | solution.py:32
  127.3 0.9 copy-done.1
  128.2 1.7 shard_map.95
  130.0 13.5 %all_to_all.73.part_ref = bf16[4,448,128]{2,1,0:T(8,128)(2,1)S(1)} all-to-all(bf16[4,448,128]{2,1,0:T(8,128)(2,1)S(1)} %get-tuple-element.14), channel_id=1, replica_groups={{0,4,8,12},{1,5,9,13},{2,6,10,14},{3,7,11,15},{16,20,24,28},{17,21,25,2..., dimensions={0} | all-to-all | bytes 917504 | tf_op jit(solution)/shard_map/all_to_all | solution.py:32
  143.5 0.1 shard_map.96
  143.5 0.0 copy-start.2
  143.5 10.2 %all_to_all.74.refs_0_ = bf16[4,448,128]{2,1,0:T(8,128)(2,1)S(1)} all-to-all(bf16[4,448,128]{2,1,0:T(8,128)(2,1)S(1)} %shard_map.96), channel_id=1, replica_groups={{0,1,2,3},{4,5,6,7},{8,9,10,11},{12,13,14,15},{16,17,18,19},{20,21,22,2..., dimensions={0} | all-to-all | bytes 917504 | tf_op jit(solution)/shard_map/all_to_all | solution.py:32
  153.8 0.7 copy-done.8
  154.4 0.9 shard_map.97
  155.4 0.7 collective-permute-start.8
  156.1 22.8 %all_to_all.75.refs_0_ = bf16[4,4,64,256]{3,2,1,0:T(8,128)(2,1)S(1)} all-to-all(bf16[4,4,64,256]{3,2,1,0:T(8,128)(2,1)S(1)} %broadcast_in_dim.5), channel_id=1, replica_groups={{0,4,8,12},{1,5,9,13},{2,6,10,14},{3,7,11,15},{16,20,24,28},{17,21,25,2..., dimensions={0} | all-to-all | bytes 1048576 | tf_op jit(solution)/shard_map/all_to_all | solution.py:32
  179.0 3.1 %shard_map.98 = bf16[4,64,1024]{2,1,0:T(8,128)(2,1)S(1)} custom-call(bf16[4,4,64,256]{3,2,1,0:T(8,128)(2,1)S(1)} %all_to_all.75.refs_0_, bf16[1024,256]{1,0:T(8,128)(2,1)S(1)} %bitcast.5, bf16[1024,256]{1,0:T(8,128)(2,1)S(1)} %collective-permute-done.4.refs_6_.refs_2_, bf16[1024,256]{1,0:T(8,128)(2,1)S(1)} %collective-permute-done.5.refs_7_.refs_3_, ...), custom_call_target="tpu_custom_call" | custom-call | flops 536870912 | bytes 3145728 | tf_op jit(solution)/shard_map/pallas_call | solution.py:85
  182.0 14.3 %all_to_all.76.part_ref = bf16[4,64,1024]{2,1,0:T(8,128)(2,1)S(1)} all-to-all(bf16[4,64,1024]{2,1,0:T(8,128)(2,1)S(1)} %shard_map.98), channel_id=1, replica_groups={{0,64,128,192},{16,80,144,208},{32,96,160,224},{48,112,176,240},{1,65,1..., dimensions={0} | all-to-all | bytes 1048576 | tf_op jit(solution)/shard_map/all_to_all | solution.py:32
  196.3 0.4 shard_map.99
  196.7 10.1 %all_to_all.77.part_ref = bf16[4,448,128]{2,1,0:T(8,128)(2,1)S(1)} all-to-all(bf16[4,448,128]{2,1,0:T(8,128)(2,1)S(1)} %get-tuple-element.17), channel_id=1, replica_groups={{0,4,8,12},{1,5,9,13},{2,6,10,14},{3,7,11,15},{16,20,24,28},{17,21,25,2..., dimensions={0} | all-to-all | bytes 917504 | tf_op jit(solution)/shard_map/all_to_all | solution.py:32
  206.8 0.1 shard_map.100
  206.9 10.8 %all_to_all.78.refs_0_ = bf16[4,448,128]{2,1,0:T(8,128)(2,1)S(1)} all-to-all(bf16[4,448,128]{2,1,0:T(8,128)(2,1)S(1)} %shard_map.100), channel_id=1, replica_groups={{0,1,2,3},{4,5,6,7},{8,9,10,11},{12,13,14,15},{16,17,18,19},{20,21,22,2..., dimensions={0} | all-to-all | bytes 917504 | tf_op jit(solution)/shard_map/all_to_all | solution.py:32
  217.7 0.7 copy-done.9
  218.3 1.0 shard_map.101
  219.4 8.4 %all_to_all.79 = bf16[4,64,256]{2,1,0:T(8,128)(2,1)S(1)} all-to-all(bf16[4,64,256]{2,1,0:T(8,128)(2,1)S(1)} %shard_map.101), channel_id=1, replica_groups={{0,1,2,3},{4,5,6,7},{8,9,10,11},{12,13,14,15},{16,17,18,19},{20,21,22,2..., dimensions={0} | all-to-all | bytes 262144 | tf_op jit(solution)/shard_map/all_to_all | solution.py:32
  227.7 0.7 convert_element_type.3
  (22 shorter events, 0.1 us)
Async XLA Ops:
  12.8 14.1 %copy-start.3 = (bf16[6,256,128]{2,1,0:T(8,128)(2,1)S(1)}, bf16[6,256,128]{2,1,0:T(8,128)(2,1)}, u32[]{:S(2)}) copy-start(bf16[6,256,128]{2,1,0:T(8,128)(2,1)} %low_ref.2) | copy-start | bytes 1179652
  12.8 14.1 %copy-start.4 = (bf16[6,256,128]{2,1,0:T(8,128)(2,1)S(1)}, bf16[6,256,128]{2,1,0:T(8,128)(2,1)}, u32[]{:S(2)}) copy-start(bf16[6,256,128]{2,1,0:T(8,128)(2,1)} %up_ref.2) | copy-start | bytes 1179652
  12.8 14.1 %copy-start.7 = (f32[4,64,256]{2,1,0:T(8,128)S(1)}, f32[4,64,256]{2,1,0:T(8,128)}, u32[]{:S(2)}) copy-start(f32[4,64,256]{2,1,0:T(8,128)} %right_ref.1) | copy-start | bytes 786436
  12.8 11.7 %all-to-all-start.3 = ((bf16[4,256,256]{2,1,0:T(8,128)(2,1)}), bf16[4,256,256]{2,1,0:T(8,128)(2,1)S(1)}, u32[]{:S(2)}, u32[]{:S(2)}) async-start(bf16[4,256,256]{2,1,0:T(8,128)(2,1)} %param.17), calls=%async_computation.3 | async-start | bytes 1048576 | tf_op jit(solution)/shard_map/all_to_all | solution.py:32
  17.9 41.8 %collective-permute-start.2 = (bf16[1024,256]{1,0:T(8,128)(2,1)S(1)}, bf16[1024,256]{1,0:T(8,128)(2,1)}, u32[]{:S(2)}, u32[]{:S(2)}) collective-permute-start(bf16[1024,256]{1,0:T(8,128)(2,1)S(1)} %bitcast.6), channel_id=1, source_target_pairs={{0,32},{1,33},{2,34},{3,35},{4,36},{5,37},{6,38},{7,39},{8,40},{9,... | collective-permute-start | bytes 1572872 | tf_op jit(solution)/shard_map/ppermute | solution.py:28
  24.5 35.2 %collective-permute-start.5 = (bf16[1024,256]{1,0:T(8,128)(2,1)S(1)}, bf16[1024,256]{1,0:T(8,128)(2,1)S(1)}, u32[]{:S(2)}, u32[]{:S(2)}) collective-permute-start(bf16[1024,256]{1,0:T(8,128)(2,1)S(1)} %bitcast.2), channel_id=1, source_target_pairs={{0,32},{1,33},{2,34},{3,35},{4,36},{5,37},{6,38},{7,39},{8,40},{9,... | collective-permute-start | bytes 1572872 | tf_op jit(solution)/shard_map/ppermute | solution.py:28
  35.8 0.7 collective-permute-start
  37.4 30.9 %all-to-all-start.1 = ((bf16[4,4,88,256]{3,2,1,0:T(8,128)(2,1)}), bf16[4,4,88,256]{3,2,1,0:T(8,128)(2,1)S(1)}, u32[]{:S(2)}, u32[]{:S(2)}) async-start(bf16[4,4,88,256]{3,2,1,0:T(8,128)(2,1)} %broadcast_in_dim.4), calls=%async_computation.1 | async-start | bytes 1441792 | tf_op jit(solution)/shard_map/all_to_all | solution.py:32
  59.2 9.1 %collective-permute-start.1 = (bf16[1024,256]{1,0:T(8,128)(2,1)S(1)}, bf16[1024,256]{1,0:T(8,128)(2,1)}, u32[]{:S(2)}, u32[]{:S(2)}) collective-permute-start(bf16[1024,256]{1,0:T(8,128)(2,1)S(1)} %bitcast.7), channel_id=1, source_target_pairs={{0,16},{1,17},{2,18},{3,19},{4,20},{5,21},{6,22},{7,23},{8,24},{9,... | collective-permute-start | bytes 1572872 | tf_op jit(solution)/shard_map/ppermute | solution.py:28
  59.2 9.1 %collective-permute-start.4 = (bf16[1024,256]{1,0:T(8,128)(2,1)S(1)}, bf16[1024,256]{1,0:T(8,128)(2,1)S(1)}, u32[]{:S(2)}, u32[]{:S(2)}) collective-permute-start(bf16[1024,256]{1,0:T(8,128)(2,1)S(1)} %bitcast.3), channel_id=1, source_target_pairs={{0,16},{1,17},{2,18},{3,19},{4,20},{5,21},{6,22},{7,23},{8,24},{9,... | collective-permute-start | bytes 1572872 | tf_op jit(solution)/shard_map/ppermute | solution.py:28
  59.7 8.6 %collective-permute-start.3 = (bf16[1024,256]{1,0:T(8,128)(2,1)}, bf16[1024,256]{1,0:T(8,128)(2,1)}, u32[]{:S(2)}, u32[]{:S(2)}) collective-permute-start(bf16[1024,256]{1,0:T(8,128)(2,1)} %collective-permute-done.2.refs_3_), channel_id=1, source_target_pairs={{0,16},{1,17},{2,18},{3,19},{4,20},{5,21},{6,22},{7,23},{8,24},{9,... | collective-permute-start | bytes 1572872 | tf_op jit(solution)/shard_map/ppermute | solution.py:28
  59.7 8.6 %collective-permute-start.6 = (bf16[1024,256]{1,0:T(8,128)(2,1)S(1)}, bf16[1024,256]{1,0:T(8,128)(2,1)S(1)}, u32[]{:S(2)}, u32[]{:S(2)}) collective-permute-start(bf16[1024,256]{1,0:T(8,128)(2,1)S(1)} %collective-permute-done.5.refs_7_.refs_3_), channel_id=1, source_target_pairs={{0,16},{1,17},{2,18},{3,19},{4,20},{5,21},{6,22},{7,23},{8,24},{9,... | collective-permute-start | bytes 1572872 | tf_op jit(solution)/shard_map/ppermute | solution.py:28
  96.7 0.7 copy-start
  97.4 3.6 %copy-start.5 = (bf16[6,256,128]{2,1,0:T(8,128)(2,1)S(1)}, bf16[6,256,128]{2,1,0:T(8,128)(2,1)}, u32[]{:S(2)}) copy-start(bf16[6,256,128]{2,1,0:T(8,128)(2,1)} %low_ref.3) | copy-start | bytes 1179652
  97.4 3.6 %copy-start.6 = (bf16[6,256,128]{2,1,0:T(8,128)(2,1)S(1)}, bf16[6,256,128]{2,1,0:T(8,128)(2,1)}, u32[]{:S(2)}) copy-start(bf16[6,256,128]{2,1,0:T(8,128)(2,1)} %up_ref.3) | copy-start | bytes 1179652
  97.4 15.6 %all-to-all-start.5 = ((bf16[8,24,1024]{2,1,0:T(8,128)(2,1)}), bf16[8,24,1024]{2,1,0:T(8,128)(2,1)S(1)}, u32[]{:S(2)}, u32[]{:S(2)}) async-start(bf16[8,24,1024]{2,1,0:T(8,128)(2,1)} %get-tuple-element.13), calls=%async_computation.5 | async-start | bytes 786432 | tf_op jit(solution)/shard_map/all_to_all | solution.py:32
  113.0 14.3 %all-to-all-start.6 = ((bf16[4,384,256]{2,1,0:T(8,128)(2,1)}), bf16[4,384,256]{2,1,0:T(8,128)(2,1)S(1)}, u32[]{:S(2)}, u32[]{:S(2)}) async-start(bf16[4,384,256]{2,1,0:T(8,128)(2,1)} %shard_map.94), calls=%async_computation.6 | async-start | bytes 1572864 | tf_op jit(solution)/shard_map/all_to_all | solution.py:32
  119.2 8.0 %collective-permute-start.7 = (bf16[8,24,1024]{2,1,0:T(8,128)(2,1)S(1)}, bf16[8,24,1024]{2,1,0:T(8,128)(2,1)}, u32[]{:S(2)}, u32[]{:S(2)}) collective-permute-start(bf16[8,24,1024]{2,1,0:T(8,128)(2,1)S(1)} %all-to-all-done.5.mine_ref), channel_id=1, source_target_pairs={{0,16},{1,17},{2,18},{3,19},{4,20},{5,21},{6,22},{7,23},{8,24},{9,... | collective-permute-start | bytes 1179656 | tf_op jit(solution)/shard_map/ppermute | solution.py:28
  127.3 1.0 copy-start.1
  143.5 10.3 %copy-start.2 = (f32[64,1024]{1,0:T(8,128)S(1)}, f32[64,1024]{1,0:T(8,128)}, u32[]{:S(2)}) copy-start(f32[64,1024]{1,0:T(8,128)} %copy-done) | copy-start | bytes 786436
  153.8 0.7 copy-start.8
  155.4 0.7 collective-permute-start.8
  217.7 0.7 copy-start.9

commit v4 on v3

--- a/solution.py
+++ b/solution.py
@@ -10,8 +10,6 @@
 F32 = jnp.float32
 SIDE = 4
 X_GROUPS = [[SIDE * y + x for x in range(SIDE)] for y in range(SIDE)]
-Y_GROUPS = [[SIDE * y + x for y in range(SIDE)] for x in range(SIDE)]
-Q_GROUPS = [[SIDE * q + j for q in range(SIDE)] for j in range(SIDE)]
 Z_GROUPS = [[2 * z + core for z in range(8)] for core in range(2)]
 
 
@@ -36,10 +34,45 @@
     return exchanged(value, "col", X_GROUPS)
 
 
-def from_everyone(value, axis, groups):
-    return exchanged(
-        jnp.broadcast_to(value[None], (len(groups[0]), *value.shape)), axis, groups
-    )
+def gathered_y(value):
+    return [value] + [
+        permuted(value, lambda q, j, y, x: (q, j, (y + s) % SIDE, x)) for s in range(1, SIDE)
+    ]
+
+
+def gathered_x(value):
+    return [value] + [
+        permuted(value, lambda q, j, y, x: (q, j, y, (x + s) % SIDE)) for s in range(1, SIDE)
+    ]
+
+
+def scattered_q(values):
+    return [values[0]] + [
+        permuted(values[s], lambda q, j, y, x: ((q + s) % SIDE, j, y, x))
+        for s in range(1, SIDE)
+    ]
+
+
+def scattered_x(values):
+    return [values[0]] + [
+        permuted(values[s], lambda q, j, y, x: (q, j, y, (x + s) % SIDE))
+        for s in range(1, SIDE)
+    ]
+
+
+def scattered_and_swapped(values):
+    return [
+        permuted(values[s], lambda q, j, y, x: (y, j, q, (x + s) % SIDE))
+        for s in range(SIDE)
+    ]
+
+
+def own_tile():
+    return lax.rem(lax.axis_index("col"), SIDE)
+
+
+def wrapped(value):
+    return lax.rem(value + 2 * SIDE, SIDE)
 
 
 def swapped(value):
@@ -73,7 +106,7 @@
     return [t for t in range(SIDE) if t != tile]
 
 
-def kernel_call(body, out_shape, smem=(), flops=0, grid=None, in_specs=None, out_specs=None):
+def kernel_call(body, out_shape, smem=(), flops=0, grid=None, in_specs=None, out_specs=None, scratch=()):
     def run(*args):
         specs = in_specs or [
             pl.BlockSpec(memory_space=pltpu.SMEM if at in smem else pltpu.VMEM)
@@ -86,6 +119,7 @@
             body,
             out_shape=out_shape,
             in_specs=specs,
+            scratch_shapes=list(scratch),
             compiler_params=pltpu.CompilerParams(vmem_limit_bytes=30 * 2**20),
             cost_estimate=pl.CostEstimate(
                 flops=flops, bytes_accessed=moved, transcendentals=0
@@ -96,7 +130,7 @@
     return run
 
 
-def pack_kernel(right_ref, low_ref, up_ref, out_ref):
+def pack_kernel(right_ref, low_ref, up_ref, *out_refs):
     n = right_ref.shape[1]
     rank_cols = low_ref.shape[2]
     share = rank_cols // lax.axis_size("row")
@@ -104,13 +138,29 @@
     at = lax.broadcasted_iota(jnp.int32, (share, rank_cols), 1)
     want = lax.broadcasted_iota(jnp.int32, (share, rank_cols), 0) + row * share
     pick = (at == want).astype(F32).astype(BF16)
-    for tile in range(SIDE):
-        out_ref[tile, :n] = right_ref[tile].astype(BF16)
-        pieces = [
-            dot_t(pick, (low_ref if t < tile else up_ref)[pair_of(tile, t)])
-            for t in partners(tile)
-        ]
-        out_ref[tile, n:] = jnp.concatenate(pieces, axis=0).astype(BF16)
+    for s, out_ref in enumerate(out_refs):
+        tile = wrapped(own_tile() + s)
+        out_ref[:n] = right_ref[tile].astype(BF16)
+        pieces = []
+        for slot in range(SIDE - 1):
+            pair, is_low = partner_pair(tile, slot)
+            piece = jnp.where(is_low, dot_t(pick, low_ref[pair]), dot_t(pick, up_ref[pair]))
+            pieces.append(piece)
+        out_ref[n:] = jnp.concatenate(pieces, axis=0).astype(BF16)
+
+
+def partner_pair(tile, slot):
+    is_low = slot < tile
+    partner = jnp.where(is_low, slot, slot + 1)
+    high = jnp.where(is_low, tile, partner)
+    low = jnp.where(is_low, partner, tile)
+    return jnp.where(high == 1, 0, jnp.where(high == 2, 1, 3)) + low, is_low
+
+
+def order_kernel(*refs):
+    out_ref = refs[-1]
+    for s in range(SIDE):
+        out_ref[wrapped(own_tile() - s)] = refs[s][...].astype(out_ref.dtype)
 
 
 def turn_kernel(low_ref, up_ref, out_ref):
@@ -126,42 +176,78 @@
             ).astype(BF16)
 
 
-def products_kernel(n, x_ref, *refs):
-    lower, upper, out_ref = refs[:SIDE], refs[SIDE : 2 * SIDE], refs[-1]
-    flip = lax.rem(lax.axis_index("row"), SIDE)
-    rows = x_ref.shape[2]
-    for span in range(SIDE):
-        blocks = [x_ref[span, at ^ flip] for at in range(SIDE)]
-        value = sum(dot_t(blocks[at], lower[at][...]) for at in range(SIDE))
+def products_kernel(n, padded, count, *refs):
+    x_refs, inverse_refs = refs[:SIDE], refs[SIDE : SIDE + count]
+    out_refs = refs[SIDE + count : 2 * SIDE + count]
+    joined_ref, extra_ref = refs[2 * SIDE + count :]
+    lower, upper = inverse_refs[:SIDE], inverse_refs[SIDE:]
+    rows = x_refs[0].shape[1]
+
+    @pl.when(pl.program_id(0) == 0)
+    def _():
+        row = lax.axis_index("row")
+        flip, q = lax.rem(row, SIDE), row // SIDE
+        y = lax.axis_index("col") // SIDE
+        for s in range(SIDE):
+            t = wrapped(y - s - q)
+            for at in range(SIDE):
+                block = x_refs[s][at ^ flip]
+                joined_ref[at, t, :rows] = block
+                if rows > n:
+                    extra_ref[at, t, : rows - n] = block[n:]
+
+    width = joined_ref.shape[3]
+    value = sum(
+        dot_t(joined_ref[at].reshape(SIDE * padded, width), lower[at][...])
+        for at in range(SIDE)
+    )
+    if rows > n:
+        other = sum(
+            dot_t(extra_ref[at].reshape(SIDE * (padded - n), width), upper[at][...])
+            for at in range(SIDE)
+        )
+        share = (rows - n) // (SIDE - 1)
+        slot = lax.broadcasted_iota(jnp.int32, (rows - n, value.shape[1]), 0) // share
+    for t in range(SIDE):
+        start = t * padded
+        out_refs[t][:n] = value[start : start + n].astype(BF16)
         if rows > n:
-            tile = lax.rem(lax.axis_index("col"), SIDE)
-            other = sum(dot_t(blocks[at][n:], upper[at][...]) for at in range(SIDE))
-            share = (rows - n) // (SIDE - 1)
-            slot = lax.broadcasted_iota(jnp.int32, other.shape, 0) // share
-            out_ref[span, :n] = value[:n].astype(BF16)
-            out_ref[span, n:] = jnp.where(slot < tile, value[n:], other).astype(BF16)
-        else:
-            out_ref[span] = value.astype(BF16)
+            mine = value[start + n : start + rows]
+            its = other[t * (padded - n) : t * (padded - n) + rows - n]
+            out_refs[t][n:] = jnp.where(slot < own_tile(), mine, its).astype(BF16)
 
 
 def products(n, gathered, *inverses):
-    spans, blocks, rows, width = gathered.shape
+    blocks, rows, width = gathered[0].shape
     total = inverses[0].shape[0]
+    padded = rows + -rows % 16
+    count = len(inverses)
+    whole = pl.BlockSpec(gathered[0].shape, lambda a: (0, 0, 0))
     return kernel_call(
-        lambda *refs: products_kernel(n, *refs),
-        jax.ShapeDtypeStruct((spans, rows, total), BF16),
-        flops=2 * spans * blocks * rows * width * total,
+        lambda *refs: products_kernel(n, padded, count, *refs),
+        [jax.ShapeDtypeStruct((rows, total), BF16)] * SIDE,
+        flops=2 * SIDE * blocks * rows * width * total,
         grid=(total // 256,),
-        in_specs=[pl.BlockSpec(gathered.shape, lambda a: (0, 0, 0, 0))]
+        in_specs=[whole] * SIDE
         + [pl.BlockSpec((256, width), lambda a: (a, 0)) for _ in inverses],
-        out_specs=pl.BlockSpec((spans, rows, 256), lambda a: (0, 0, a)),
-    )(gathered, *inverses)
-
-
-def total_kernel(n, part_ref, dense_ref, extra_ref):
-    whole = part_ref[0].astype(F32)
-    for at in range(1, SIDE):
-        whole = whole + part_ref[at].astype(F32)
+        out_specs=[pl.BlockSpec((rows, 256), lambda a: (0, a))] * SIDE,
+        scratch=[
+            pltpu.VMEM((blocks, SIDE, padded, width), BF16),
+            pltpu.VMEM((blocks, SIDE, max(padded - n, 16), width), BF16),
+        ],
+    )(*gathered, *inverses)
+
+
+def summed(refs):
+    whole = refs[0][...].astype(F32)
+    for ref in refs[1:]:
+        whole = whole + ref[...].astype(F32)
+    return whole
+
+
+def total_kernel(n, *refs):
+    dense_ref, extra_ref = refs[SIDE:]
+    whole = summed(refs[:SIDE])
     dense_ref[...] = whole[:n]
     extra = whole[n:].astype(BF16)
     for at in range(extra_ref.shape[0]):
@@ -214,42 +300,37 @@
     one = tile == 1
     pick = lambda a, b: jnp.where(one, a, b)
     pieces += [coupling(0, pick(1, 2)), coupling(pick(0, 1), 2)]
-    send = jnp.concatenate(pieces, axis=0).astype(BF16)
-    for at in range(SIDE):
-        send_ref[at] = send
+    send_ref[...] = jnp.concatenate(pieces, axis=0).astype(BF16)
     later_ref[:rank_cols] = coupling(pick(1, 2), 0).astype(BF16)
     later_ref[rank_cols:] = coupling(2, pick(0, 1)).astype(BF16)
 
 
-def last_project_kernel(part_ref, turned_ref, later_ref, dense_ref, send_ref):
+def last_project_kernel(*refs):
+    turned_ref, later_ref, dense_ref, send_ref = refs[SIDE:]
     slots = SIDE - 1
     rank_cols = turned_ref.shape[1] // slots
-    whole = part_ref[0].astype(F32)
-    for at in range(1, SIDE):
-        whole = whole + part_ref[at].astype(F32)
+    whole = summed(refs[:SIDE])
     dense_ref[...] = whole
     dense = whole.astype(BF16)
     pieces = [project(dense, turned_ref, slot, rank_cols) for slot in range(slots)]
     send = jnp.concatenate(pieces, axis=0).astype(BF16)
     n = send.shape[0]
-    for at in range(SIDE):
-        send_ref[at, :n] = send
-        send_ref[at, n:] = later_ref[...]
-
-
-def add_kernel(part_ref, out_ref):
-    whole = part_ref[0].astype(F32)
-    for at in range(1, SIDE):
-        whole = whole + part_ref[at].astype(F32)
-    whole = whole.astype(BF16)
-    for at in range(SIDE):
-        out_ref[at] = whole
-
-
-def finish_kernel(is_lower, sums_ref, dense_ref, extra_ref, ranks_ref, out_ref):
+    send_ref[:n] = send
+    send_ref[n:] = later_ref[...]
+
+
+def add_kernel(*refs):
+    refs[-1][...] = summed(refs[:-1]).astype(BF16)
+
+
+def finish_kernel(is_lower, *refs):
+    dense_ref, extra_ref, ranks_ref = refs[SIDE : SIDE + 3]
+    out_refs, (sums_ref, held_ref) = refs[SIDE + 3 : -2], refs[-2:]
+    for s in range(SIDE):
+        sums_ref[wrapped(own_tile() - s)] = refs[s][...]
     n = dense_ref.shape[0]
     rank_cols = extra_ref.shape[0] // (SIDE - 1)
-    width = out_ref.shape[2]
+    width = held_ref.shape[2]
     tile = lax.rem(lax.axis_index("col"), SIDE)
     columns = lax.broadcasted_iota(jnp.int32, (n, rank_cols), 1)
     at_coupling = (SIDE - 1) * n
@@ -289,8 +370,14 @@
             mine, extra_ref[slot * rank_cols : (slot + 1) * rank_cols]
         )
     result = result.astype(BF16)
-    for at in range(SIDE):
-        out_ref[at] = result[:, at * width : (at + 1) * width]
+    if is_lower:
+        for at in range(SIDE):
+            out_refs[0][at] = result[:, at * width : (at + 1) * width]
+    else:
+        for at in range(SIDE):
+            held_ref[at] = result[:, at * width : (at + 1) * width]
+        for s in range(SIDE):
+            out_refs[s][...] = held_ref[wrapped(own_tile() + s)]
 
 
 def quad_of(value):
@@ -308,24 +395,28 @@
     total = SIDE * width
     shape = jax.ShapeDtypeStruct
 
+    height = n + slots * share
+    rows = kernel_call(pack_kernel, [shape((height, width), BF16)] * SIDE)(
+        right_sides, low_left, up_left
+    )
+    inv_lower, inv_upper, low_right, up_right, *rows = lax.optimization_barrier(
+        (inv_lower, inv_upper, low_right, up_right, *rows)
+    )
     lower = quad_of(over_x(inv_lower).reshape(total, width))
-    rows = kernel_call(
-        pack_kernel, shape((SIDE, n + slots * share, width), BF16)
-    )(right_sides, low_left, up_left)
-    rows = swapped(over_x(rows))
     upper = quad_of(over_x(inv_upper).reshape(total, width))
-    gathered = from_everyone(rows, "col", Y_GROUPS).reshape(SIDE, SIDE, -1, width)
     turned = over_x(
         kernel_call(turn_kernel, shape((SIDE, slots * rank_cols, width), BF16))(
             low_right, up_right
         )
     )
-    partial = products(n, gathered, *lower, *upper)
-    received = exchanged(partial, "row", Q_GROUPS)
+    rows = kernel_call(order_kernel, shape((SIDE, height, width), BF16))(
+        *scattered_and_swapped(rows)
+    )
+    partial = products(n, gathered_y(rows), *lower, *upper)
     dense, extra = kernel_call(
         lambda *refs: total_kernel(n, *refs),
         (shape((n, total), F32), shape((8, slots * share, total), BF16)),
-    )(received)
+    )(*scattered_q(partial))
     mine = exchanged(extra, "row", Z_GROUPS)
     other = swap_core(mine)
     packed = slots * n + 2 * rank_cols
@@ -333,31 +424,32 @@
         couple_kernel,
         (
             shape((slots * rank_cols, total), BF16),
-            shape((SIDE, packed, rank_cols), BF16),
+            shape((packed, rank_cols), BF16),
             shape((2 * rank_cols, rank_cols), BF16),
         ),
     )(dense, mine, other, turned)
 
     def finished(is_lower, send, dense, ranks):
-        sums = kernel_call(add_kernel, shape((SIDE, packed, rank_cols), BF16))(
-            exchanged(send, "col", Y_GROUPS)
-        )
+        sums = kernel_call(add_kernel, shape((packed, rank_cols), BF16))(*gathered_y(send))
+        outs = [shape((SIDE, n, width), BF16)] if is_lower else [shape((n, width), BF16)] * SIDE
         return kernel_call(
             lambda *refs: finish_kernel(is_lower, *refs),
-            shape((SIDE, n, width), BF16),
-            smem=(3,),
-        )(over_x(sums), dense, extra, ranks)
-
-    rows = finished(True, send, dense, low_ranks)
-    gathered = from_everyone(swapped(rows), "col", Y_GROUPS)
-    gathered = gathered.reshape(SIDE, SIDE, n, width)
-    received = exchanged(products(n, gathered, *upper), "row", Q_GROUPS)
+            outs,
+            smem=(SIDE + 2,),
+            scratch=[
+                pltpu.VMEM((SIDE, packed, rank_cols), BF16),
+                pltpu.VMEM((SIDE, n, width), BF16),
+            ],
+        )(*gathered_x(sums), dense, extra, ranks)
+
+    [rows] = finished(True, send, dense, low_ranks)
+    received = scattered_q(products(n, gathered_y(swapped(rows)), *upper))
     dense, send = kernel_call(
         last_project_kernel,
-        (shape((n, total), F32), shape((SIDE, packed, rank_cols), BF16)),
-    )(received, turned, later)
+        (shape((n, total), F32), shape((packed, rank_cols), BF16)),
+    )(*received, turned, later)
     rows = finished(False, send, dense, up_ranks)
-    return over_x(rows).astype(F32)
+    return kernel_call(order_kernel, shape((SIDE, n, width), F32))(*scattered_x(rows))
 
 
 def solution(mesh):

time: 229 us -> 221 us (0.965)
  blocking collectives: 132 us -> 12.6 us
  starting transfers between devices: 43.3 us -> 102 us
  waiting for transfers between devices: 31.6 us -> 89.6 us
  Pallas kernels: 16.3 us -> 11.6 us
    all_to_all x10 -> x1, blocking collectives: 132 us -> 12.6 us  [exchanged(): lax.all_to_all(value, axis, 0, 0, tiled=True, axis_index_groups=groups)]
    ppermute x9 -> x39, starting transfers between devices: 6.67 us -> 85.3 us  [permuted(): return lax.ppermute(value, ('row', 'col'), routes(to))]
    ppermute x9 -> x39, waiting for transfers between devices: 0.02 us -> 65.8 us  [permuted(): return lax.ppermute(value, ('row', 'col'), routes(to))]
    all_to_all x4 -> x3, starting transfers between devices: 36.6 us -> 16.6 us  [exchanged(): lax.all_to_all(value, axis, 0, 0, tiled=True, axis_index_groups=groups)]
    all_to_all x4 -> x3, waiting for transfers between devices: 31.6 us -> 23.8 us  [exchanged(): lax.all_to_all(value, axis, 0, 0, tiled=True, axis_index_groups=groups)]
    pallas_call x11 -> x13, Pallas kernels: 16.3 us -> 11.6 us  [run(): pl.pallas_call(body, out_shape=out_shape, in_specs=specs, scratch_shapes=...]
  transfers between devices with their start and end apart: 13 -> 42, of which waited for: 4 -> 29; matrix products, arithmetic and copies ran while one was open for 0% -> 0% of each run, Pallas kernels for 1% -> 1%
where the time goes in v4:
time: 221 us; the launch traced here: 219 us
  starting transfers between devices  102 us (46%)
  waiting for transfers between devices  89.6 us (41%)
  blocking collectives  12.6 us (6%)
  Pallas kernels  11.6 us (5%)
  local copies, waits for them, and re-layouts  3.49 us (2%)
    ppermute x39, starting transfers between devices, permuted(): return lax.ppermute(value, ('row', 'col'), routes(to))  85.3 us
    ppermute x39, waiting for transfers between devices, permuted(): return lax.ppermute(value, ('row', 'col'), routes(to))  65.8 us
    all_to_all x3, waiting for transfers between devices, exchanged(): lax.all_to_all(value, axis, 0, 0, tiled=True, axis_index_groups=groups)  23.8 us
    all_to_all x3, starting transfers between devices, exchanged(): lax.all_to_all(value, axis, 0, 0, tiled=True, axis_index_groups=groups)  16.6 us
    all_to_all x1, blocking collectives, exchanged(): lax.all_to_all(value, axis, 0, 0, tiled=True, axis_index_groups=groups)  12.6 us
    pallas_call x13, Pallas kernels, run(): pl.pallas_call(body, out_shape=out_shape, in_specs=specs, scratch_shapes=...  11.6 us
  transfers between devices with their start and end apart: 42, of which 29 were waited for; matrix products, arithmetic and copies ran while one was open for 0% of the time, Pallas kernels for 1%

profile of v4, /device:TPU:2, one launch (start us, length us, event | category | flops | bytes accessed | tf_op | source)
XLA Modules:
  0.0 219.4 jit_solution(13632761835915843520)
XLA Ops:
  4.0 12.6 %all_to_all.20 = bf16[4,256,256]{2,1,0:T(8,128)(2,1)S(1)} all-to-all(bf16[4,256,256]{2,1,0:T(8,128)(2,1)S(1)} %copy-done.7), channel_id=1, replica_groups={{0,1,2,3},{4,5,6,7},{8,9,10,11},{12,13,14,15},{16,17,18,19},{20,21,22,2..., dimensions={0} | all-to-all | bytes 1048576 | tf_op jit(solution)/shard_map/all_to_all | solution.py:30
  16.6 4.9 %all-to-all-start = ((bf16[4,256,256]{2,1,0:T(8,128)(2,1)}), bf16[4,256,256]{2,1,0:T(8,128)(2,1)S(1)}, u32[]{:S(2)}, u32[]{:S(2)}) async-start(bf16[4,256,256]{2,1,0:T(8,128)(2,1)} %param.16), calls=%async_computation | async-start | bytes 1048576 | tf_op jit(solution)/shard_map/all_to_all | solution.py:30
  21.5 1.9 collective-permute-start.11
  23.4 5.1 %all-to-all-done = bf16[4,256,256]{2,1,0:T(8,128)(2,1)S(1)} async-done(((bf16[4,256,256]{2,1,0:T(8,128)(2,1)}), bf16[4,256,256]{2,1,0:T(8,128)(2,1)S(1)}, u32[]{:S(2)}, u32[]{:S(2)}) %all-to-all-start) | async-done | bytes 524320 | tf_op jit(solution)/shard_map/all_to_all | solution.py:30
  28.6 2.0 collective-permute-start.8
  31.3 3.5 %collective-permute-start.2 = (bf16[88,256]{1,0:T(8,128)(2,1)S(1)}, bf16[88,256]{1,0:T(8,128)(2,1)S(1)}, u32[]{:S(2)}, u32[]{:S(2)}) collective-permute-start(bf16[88,256]{1,0:T(8,128)(2,1)S(1)} %get-tuple-element.42), channel_id=1, source_target_pairs={{0,2},{1,3},{2,0},{3,1},{4,66},{5,67},{6,64},{7,65},{8,130},{9,131... | collective-permute-start | bytes 135176 | tf_op jit(solution)/shard_map/ppermute | solution.py:26
  35.4 1.5 collective-permute-done.2.refs_2_
  36.9 1.9 collective-permute-done.3.refs_3_
  38.9 28.8 %collective-permute-start.6 = (bf16[4,88,256]{2,1,0:T(8,128)(2,1)S(1)}, bf16[4,88,256]{2,1,0:T(8,128)(2,1)S(1)}, u32[]{:S(2)}, u32[]{:S(2)}) collective-permute-start(bf16[4,88,256]{2,1,0:T(8,128)(2,1)S(1)} %shard_map.92.refs_0_), channel_id=1, source_target_pairs={{0,12},{1,13},{2,14},{3,15},{4,0},{5,1},{6,2},{7,3},{8,4},{9,5},{1... | collective-permute-start | bytes 540680 | tf_op jit(solution)/shard_map/ppermute | solution.py:26
  68.7 3.9 %collective-permute-done.6.refs_3_ = bf16[4,88,256]{2,1,0:T(8,128)(2,1)S(1)} collective-permute-done((bf16[4,88,256]{2,1,0:T(8,128)(2,1)S(1)}, bf16[4,88,256]{2,1,0:T(8,128)(2,1)S(1)}, u32[]{:S(2)}, u32[]{:S(2)}) %collective-permute-start.6) | collective-permute-done | bytes 180256 | tf_op jit(solution)/shard_map/ppermute | solution.py:26
  72.6 2.3 %collective-permute-start.5 = (bf16[4,88,256]{2,1,0:T(8,128)(2,1)S(1)}, bf16[4,88,256]{2,1,0:T(8,128)(2,1)S(1)}, u32[]{:S(2)}, u32[]{:S(2)}) collective-permute-start(bf16[4,88,256]{2,1,0:T(8,128)(2,1)S(1)} %shard_map.92.refs_0_), channel_id=1, source_target_pairs={{0,8},{1,9},{2,10},{3,11},{4,12},{5,13},{6,14},{7,15},{8,0},{9,1},... | collective-permute-start | bytes 540680 | tf_op jit(solution)/shard_map/ppermute | solution.py:26
  74.9 6.6 %collective-permute-done.5.refs_2_ = bf16[4,88,256]{2,1,0:T(8,128)(2,1)S(1)} collective-permute-done((bf16[4,88,256]{2,1,0:T(8,128)(2,1)S(1)}, bf16[4,88,256]{2,1,0:T(8,128)(2,1)S(1)}, u32[]{:S(2)}, u32[]{:S(2)}) %collective-permute-start.5) | collective-permute-done | bytes 180256 | tf_op jit(solution)/shard_map/ppermute | solution.py:26
  81.5 6.7 %collective-permute-done.4.refs_1_ = bf16[4,88,256]{2,1,0:T(8,128)(2,1)S(1)} collective-permute-done((bf16[4,88,256]{2,1,0:T(8,128)(2,1)S(1)}, bf16[4,88,256]{2,1,0:T(8,128)(2,1)S(1)}, u32[]{:S(2)}, u32[]{:S(2)}) %collective-permute-start.4) | collective-permute-done | bytes 180256 | tf_op jit(solution)/shard_map/ppermute | solution.py:26
  88.2 2.4 %shard_map.93 = (bf16[88,1024]{1,0:T(8,128)(2,1)S(1)}, bf16[88,1024]{1,0:T(8,128)(2,1)S(1)}, bf16[88,1024]{1,0:T(8,128)(2,1)S(1)}, bf16[88,1024]{1,0:T(8,128)(2,1)S(1)}) custom-call(bf16[4,88,256]{2,1,0:T(8,128)(2,1)S(1)} %shard_map.92.refs_0_, bf16[4,88,256]{2,1,0:T(8,128)(2,1)S(1)} %collective-permute-done.4.refs_1_, ...), custom_call_target="tpu_custom_call" | custom-call | flops 738197504 | bytes 5636096 | tf_op jit(solution)/shard_map/pallas_call | solution.py:118
  90.6 1.8 collective-permute-start.13
  93.2 3.1 %collective-permute-start.15 = (bf16[88,1024]{1,0:T(8,128)(2,1)S(1)}, bf16[88,1024]{1,0:T(8,128)(2,1)S(1)}, u32[]{:S(2)}, u32[]{:S(2)}) collective-permute-start(bf16[88,1024]{1,0:T(8,128)(2,1)S(1)} %get-tuple-element.49), channel_id=1, source_target_pairs={{0,192},{1,193},{2,194},{3,195},{4,196},{5,197},{6,198},{7,199},{8... | collective-permute-start | bytes 540680 | tf_op jit(solution)/shard_map/ppermute | solution.py:26
  96.4 4.9 %collective-permute-done.13.refs_1_ = bf16[88,1024]{1,0:T(8,128)(2,1)S(1)} collective-permute-done((bf16[88,1024]{1,0:T(8,128)(2,1)S(1)}, bf16[88,1024]{1,0:T(8,128)(2,1)S(1)}, u32[]{:S(2)}, u32[]{:S(2)}) %collective-permute-start.13) | collective-permute-done | bytes 180256 | tf_op jit(solution)/shard_map/ppermute | solution.py:26
  101.2 3.2 %collective-permute-done.14.refs_2_ = bf16[88,1024]{1,0:T(8,128)(2,1)S(1)} collective-permute-done((bf16[88,1024]{1,0:T(8,128)(2,1)S(1)}, bf16[88,1024]{1,0:T(8,128)(2,1)S(1)}, u32[]{:S(2)}, u32[]{:S(2)}) %collective-permute-start.14) | collective-permute-done | bytes 180256 | tf_op jit(solution)/shard_map/ppermute | solution.py:26
  105.3 6.2 %all-to-all-start.2 = ((bf16[8,24,1024]{2,1,0:T(8,128)(2,1)}), bf16[8,24,1024]{2,1,0:T(8,128)(2,1)S(1)}, u32[]{:S(2)}, u32[]{:S(2)}) async-start(bf16[8,24,1024]{2,1,0:T(8,128)(2,1)} %get-tuple-element.51), calls=%async_computation.2 | async-start | bytes 786432 | tf_op jit(solution)/shard_map/all_to_all | solution.py:30
  112.8 10.6 %all-to-all-done.2.mine_ref = bf16[8,24,1024]{2,1,0:T(8,128)(2,1)S(1)} async-done(((bf16[8,24,1024]{2,1,0:T(8,128)(2,1)}), bf16[8,24,1024]{2,1,0:T(8,128)(2,1)S(1)}, u32[]{:S(2)}, u32[]{:S(2)}) %all-to-all-start.2) | async-done | bytes 393248 | tf_op jit(solution)/shard_map/all_to_all | solution.py:30
  123.4 5.5 %all-to-all-start.3 = ((bf16[4,384,256]{2,1,0:T(8,128)(2,1)}), bf16[4,384,256]{2,1,0:T(8,128)(2,1)S(1)}, u32[]{:S(2)}, u32[]{:S(2)}) async-start(bf16[4,384,256]{2,1,0:T(8,128)(2,1)} %shard_map.95), calls=%async_computation.3 | async-start | bytes 1572864 | tf_op jit(solution)/shard_map/all_to_all | solution.py:30
  128.9 8.0 %all-to-all-done.3.turned_ref.refs_4_ = bf16[4,384,256]{2,1,0:T(8,128)(2,1)S(1)} async-done(((bf16[4,384,256]{2,1,0:T(8,128)(2,1)}), bf16[4,384,256]{2,1,0:T(8,128)(2,1)S(1)}, u32[]{:S(2)}, u32[]{:S(2)}) %all-to-all-start.3) | async-done | bytes 786464 | tf_op jit(solution)/shard_map/all_to_all | solution.py:30
  136.9 1.7 shard_map.96
  140.2 1.3 collective-permute-start.17
  141.5 2.0 collective-permute-done.19.refs_3_
  143.5 2.1 collective-permute-done.18.refs_2_
  146.9 1.5 collective-permute-start.22
  148.5 2.5 %collective-permute-start.20 = (bf16[448,128]{1,0:T(8,128)(2,1)S(1)}, bf16[448,128]{1,0:T(8,128)(2,1)S(1)}, u32[]{:S(2)}, u32[]{:S(2)}) collective-permute-start(bf16[448,128]{1,0:T(8,128)(2,1)S(1)} %shard_map.97.refs_0_), channel_id=1, source_target_pairs={{0,1},{1,2},{2,3},{3,0},{4,5},{5,6},{6,7},{7,4},{8,9},{9,10},{10,1... | collective-permute-start | bytes 344072 | tf_op jit(solution)/shard_map/ppermute | solution.py:26
  151.7 3.0 %collective-permute-done.21.refs_2_ = bf16[448,128]{1,0:T(8,128)(2,1)S(1)} collective-permute-done((bf16[448,128]{1,0:T(8,128)(2,1)S(1)}, bf16[448,128]{1,0:T(8,128)(2,1)S(1)}, u32[]{:S(2)}, u32[]{:S(2)}) %collective-permute-start.21) | collective-permute-done | bytes 114720 | tf_op jit(solution)/shard_map/ppermute | solution.py:26
  156.7 13.3 %collective-permute-start.26 = (bf16[4,64,256]{2,1,0:T(8,128)(2,1)S(1)}, bf16[4,64,256]{2,1,0:T(8,128)(2,1)S(1)}, u32[]{:S(2)}, u32[]{:S(2)}) collective-permute-start(bf16[4,64,256]{2,1,0:T(8,128)(2,1)S(1)} %collective-permute-done.23.refs_0_), channel_id=1, source_target_pairs={{0,12},{1,13},{2,14},{3,15},{4,0},{5,1},{6,2},{7,3},{8,4},{9,5},{1... | collective-permute-start | bytes 393224 | tf_op jit(solution)/shard_map/ppermute | solution.py:26
  170.4 1.4 collective-permute-start.24
  172.6 4.0 %collective-permute-done.25.refs_2_ = bf16[4,64,256]{2,1,0:T(8,128)(2,1)S(1)} collective-permute-done((bf16[4,64,256]{2,1,0:T(8,128)(2,1)S(1)}, bf16[4,64,256]{2,1,0:T(8,128)(2,1)S(1)}, u32[]{:S(2)}, u32[]{:S(2)}) %collective-permute-start.25) | collective-permute-done | bytes 131104 | tf_op jit(solution)/shard_map/ppermute | solution.py:26
  177.9 1.5 shard_map.99
  179.9 2.0 collective-permute-start.28
  181.9 1.8 collective-permute-start.29
  183.7 3.0 %collective-permute-done.27.refs_1_ = bf16[64,1024]{1,0:T(8,128)(2,1)S(1)} collective-permute-done((bf16[64,1024]{1,0:T(8,128)(2,1)S(1)}, bf16[64,1024]{1,0:T(8,128)(2,1)S(1)}, u32[]{:S(2)}, u32[]{:S(2)}) %collective-permute-start.27) | collective-permute-done | bytes 131104 | tf_op jit(solution)/shard_map/ppermute | solution.py:26
  186.7 2.2 %collective-permute-done.28.refs_2_ = bf16[64,1024]{1,0:T(8,128)(2,1)S(1)} collective-permute-done((bf16[64,1024]{1,0:T(8,128)(2,1)S(1)}, bf16[64,1024]{1,0:T(8,128)(2,1)S(1)}, u32[]{:S(2)}, u32[]{:S(2)}) %collective-permute-start.28) | collective-permute-done | bytes 131104 | tf_op jit(solution)/shard_map/ppermute | solution.py:26
  189.0 2.9 %collective-permute-done.29.refs_3_ = bf16[64,1024]{1,0:T(8,128)(2,1)S(1)} collective-permute-done((bf16[64,1024]{1,0:T(8,128)(2,1)S(1)}, bf16[64,1024]{1,0:T(8,128)(2,1)S(1)}, u32[]{:S(2)}, u32[]{:S(2)}) %collective-permute-start.29) | collective-permute-done | bytes 131104 | tf_op jit(solution)/shard_map/ppermute | solution.py:26
  193.0 1.8 collective-permute-start.31
  194.8 2.4 %collective-permute-done.32.refs_3_ = bf16[448,128]{1,0:T(8,128)(2,1)S(1)} collective-permute-done((bf16[448,128]{1,0:T(8,128)(2,1)S(1)}, bf16[448,128]{1,0:T(8,128)(2,1)S(1)}, u32[]{:S(2)}, u32[]{:S(2)}) %collective-permute-start.32) | collective-permute-done | bytes 114720 | tf_op jit(solution)/shard_map/ppermute | solution.py:26
  197.2 2.1 collective-permute-done.31.refs_2_
  199.3 1.5 collective-permute-done.30.refs_1_
  200.8 2.4 %collective-permute-start.35 = (bf16[448,128]{1,0:T(8,128)(2,1)S(1)}, bf16[448,128]{1,0:T(8,128)(2,1)S(1)}, u32[]{:S(2)}, u32[]{:S(2)}) collective-permute-start(bf16[448,128]{1,0:T(8,128)(2,1)S(1)} %shard_map.101.refs_0_), channel_id=1, source_target_pairs={{0,3},{1,0},{2,1},{3,2},{4,7},{5,4},{6,5},{7,6},{8,11},{9,8},{10,9... | collective-permute-start | bytes 344072 | tf_op jit(solution)/shard_map/ppermute | solution.py:26
  204.0 1.4 collective-permute-start.33
  205.9 3.6 %collective-permute-done.34.refs_2_ = bf16[448,128]{1,0:T(8,128)(2,1)S(1)} collective-permute-done((bf16[448,128]{1,0:T(8,128)(2,1)S(1)}, bf16[448,128]{1,0:T(8,128)(2,1)S(1)}, u32[]{:S(2)}, u32[]{:S(2)}) %collective-permute-start.34) | collective-permute-done | bytes 114720 | tf_op jit(solution)/shard_map/ppermute | solution.py:26
  211.9 2.9 %collective-permute-start.37 = (bf16[64,256]{1,0:T(8,128)(2,1)S(1)}, bf16[64,256]{1,0:T(8,128)(2,1)S(1)}, u32[]{:S(2)}, u32[]{:S(2)}) collective-permute-start(bf16[64,256]{1,0:T(8,128)(2,1)S(1)} %get-tuple-element.65), channel_id=1, source_target_pairs={{0,2},{1,3},{2,0},{3,1},{4,6},{5,7},{6,4},{7,5},{8,10},{9,11},{10,... | collective-permute-start | bytes 98312 | tf_op jit(solution)/shard_map/ppermute | solution.py:26
  215.3 1.9 collective-permute-done.37.refs_2_
  217.3 1.4 collective-permute-done.38.refs_3_
  (66 shorter events, 23.7 us)
Async XLA Ops:
  0.0 1.0 copy-start
  2.9 1.0 copy-start.7
  16.6 12.0 %all-to-all-start = ((bf16[4,256,256]{2,1,0:T(8,128)(2,1)}), bf16[4,256,256]{2,1,0:T(8,128)(2,1)S(1)}, u32[]{:S(2)}, u32[]{:S(2)}) async-start(bf16[4,256,256]{2,1,0:T(8,128)(2,1)} %param.16), calls=%async_computation | async-start | bytes 1048576 | tf_op jit(solution)/shard_map/all_to_all | solution.py:30
  21.5 46.6 %collective-permute-start.11 = (bf16[1024,256]{1,0:T(8,128)(2,1)S(1)}, bf16[1024,256]{1,0:T(8,128)(2,1)S(1)}, u32[]{:S(2)}, u32[]{:S(2)}) collective-permute-start(bf16[1024,256]{1,0:T(8,128)(2,1)S(1)} %bitcast.2), channel_id=1, source_target_pairs={{0,32},{1,33},{2,34},{3,35},{4,36},{5,37},{6,38},{7,39},{8,40},{9,... | collective-permute-start | bytes 1572872 | tf_op jit(solution)/shard_map/ppermute | solution.py:26
  28.6 39.6 %collective-permute-start.8 = (bf16[1024,256]{1,0:T(8,128)(2,1)S(1)}, bf16[1024,256]{1,0:T(8,128)(2,1)S(1)}, u32[]{:S(2)}, u32[]{:S(2)}) collective-permute-start(bf16[1024,256]{1,0:T(8,128)(2,1)S(1)} %bitcast.6), channel_id=1, source_target_pairs={{0,32},{1,33},{2,34},{3,35},{4,36},{5,37},{6,38},{7,39},{8,40},{9,... | collective-permute-start | bytes 1572872 | tf_op jit(solution)/shard_map/ppermute | solution.py:26
  30.6 4.3 %collective-permute-start = (bf16[88,256]{1,0:T(8,128)(2,1)S(1)}, bf16[88,256]{1,0:T(8,128)(2,1)S(1)}, u32[]{:S(2)}, u32[]{:S(2)}) collective-permute-start(bf16[88,256]{1,0:T(8,128)(2,1)S(1)} %get-tuple-element.40), channel_id=1, source_target_pairs={{0,0},{1,1},{2,2},{3,3},{4,64},{5,65},{6,66},{7,67},{8,128},{9,129... | collective-permute-start | bytes 135176 | tf_op jit(solution)/shard_map/ppermute | solution.py:26
  31.2 4.2 %collective-permute-start.1 = (bf16[88,256]{1,0:T(8,128)(2,1)S(1)}, bf16[88,256]{1,0:T(8,128)(2,1)S(1)}, u32[]{:S(2)}, u32[]{:S(2)}) collective-permute-start(bf16[88,256]{1,0:T(8,128)(2,1)S(1)} %get-tuple-element.41), channel_id=1, source_target_pairs={{0,1},{1,2},{2,3},{3,0},{4,65},{5,66},{6,67},{7,64},{8,129},{9,130... | collective-permute-start | bytes 135176 | tf_op jit(solution)/shard_map/ppermute | solution.py:26
  31.3 5.6 %collective-permute-start.2 = (bf16[88,256]{1,0:T(8,128)(2,1)S(1)}, bf16[88,256]{1,0:T(8,128)(2,1)S(1)}, u32[]{:S(2)}, u32[]{:S(2)}) collective-permute-start(bf16[88,256]{1,0:T(8,128)(2,1)S(1)} %get-tuple-element.42), channel_id=1, source_target_pairs={{0,2},{1,3},{2,0},{3,1},{4,66},{5,67},{6,64},{7,65},{8,130},{9,131... | collective-permute-start | bytes 135176 | tf_op jit(solution)/shard_map/ppermute | solution.py:26
  34.8 4.0 %collective-permute-start.3 = (bf16[88,256]{1,0:T(8,128)(2,1)S(1)}, bf16[88,256]{1,0:T(8,128)(2,1)S(1)}, u32[]{:S(2)}, u32[]{:S(2)}) collective-permute-start(bf16[88,256]{1,0:T(8,128)(2,1)S(1)} %get-tuple-element.43), channel_id=1, source_target_pairs={{0,3},{1,0},{2,1},{3,2},{4,67},{5,64},{6,65},{7,66},{8,131},{9,128... | collective-permute-start | bytes 135176 | tf_op jit(solution)/shard_map/ppermute | solution.py:26
  38.9 33.7 %collective-permute-start.6 = (bf16[4,88,256]{2,1,0:T(8,128)(2,1)S(1)}, bf16[4,88,256]{2,1,0:T(8,128)(2,1)S(1)}, u32[]{:S(2)}, u32[]{:S(2)}) collective-permute-start(bf16[4,88,256]{2,1,0:T(8,128)(2,1)S(1)} %shard_map.92.refs_0_), channel_id=1, source_target_pairs={{0,12},{1,13},{2,14},{3,15},{4,0},{5,1},{6,2},{7,3},{8,4},{9,5},{1... | collective-permute-start | bytes 540680 | tf_op jit(solution)/shard_map/ppermute | solution.py:26
  67.7 20.5 %collective-permute-start.10 = (bf16[1024,256]{1,0:T(8,128)(2,1)S(1)}, bf16[1024,256]{1,0:T(8,128)(2,1)S(1)}, u32[]{:S(2)}, u32[]{:S(2)}) collective-permute-start(bf16[1024,256]{1,0:T(8,128)(2,1)S(1)} %bitcast.3), channel_id=1, source_target_pairs={{0,16},{1,17},{2,18},{3,19},{4,20},{5,21},{6,22},{7,23},{8,24},{9,... | collective-permute-start | bytes 1572872 | tf_op jit(solution)/shard_map/ppermute | solution.py:26
  67.7 20.5 %collective-permute-start.7 = (bf16[1024,256]{1,0:T(8,128)(2,1)S(1)}, bf16[1024,256]{1,0:T(8,128)(2,1)S(1)}, u32[]{:S(2)}, u32[]{:S(2)}) collective-permute-start(bf16[1024,256]{1,0:T(8,128)(2,1)S(1)} %bitcast.7), channel_id=1, source_target_pairs={{0,16},{1,17},{2,18},{3,19},{4,20},{5,21},{6,22},{7,23},{8,24},{9,... | collective-permute-start | bytes 1572872 | tf_op jit(solution)/shard_map/ppermute | solution.py:26
  68.2 20.0 %collective-permute-start.12 = (bf16[1024,256]{1,0:T(8,128)(2,1)S(1)}, bf16[1024,256]{1,0:T(8,128)(2,1)S(1)}, u32[]{:S(2)}, u32[]{:S(2)}) collective-permute-start(bf16[1024,256]{1,0:T(8,128)(2,1)S(1)} %collective-permute-done.11.refs_10_.refs_6_), channel_id=1, source_target_pairs={{0,16},{1,17},{2,18},{3,19},{4,20},{5,21},{6,22},{7,23},{8,24},{9,... | collective-permute-start | bytes 1572872 | tf_op jit(solution)/shard_map/ppermute | solution.py:26
  68.2 20.0 %collective-permute-start.9 = (bf16[1024,256]{1,0:T(8,128)(2,1)S(1)}, bf16[1024,256]{1,0:T(8,128)(2,1)S(1)}, u32[]{:S(2)}, u32[]{:S(2)}) collective-permute-start(bf16[1024,256]{1,0:T(8,128)(2,1)S(1)} %collective-permute-done.8.refs_6_), channel_id=1, source_target_pairs={{0,16},{1,17},{2,18},{3,19},{4,20},{5,21},{6,22},{7,23},{8,24},{9,... | collective-permute-start | bytes 1572872 | tf_op jit(solution)/shard_map/ppermute | solution.py:26
  72.6 8.8 %collective-permute-start.5 = (bf16[4,88,256]{2,1,0:T(8,128)(2,1)S(1)}, bf16[4,88,256]{2,1,0:T(8,128)(2,1)S(1)}, u32[]{:S(2)}, u32[]{:S(2)}) collective-permute-start(bf16[4,88,256]{2,1,0:T(8,128)(2,1)S(1)} %shard_map.92.refs_0_), channel_id=1, source_target_pairs={{0,8},{1,9},{2,10},{3,11},{4,12},{5,13},{6,14},{7,15},{8,0},{9,1},... | collective-permute-start | bytes 540680 | tf_op jit(solution)/shard_map/ppermute | solution.py:26
  81.5 6.7 %collective-permute-start.4 = (bf16[4,88,256]{2,1,0:T(8,128)(2,1)S(1)}, bf16[4,88,256]{2,1,0:T(8,128)(2,1)S(1)}, u32[]{:S(2)}, u32[]{:S(2)}) collective-permute-start(bf16[4,88,256]{2,1,0:T(8,128)(2,1)S(1)} %shard_map.92.refs_0_), channel_id=1, source_target_pairs={{0,4},{1,5},{2,6},{3,7},{4,8},{5,9},{6,10},{7,11},{8,12},{9,13},{1... | collective-permute-start | bytes 540680 | tf_op jit(solution)/shard_map/ppermute | solution.py:26
  90.6 10.6 %collective-permute-start.13 = (bf16[88,1024]{1,0:T(8,128)(2,1)S(1)}, bf16[88,1024]{1,0:T(8,128)(2,1)S(1)}, u32[]{:S(2)}, u32[]{:S(2)}) collective-permute-start(bf16[88,1024]{1,0:T(8,128)(2,1)S(1)} %get-tuple-element.47), channel_id=1, source_target_pairs={{0,64},{1,65},{2,66},{3,67},{4,68},{5,69},{6,70},{7,71},{8,72},{9,... | collective-permute-start | bytes 540680 | tf_op jit(solution)/shard_map/ppermute | solution.py:26
  92.5 12.0 %collective-permute-start.14 = (bf16[88,1024]{1,0:T(8,128)(2,1)S(1)}, bf16[88,1024]{1,0:T(8,128)(2,1)S(1)}, u32[]{:S(2)}, u32[]{:S(2)}) collective-permute-start(bf16[88,1024]{1,0:T(8,128)(2,1)S(1)} %get-tuple-element.48), channel_id=1, source_target_pairs={{0,128},{1,129},{2,130},{3,131},{4,132},{5,133},{6,134},{7,135},{8... | collective-permute-start | bytes 540680 | tf_op jit(solution)/shard_map/ppermute | solution.py:26
  93.2 11.2 %collective-permute-start.15 = (bf16[88,1024]{1,0:T(8,128)(2,1)S(1)}, bf16[88,1024]{1,0:T(8,128)(2,1)S(1)}, u32[]{:S(2)}, u32[]{:S(2)}) collective-permute-start(bf16[88,1024]{1,0:T(8,128)(2,1)S(1)} %get-tuple-element.49), channel_id=1, source_target_pairs={{0,192},{1,193},{2,194},{3,195},{4,196},{5,197},{6,198},{7,199},{8... | collective-permute-start | bytes 540680 | tf_op jit(solution)/shard_map/ppermute | solution.py:26
  105.3 6.2 %copy-start.2 = (bf16[6,256,128]{2,1,0:T(8,128)(2,1)S(1)}, bf16[6,256,128]{2,1,0:T(8,128)(2,1)}, u32[]{:S(2)}) copy-start(bf16[6,256,128]{2,1,0:T(8,128)(2,1)} %low_ref.2) | copy-start | bytes 1179652
  105.3 6.2 %copy-start.3 = (bf16[6,256,128]{2,1,0:T(8,128)(2,1)S(1)}, bf16[6,256,128]{2,1,0:T(8,128)(2,1)}, u32[]{:S(2)}) copy-start(bf16[6,256,128]{2,1,0:T(8,128)(2,1)} %up_ref.2) | copy-start | bytes 1179652
  105.3 18.1 %all-to-all-start.2 = ((bf16[8,24,1024]{2,1,0:T(8,128)(2,1)}), bf16[8,24,1024]{2,1,0:T(8,128)(2,1)S(1)}, u32[]{:S(2)}, u32[]{:S(2)}) async-start(bf16[8,24,1024]{2,1,0:T(8,128)(2,1)} %get-tuple-element.51), calls=%async_computation.2 | async-start | bytes 786432 | tf_op jit(solution)/shard_map/all_to_all | solution.py:30
  123.4 13.5 %all-to-all-start.3 = ((bf16[4,384,256]{2,1,0:T(8,128)(2,1)}), bf16[4,384,256]{2,1,0:T(8,128)(2,1)S(1)}, u32[]{:S(2)}, u32[]{:S(2)}) async-start(bf16[4,384,256]{2,1,0:T(8,128)(2,1)} %shard_map.95), calls=%async_computation.3 | async-start | bytes 1572864 | tf_op jit(solution)/shard_map/all_to_all | solution.py:30
  128.9 8.0 %collective-permute-start.16 = (bf16[8,24,1024]{2,1,0:T(8,128)(2,1)S(1)}, bf16[8,24,1024]{2,1,0:T(8,128)(2,1)}, u32[]{:S(2)}, u32[]{:S(2)}) collective-permute-start(bf16[8,24,1024]{2,1,0:T(8,128)(2,1)S(1)} %all-to-all-done.2.mine_ref), channel_id=1, source_target_pairs={{0,16},{1,17},{2,18},{3,19},{4,20},{5,21},{6,22},{7,23},{8,24},{9,... | collective-permute-start | bytes 1179656 | tf_op jit(solution)/shard_map/ppermute | solution.py:26
  138.7 4.9 %collective-permute-start.19 = (bf16[448,128]{1,0:T(8,128)(2,1)S(1)}, bf16[448,128]{1,0:T(8,128)(2,1)S(1)}, u32[]{:S(2)}, u32[]{:S(2)}) collective-permute-start(bf16[448,128]{1,0:T(8,128)(2,1)S(1)} %get-tuple-element.54.refs_0_), channel_id=1, source_target_pairs={{0,12},{1,13},{2,14},{3,15},{4,0},{5,1},{6,2},{7,3},{8,4},{9,5},{1... | collective-permute-start | bytes 344072 | tf_op jit(solution)/shard_map/ppermute | solution.py:26
  139.3 6.4 %collective-permute-start.18 = (bf16[448,128]{1,0:T(8,128)(2,1)S(1)}, bf16[448,128]{1,0:T(8,128)(2,1)S(1)}, u32[]{:S(2)}, u32[]{:S(2)}) collective-permute-start(bf16[448,128]{1,0:T(8,128)(2,1)S(1)} %get-tuple-element.54.refs_0_), channel_id=1, source_target_pairs={{0,8},{1,9},{2,10},{3,11},{4,12},{5,13},{6,14},{7,15},{8,0},{9,1},... | collective-permute-start | bytes 344072 | tf_op jit(solution)/shard_map/ppermute | solution.py:26
  140.2 6.6 %collective-permute-start.17 = (bf16[448,128]{1,0:T(8,128)(2,1)S(1)}, bf16[448,128]{1,0:T(8,128)(2,1)S(1)}, u32[]{:S(2)}, u32[]{:S(2)}) collective-permute-start(bf16[448,128]{1,0:T(8,128)(2,1)S(1)} %get-tuple-element.54.refs_0_), channel_id=1, source_target_pairs={{0,4},{1,5},{2,6},{3,7},{4,8},{5,9},{6,10},{7,11},{8,12},{9,13},{1... | collective-permute-start | bytes 344072 | tf_op jit(solution)/shard_map/ppermute | solution.py:26
  146.9 8.2 %copy-start.5 = (s32[6]{0:T(128)S(1)}, s32[6]{0:T(128)}, u32[]{:S(2)}) copy-start(s32[6]{0:T(128)} %refs_6_.2) | copy-start | bytes 76
  146.9 4.9 %collective-permute-start.22 = (bf16[448,128]{1,0:T(8,128)(2,1)S(1)}, bf16[448,128]{1,0:T(8,128)(2,1)S(1)}, u32[]{:S(2)}, u32[]{:S(2)}) collective-permute-start(bf16[448,128]{1,0:T(8,128)(2,1)S(1)} %shard_map.97.refs_0_), channel_id=1, source_target_pairs={{0,3},{1,0},{2,1},{3,2},{4,7},{5,4},{6,5},{7,6},{8,11},{9,8},{10,9... | collective-permute-start | bytes 344072 | tf_op jit(solution)/shard_map/ppermute | solution.py:26
  148.4 6.3 %collective-permute-start.21 = (bf16[448,128]{1,0:T(8,128)(2,1)S(1)}, bf16[448,128]{1,0:T(8,128)(2,1)S(1)}, u32[]{:S(2)}, u32[]{:S(2)}) collective-permute-start(bf16[448,128]{1,0:T(8,128)(2,1)S(1)} %shard_map.97.refs_0_), channel_id=1, source_target_pairs={{0,2},{1,3},{2,0},{3,1},{4,6},{5,7},{6,4},{7,5},{8,10},{9,11},{10,... | collective-permute-start | bytes 344072 | tf_op jit(solution)/shard_map/ppermute | solution.py:26
  148.5 6.5 %collective-permute-start.20 = (bf16[448,128]{1,0:T(8,128)(2,1)S(1)}, bf16[448,128]{1,0:T(8,128)(2,1)S(1)}, u32[]{:S(2)}, u32[]{:S(2)}) collective-permute-start(bf16[448,128]{1,0:T(8,128)(2,1)S(1)} %shard_map.97.refs_0_), channel_id=1, source_target_pairs={{0,1},{1,2},{2,3},{3,0},{4,5},{5,6},{6,7},{7,4},{8,9},{9,10},{10,1... | collective-permute-start | bytes 344072 | tf_op jit(solution)/shard_map/ppermute | solution.py:26
  156.1 0.7 collective-permute-start.23
  156.7 15.9 %collective-permute-start.26 = (bf16[4,64,256]{2,1,0:T(8,128)(2,1)S(1)}, bf16[4,64,256]{2,1,0:T(8,128)(2,1)S(1)}, u32[]{:S(2)}, u32[]{:S(2)}) collective-permute-start(bf16[4,64,256]{2,1,0:T(8,128)(2,1)S(1)} %collective-permute-done.23.refs_0_), channel_id=1, source_target_pairs={{0,12},{1,13},{2,14},{3,15},{4,0},{5,1},{6,2},{7,3},{8,4},{9,5},{1... | collective-permute-start | bytes 393224 | tf_op jit(solution)/shard_map/ppermute | solution.py:26
  170.1 6.6 %collective-permute-start.25 = (bf16[4,64,256]{2,1,0:T(8,128)(2,1)S(1)}, bf16[4,64,256]{2,1,0:T(8,128)(2,1)S(1)}, u32[]{:S(2)}, u32[]{:S(2)}) collective-permute-start(bf16[4,64,256]{2,1,0:T(8,128)(2,1)S(1)} %collective-permute-done.23.refs_0_), channel_id=1, source_target_pairs={{0,8},{1,9},{2,10},{3,11},{4,12},{5,13},{6,14},{7,15},{8,0},{9,1},... | collective-permute-start | bytes 393224 | tf_op jit(solution)/shard_map/ppermute | solution.py:26
  170.4 7.6 %collective-permute-start.24 = (bf16[4,64,256]{2,1,0:T(8,128)(2,1)S(1)}, bf16[4,64,256]{2,1,0:T(8,128)(2,1)S(1)}, u32[]{:S(2)}, u32[]{:S(2)}) collective-permute-start(bf16[4,64,256]{2,1,0:T(8,128)(2,1)S(1)} %collective-permute-done.23.refs_0_), channel_id=1, source_target_pairs={{0,4},{1,5},{2,6},{3,7},{4,8},{5,9},{6,10},{7,11},{8,12},{9,13},{1... | collective-permute-start | bytes 393224 | tf_op jit(solution)/shard_map/ppermute | solution.py:26
  179.5 7.3 %collective-permute-start.27 = (bf16[64,1024]{1,0:T(8,128)(2,1)S(1)}, bf16[64,1024]{1,0:T(8,128)(2,1)S(1)}, u32[]{:S(2)}, u32[]{:S(2)}) collective-permute-start(bf16[64,1024]{1,0:T(8,128)(2,1)S(1)} %get-tuple-element.57), channel_id=1, source_target_pairs={{0,64},{1,65},{2,66},{3,67},{4,68},{5,69},{6,70},{7,71},{8,72},{9,... | collective-permute-start | bytes 393224 | tf_op jit(solution)/shard_map/ppermute | solution.py:26
  179.9 9.0 %collective-permute-start.28 = (bf16[64,1024]{1,0:T(8,128)(2,1)S(1)}, bf16[64,1024]{1,0:T(8,128)(2,1)S(1)}, u32[]{:S(2)}, u32[]{:S(2)}) collective-permute-start(bf16[64,1024]{1,0:T(8,128)(2,1)S(1)} %get-tuple-element.58), channel_id=1, source_target_pairs={{0,128},{1,129},{2,130},{3,131},{4,132},{5,133},{6,134},{7,135},{8... | collective-permute-start | bytes 393224 | tf_op jit(solution)/shard_map/ppermute | solution.py:26
  181.9 10.0 %collective-permute-start.29 = (bf16[64,1024]{1,0:T(8,128)(2,1)S(1)}, bf16[64,1024]{1,0:T(8,128)(2,1)S(1)}, u32[]{:S(2)}, u32[]{:S(2)}) collective-permute-start(bf16[64,1024]{1,0:T(8,128)(2,1)S(1)} %get-tuple-element.59), channel_id=1, source_target_pairs={{0,192},{1,193},{2,194},{3,195},{4,196},{5,197},{6,198},{7,199},{8... | collective-permute-start | bytes 393224 | tf_op jit(solution)/shard_map/ppermute | solution.py:26
  192.3 4.9 %collective-permute-start.32 = (bf16[448,128]{1,0:T(8,128)(2,1)S(1)}, bf16[448,128]{1,0:T(8,128)(2,1)S(1)}, u32[]{:S(2)}, u32[]{:S(2)}) collective-permute-start(bf16[448,128]{1,0:T(8,128)(2,1)S(1)} %get-tuple-element.61.refs_0_), channel_id=1, source_target_pairs={{0,12},{1,13},{2,14},{3,15},{4,0},{5,1},{6,2},{7,3},{8,4},{9,5},{1... | collective-permute-start | bytes 344072 | tf_op jit(solution)/shard_map/ppermute | solution.py:26
  193.0 6.3 %collective-permute-start.31 = (bf16[448,128]{1,0:T(8,128)(2,1)S(1)}, bf16[448,128]{1,0:T(8,128)(2,1)S(1)}, u32[]{:S(2)}, u32[]{:S(2)}) collective-permute-start(bf16[448,128]{1,0:T(8,128)(2,1)S(1)} %get-tuple-element.61.refs_0_), channel_id=1, source_target_pairs={{0,8},{1,9},{2,10},{3,11},{4,12},{5,13},{6,14},{7,15},{8,0},{9,1},... | collective-permute-start | bytes 344072 | tf_op jit(solution)/shard_map/ppermute | solution.py:26
  194.8 6.0 %collective-permute-start.30 = (bf16[448,128]{1,0:T(8,128)(2,1)S(1)}, bf16[448,128]{1,0:T(8,128)(2,1)S(1)}, u32[]{:S(2)}, u32[]{:S(2)}) collective-permute-start(bf16[448,128]{1,0:T(8,128)(2,1)S(1)} %get-tuple-element.61.refs_0_), channel_id=1, source_target_pairs={{0,4},{1,5},{2,6},{3,7},{4,8},{5,9},{6,10},{7,11},{8,12},{9,13},{1... | collective-permute-start | bytes 344072 | tf_op jit(solution)/shard_map/ppermute | solution.py:26
  200.8 8.7 %copy-start.6 = (s32[6]{0:T(128)S(1)}, s32[6]{0:T(128)}, u32[]{:S(2)}) copy-start(s32[6]{0:T(128)} %refs_6_.3) | copy-start | bytes 76
  200.8 5.1 %collective-permute-start.35 = (bf16[448,128]{1,0:T(8,128)(2,1)S(1)}, bf16[448,128]{1,0:T(8,128)(2,1)S(1)}, u32[]{:S(2)}, u32[]{:S(2)}) collective-permute-start(bf16[448,128]{1,0:T(8,128)(2,1)S(1)} %shard_map.101.refs_0_), channel_id=1, source_target_pairs={{0,3},{1,0},{2,1},{3,2},{4,7},{5,4},{6,5},{7,6},{8,11},{9,8},{10,9... | collective-permute-start | bytes 344072 | tf_op jit(solution)/shard_map/ppermute | solution.py:26
  203.2 6.3 %collective-permute-start.34 = (bf16[448,128]{1,0:T(8,128)(2,1)S(1)}, bf16[448,128]{1,0:T(8,128)(2,1)S(1)}, u32[]{:S(2)}, u32[]{:S(2)}) collective-permute-start(bf16[448,128]{1,0:T(8,128)(2,1)S(1)} %shard_map.101.refs_0_), channel_id=1, source_target_pairs={{0,2},{1,3},{2,0},{3,1},{4,6},{5,7},{6,4},{7,5},{8,10},{9,11},{10,... | collective-permute-start | bytes 344072 | tf_op jit(solution)/shard_map/ppermute | solution.py:26
  204.0 5.5 %collective-permute-start.33 = (bf16[448,128]{1,0:T(8,128)(2,1)S(1)}, bf16[448,128]{1,0:T(8,128)(2,1)S(1)}, u32[]{:S(2)}, u32[]{:S(2)}) collective-permute-start(bf16[448,128]{1,0:T(8,128)(2,1)S(1)} %shard_map.101.refs_0_), channel_id=1, source_target_pairs={{0,1},{1,2},{2,3},{3,0},{4,5},{5,6},{6,7},{7,4},{8,9},{9,10},{10,1... | collective-permute-start | bytes 344072 | tf_op jit(solution)/shard_map/ppermute | solution.py:26
  210.6 4.7 %collective-permute-start.36 = (bf16[64,256]{1,0:T(8,128)(2,1)S(1)}, bf16[64,256]{1,0:T(8,128)(2,1)S(1)}, u32[]{:S(2)}, u32[]{:S(2)}) collective-permute-start(bf16[64,256]{1,0:T(8,128)(2,1)S(1)} %get-tuple-element.64), channel_id=1, source_target_pairs={{0,1},{1,2},{2,3},{3,0},{4,5},{5,6},{6,7},{7,4},{8,9},{9,10},{10,1... | collective-permute-start | bytes 98312 | tf_op jit(solution)/shard_map/ppermute | solution.py:26
  211.9 5.4 %collective-permute-start.37 = (bf16[64,256]{1,0:T(8,128)(2,1)S(1)}, bf16[64,256]{1,0:T(8,128)(2,1)S(1)}, u32[]{:S(2)}, u32[]{:S(2)}) collective-permute-start(bf16[64,256]{1,0:T(8,128)(2,1)S(1)} %get-tuple-element.65), channel_id=1, source_target_pairs={{0,2},{1,3},{2,0},{3,1},{4,6},{5,7},{6,4},{7,5},{8,10},{9,11},{10,... | collective-permute-start | bytes 98312 | tf_op jit(solution)/shard_map/ppermute | solution.py:26
  214.8 3.9 %collective-permute-start.38 = (bf16[64,256]{1,0:T(8,128)(2,1)S(1)}, bf16[64,256]{1,0:T(8,128)(2,1)S(1)}, u32[]{:S(2)}, u32[]{:S(2)}) collective-permute-start(bf16[64,256]{1,0:T(8,128)(2,1)S(1)} %get-tuple-element.66), channel_id=1, source_target_pairs={{0,3},{1,0},{2,1},{3,2},{4,7},{5,4},{6,5},{7,6},{8,11},{9,8},{10,9... | collective-permute-start | bytes 98312 | tf_op jit(solution)/shard_map/ppermute | solution.py:26
  (2 other events, 1.9 us)
